TPU v7x, 32 devices: a whole 2x2x4 slice. The times are simulated.
32 devices in a mesh: replica: 8 (over z, core), shard: 4 (over y, x).
Axes of the slice: x: 2, y: 2, z: 4, core: 2. Of those that a mesh axis runs over, the one named last changes fastest.
Arguments:
- hidden_in: bfloat16 [4, 2048, 2048], P('shard', 'replica'), may hold values from -6 to 6
- piece_index: int32 [4, 2048], P('shard', 'replica'), may hold values from -1 to 7, as said below
- pad_flags: int32 [4, 2048], P('shard', 'replica'), may hold values from 0 to 1, as said below
- cotangent: bfloat16 [4, 2048, 2048], P('shard', 'replica'), may hold values from -6 to 6
- query_weight: bfloat16 [2048, 2048], P('shard'), may hold values from -0.125 to 0.125
- key_weight: bfloat16 [2048, 2048], P('shard'), may hold values from -0.125 to 0.125
- value_weight: bfloat16 [2048, 2048], P('shard'), may hold values from -0.125 to 0.125
- output_weight: bfloat16 [2048, 2048], P('shard'), may hold values from -0.125 to 0.125
- gate_weight: bfloat16 [2048, 8192], P('shard'), may hold values from -0.125 to 0.125
- up_weight: bfloat16 [2048, 8192], P('shard'), may hold values from -0.125 to 0.125
- down_weight: bfloat16 [8192, 2048], P('shard'), may hold values from -0.0625 to 0.0625
- query_gain: bfloat16 [2048], P('shard'), may hold values from 0.25 to 1.75
- key_gain: bfloat16 [2048], P('shard'), may hold values from 0.25 to 1.75
- attention_gain: bfloat16 [2048], P('shard'), may hold values from 0.25 to 1.75
- feed_gain: bfloat16 [2048], P('shard'), may hold values from 0.25 to 1.75
Outputs:
- result: float32 [4, 2048, 2048], P('shard', 'replica')
- grad_hidden: float32 [4, 2048, 2048], P('shard', 'replica')
- grad_query_weight: float32 [2048, 2048], P('shard')
- grad_key_weight: float32 [2048, 2048], P('shard')
- grad_value_weight: float32 [2048, 2048], P('shard')
- grad_output_weight: float32 [2048, 2048], P('shard')
- grad_gate_weight: float32 [2048, 8192], P('shard')
- grad_up_weight: float32 [2048, 8192], P('shard')
- grad_down_weight: float32 [8192, 2048], P('shard')
- grad_query_gain: float32 [2048], P('shard')
- grad_key_gain: float32 [2048], P('shard')
- grad_attention_gain: float32 [2048], P('shard')
- grad_feed_gain: float32 [2048], P('shard')
- stats: float32 [3], replicated
Inputs may be any that keep to these rules, and one draw needn't show every extreme that they name: `piece_index`: -1 marks text. A picture piece is an aligned run of 256 tokens of one sequence, all holding that run's index within the sequence; the first run of every sequence is text and the last run of every sequence is a picture piece. `pad_flags`: each sequence ends in a run of one or more padded tokens and has none elsewhere.
All inputs are finite; a program needn't handle non-finite values.
Results may differ from a plain program's by a relative error of at most 0.025.
Values may be sent and summed in bfloat16 or wider, within the bound.
No kernel may reach another device: no remote copies, remote signals or barrier semaphores. Data moves between devices by JAX's collectives and lax.ppermute only.
A program may use at most 576 MiB of HBM per device.

v0:
```python
import math

import jax
import jax.numpy as jnp
from jax import lax
from jax.sharding import PartitionSpec as P

HEADS = 16
HEAD = 128


epsilon = 1e-06
theta_base = 500000.0
masked_score = -1e30


def norm_rows(values, gain):
    scaled = values * lax.rsqrt(jnp.mean(values * values, axis=-1, keepdims=True) + epsilon)
    return scaled * gain


def angle_table(positions):
    half_head = HEAD // 2
    rates = theta_base ** (-jnp.arange(half_head).astype(jnp.float32) * (2.0 / HEAD))
    angles = positions.astype(jnp.float32)[:, None] * rates[None, :]
    return (jnp.cos(angles), jnp.sin(angles))


def rotate(values, cosine, sine):
    half_head = HEAD // 2
    first_half = values[..., :half_head]
    second_half = values[..., half_head:]
    cos_wide = cosine[:, None, :]
    sin_wide = sine[:, None, :]
    return jnp.concatenate(
        [
            first_half * cos_wide - second_half * sin_wide,
            second_half * cos_wide + first_half * sin_wide,
        ],
        axis=-1,
    )


def turn_heads(flat_rows, gain, cosine, sine):
    rows_here = flat_rows.shape[0]
    normed = norm_rows(flat_rows, gain).reshape(rows_here, HEADS, HEAD)
    return rotate(normed, cosine, sine).reshape(rows_here, HEADS * HEAD)


def contract_rows(left, right):
    return lax.dot_general(
        left, right, (((0,), (0,)), ((), ())), preferred_element_type=jnp.float32
    )


def contract_cols(left, right):
    return lax.dot_general(
        left, right, (((1,), (1,)), ((), ())), preferred_element_type=jnp.float32
    )


def block_scores(queries, keys_part, info_part, query_place, query_piece, start_key):
    rows_here = queries.shape[0]
    block_rows = keys_part.shape[0]
    scores = jnp.einsum(
        "qhd,khd->hqk",
        queries.reshape(rows_here, HEADS, HEAD),
        keys_part.reshape(block_rows, HEADS, HEAD),
        preferred_element_type=jnp.float32,
    ) * HEAD ** (-0.5)
    key_place = start_key + jnp.arange(block_rows, dtype=jnp.int32)
    key_piece = info_part.astype(jnp.float32)
    allowed = (key_place[None, :] <= query_place[:, None]) | (query_piece[:, None] >= 0.0) & (
        query_piece[:, None] == key_piece[None, :]
    )
    allowed = allowed & (key_piece[None, :] > -1.5)
    return jnp.where(allowed[None], scores, masked_score)


def per_device(
    hidden_in,
    piece_index,
    pad_flags,
    cotangent,
    query_weight,
    key_weight,
    value_weight,
    output_weight,
    gate_weight,
    up_weight,
    down_weight,
    query_gain,
    key_gain,
    attention_gain,
    feed_gain,
):
    tokens = hidden_in[0]
    rows_here = tokens.shape[0]
    width_all = tokens.shape[1]
    hidden_all = gate_weight.shape[1]
    seq_len = rows_here * lax.axis_size("replica")
    first_row = lax.axis_index("replica") * rows_here
    positions = first_row + jnp.arange(rows_here, dtype=jnp.int32)
    cosine, sine = angle_table(positions)
    score_scale = HEAD ** (-0.5)
    input_whole = ()
    feed_whole = ()
    start = jnp.int32(0)
    whole_in = input_whole
    piece_query = lax.all_gather(query_weight, "shard", axis=0, tiled=True)
    piece_key = lax.all_gather(key_weight, "shard", axis=0, tiled=True)
    piece_value = lax.all_gather(value_weight, "shard", axis=0, tiled=True)
    piece_out = lax.all_gather(output_weight, "shard", axis=0, tiled=True)
    gain_one = lax.all_gather(query_gain, "shard", axis=0, tiled=True)
    gain_two = lax.all_gather(key_gain, "shard", axis=0, tiled=True)
    gain_three = lax.all_gather(attention_gain, "shard", axis=0, tiled=True)
    gain_four = lax.all_gather(feed_gain, "shard", axis=0, tiled=True)
    columns = tokens
    sums = tuple(
        (
            jnp.dot(columns, piece, preferred_element_type=jnp.float32)
            for piece in (piece_query, piece_key, piece_value)
        )
    )
    stacked = jnp.stack([gain_one, gain_two, gain_three, gain_four])
    gain_rows = stacked
    whole_in = tuple(
        (
            lax.dynamic_update_slice_in_dim(whole, piece, start, 0)
            for whole, piece in zip(whole_in, (piece_query, piece_key, piece_value))
        )
    )
    (query_raw, key_raw, value_raw), out_whole, gain_rows, input_whole = (
        sums,
        piece_out,
        gain_rows,
        whole_in,
    )
    gains_wide = gain_rows.astype(jnp.float32)

    def turn_local(raw_rows, gain):
        return turn_heads(raw_rows, gain, cosine, sine)

    query_turned, query_pull = jax.vjp(turn_local, query_raw, gains_wide[0])
    key_turned, key_pull = jax.vjp(turn_local, key_raw, gains_wide[1])
    query_low = query_turned.astype(jnp.bfloat16)
    key_low = key_turned.astype(jnp.bfloat16)
    value_low = value_raw.astype(jnp.bfloat16)
    key_info = jnp.where(pad_flags[0] > 0, -2, piece_index[0]).astype(jnp.bfloat16)
    keys_all, values_all, info_all = (
        lax.all_gather(key_low, "replica", axis=0, tiled=True),
        lax.all_gather(value_low, "replica", axis=0, tiled=True),
        lax.all_gather(key_info, "replica", axis=0, tiled=True),
    )
    query_piece = piece_index[0].astype(jnp.float32)
    block_rows = math.gcd(seq_len, 512)
    block_count = seq_len // block_rows

    def scores_at(index):
        start_key = index * block_rows
        keys_part = lax.dynamic_slice_in_dim(keys_all, start_key, block_rows, 0)
        info_part = lax.dynamic_slice_in_dim(info_all, start_key, block_rows, 0)
        return block_scores(query_low, keys_part, info_part, positions, query_piece, start_key)

    def bound_step(index, carried):
        highest, summed = carried
        scores = scores_at(index)
        raised = jnp.maximum(highest, jnp.max(scores, axis=-1))
        summed = summed * jnp.exp(highest - raised) + jnp.sum(
            jnp.exp(scores - raised[..., None]), axis=-1
        )
        return (raised, summed)

    highest, summed = lax.fori_loop(
        0,
        block_count,
        bound_step,
        (
            jnp.full((HEADS, rows_here), masked_score, jnp.float32),
            jnp.zeros((HEADS, rows_here), jnp.float32),
        ),
    )
    log_total = highest + jnp.log(summed)

    def value_step(index, carried):
        start_key = index * block_rows
        weights_low = jnp.exp(scores_at(index) - log_total[..., None]).astype(jnp.bfloat16)
        values_part = lax.dynamic_slice_in_dim(values_all, start_key, block_rows, 0).reshape(
            block_rows, HEADS, HEAD
        )
        return carried + jnp.einsum(
            "hqk,khd->qhd", weights_low, values_part, preferred_element_type=jnp.float32
        )

    mixed = lax.fori_loop(
        0, block_count, value_step, jnp.zeros((rows_here, HEADS, HEAD), jnp.float32)
    )
    attended_low = mixed.reshape(rows_here, width_all).astype(jnp.bfloat16)
    branch_attn = jnp.dot(attended_low, out_whole, preferred_element_type=jnp.float32)
    normed_attn, attn_pull = jax.vjp(norm_rows, branch_attn, gains_wide[2])
    residual = tokens.astype(jnp.float32) + normed_attn
    residual_low = residual.astype(jnp.bfloat16)
    pieces = (
        lax.all_gather(gate_weight, "shard", axis=0, tiled=True),
        lax.all_gather(up_weight, "shard", axis=0, tiled=True),
    )
    start = jnp.int32(0)
    whole_list = feed_whole
    columns = residual_low
    sums = tuple((jnp.dot(columns, piece, preferred_element_type=jnp.float32) for piece in pieces))
    whole_list = tuple(
        (
            lax.dynamic_update_slice_in_dim(whole, piece, start, 0)
            for whole, piece in zip(whole_list, pieces)
        )
    )
    (gate_sum, up_sum), feed_whole = (sums, whole_list)

    def activate(gate_values, up_values):
        return jax.nn.silu(gate_values) * up_values

    activated, act_pull = jax.vjp(activate, gate_sum, up_sum)
    activated_low = activated.astype(jnp.bfloat16)
    piece = lax.all_gather(down_weight, "shard", axis=0, tiled=True)
    columns = activated_low
    partial_sum = jnp.dot(columns, piece, preferred_element_type=jnp.float32)
    normed_feed, feed_pull = jax.vjp(norm_rows, partial_sum, gains_wide[3])
    result = residual + normed_feed
    grad_out = cotangent[0].astype(jnp.float32)
    grad_feed, grad_feed_gain = feed_pull(grad_out)
    grad_feed_low = grad_feed.astype(jnp.bfloat16)
    grad_act = contract_cols(
        grad_feed_low, lax.all_gather(down_weight, "shard", axis=0, tiled=True)
    )
    down_share = lax.psum_scatter(
        contract_rows(activated_low, grad_feed_low).astype(jnp.bfloat16),
        "shard",
        scatter_dimension=0,
        tiled=True,
    ).astype(jnp.float32)
    grad_gate, grad_up = act_pull(grad_act)
    grad_gate_low = grad_gate.astype(jnp.bfloat16)
    grad_up_low = grad_up.astype(jnp.bfloat16)
    pieces = (
        lax.all_gather(gate_weight, "shard", axis=0, tiled=True),
        lax.all_gather(up_weight, "shard", axis=0, tiled=True),
    )
    part_sum = contract_cols(grad_gate_low, pieces[0]) + contract_cols(grad_up_low, pieces[1])
    grad_feed_in = part_sum
    grad_both = jnp.concatenate([grad_gate_low, grad_up_low], axis=1)
    feed_share = lax.psum_scatter(
        contract_rows(residual_low, grad_both).astype(jnp.bfloat16),
        "shard",
        scatter_dimension=0,
        tiled=True,
    ).astype(jnp.float32)
    grad_resid = grad_out + grad_feed_in
    grad_branch, grad_attention_gain = attn_pull(grad_resid)
    grad_branch_low = grad_branch.astype(jnp.bfloat16)
    grad_attended = contract_cols(
        grad_branch_low, lax.all_gather(output_weight, "shard", axis=0, tiled=True)
    )
    grad_mixed = grad_attended.astype(jnp.bfloat16).reshape(rows_here, HEADS, HEAD)
    delta = jnp.einsum("qhd,qhd->hq", grad_mixed.astype(jnp.float32), mixed)
    query_heads = query_low.reshape(rows_here, HEADS, HEAD)

    def back_step(index, carried):
        grad_query, grad_keys, grad_values = carried
        start_key = index * block_rows
        probs = jnp.exp(scores_at(index) - log_total[..., None])
        keys_part = lax.dynamic_slice_in_dim(keys_all, start_key, block_rows, 0).reshape(
            block_rows, HEADS, HEAD
        )
        values_part = lax.dynamic_slice_in_dim(values_all, start_key, block_rows, 0).reshape(
            block_rows, HEADS, HEAD
        )
        value_share = jnp.einsum(
            "hqk,qhd->khd",
            probs.astype(jnp.bfloat16),
            grad_mixed,
            preferred_element_type=jnp.float32,
        )
        grad_probs = jnp.einsum(
            "qhd,khd->hqk", grad_mixed, values_part, preferred_element_type=jnp.float32
        )
        grad_scores = (probs * (grad_probs - delta[..., None])).astype(jnp.bfloat16)
        grad_query = grad_query + jnp.einsum(
            "hqk,khd->qhd", grad_scores, keys_part, preferred_element_type=jnp.float32
        )
        key_share = (
            jnp.einsum("hqk,qhd->khd", grad_scores, query_heads, preferred_element_type=jnp.float32)
            * score_scale
        )
        grad_keys = lax.dynamic_update_slice_in_dim(
            grad_keys, key_share.reshape(block_rows, width_all), start_key, 0
        )
        grad_values = lax.dynamic_update_slice_in_dim(
            grad_values, value_share.reshape(block_rows, width_all), start_key, 0
        )
        return (grad_query, grad_keys, grad_values)

    zero_keys = jnp.zeros((seq_len, width_all), jnp.float32)
    grad_query, grad_keys, grad_values = lax.fori_loop(
        0,
        block_count,
        back_step,
        (jnp.zeros((rows_here, HEADS, HEAD), jnp.float32), zero_keys, zero_keys),
    )
    key_sum, value_sum = (
        lax.psum_scatter(
            grad_keys.astype(jnp.bfloat16), "replica", scatter_dimension=0, tiled=True
        ).astype(jnp.float32),
        lax.psum_scatter(
            grad_values.astype(jnp.bfloat16), "replica", scatter_dimension=0, tiled=True
        ).astype(jnp.float32),
    )
    grad_query_raw, grad_query_gain = query_pull(
        (grad_query * score_scale).reshape(rows_here, width_all)
    )
    grad_key_raw, grad_key_gain = key_pull(key_sum)
    query_back_low = grad_query_raw.astype(jnp.bfloat16)
    key_back_low = grad_key_raw.astype(jnp.bfloat16)
    value_back_low = value_sum.astype(jnp.bfloat16)
    pieces = (
        lax.all_gather(query_weight, "shard", axis=0, tiled=True),
        lax.all_gather(key_weight, "shard", axis=0, tiled=True),
        lax.all_gather(value_weight, "shard", axis=0, tiled=True),
    )
    part_sum = (
        contract_cols(query_back_low, pieces[0])
        + contract_cols(key_back_low, pieces[1])
        + contract_cols(value_back_low, pieces[2])
    )
    grad_tokens = grad_resid + part_sum
    grad_inputs = jnp.concatenate([query_back_low, key_back_low, value_back_low], axis=1)
    input_share = lax.psum_scatter(
        jnp.concatenate(
            [contract_rows(tokens, grad_inputs), contract_rows(attended_low, grad_branch_low)],
            axis=1,
        ).astype(jnp.bfloat16),
        "shard",
        scatter_dimension=0,
        tiled=True,
    ).astype(jnp.float32)
    input_share, feed_share, down_share = (
        lax.psum(input_share.astype(jnp.bfloat16), "replica").astype(jnp.float32),
        lax.psum(feed_share.astype(jnp.bfloat16), "replica").astype(jnp.float32),
        lax.psum(down_share.astype(jnp.bfloat16), "replica").astype(jnp.float32),
    )
    valid = (pad_flags[0] == 0).astype(jnp.float32)[:, None]
    stat_terms = jnp.stack(
        [
            jnp.sum(valid * result * result),
            jnp.sum(valid * branch_attn * branch_attn),
            jnp.sum(valid * partial_sum * partial_sum),
            jnp.sum(valid),
        ]
    )
    gain_terms = jnp.stack([grad_query_gain, grad_key_gain, grad_attention_gain, grad_feed_gain])
    gain_terms, stat_terms = lax.psum((gain_terms, stat_terms), ("replica", "shard"))
    gain_width = query_gain.shape[0]
    gain_mine = lax.dynamic_slice_in_dim(
        gain_terms, lax.axis_index("shard") * gain_width, gain_width, 1
    )
    stats = jnp.sqrt(stat_terms[:3] / (stat_terms[3] * width_all))
    return (
        result[None],
        grad_tokens[None],
        input_share[:, :width_all],
        input_share[:, width_all : 2 * width_all],
        input_share[:, 2 * width_all : 3 * width_all],
        input_share[:, 3 * width_all :],
        feed_share[:, :hidden_all],
        feed_share[:, hidden_all:],
        down_share,
        gain_mine[0],
        gain_mine[1],
        gain_mine[2],
        gain_mine[3],
        stats,
    )


def solution(mesh):
    placed = (
        P("shard", "replica", None),
        P("shard", "replica"),
        P("shard", "replica"),
        P("shard", "replica", None),
        P("shard", None),
        P("shard", None),
        P("shard", None),
        P("shard", None),
        P("shard", None),
        P("shard", None),
        P("shard", None),
        P("shard"),
        P("shard"),
        P("shard"),
        P("shard"),
    )
    return jax.shard_map(
        per_device,
        mesh=mesh,
        in_specs=placed,
        out_specs=(
            P("shard", "replica", None),
            P("shard", "replica", None),
            P("shard", None),
            P("shard", None),
            P("shard", None),
            P("shard", None),
            P("shard", None),
            P("shard", None),
            P("shard", None),
            P("shard"),
            P("shard"),
            P("shard"),
            P("shard"),
            P(),
        ),
        check_vma=False,
    )
```

profile of v0, /device:TPU:0, one launch (start us, length us, event | category | flops | bytes accessed | tf_op | source)
XLA Modules:
  0.0 3683.2 jit_solution(10131605898892978450)
XLA Ops:
  9.5 90.7 %all-gather.15.cloned.1.call-done = bf16[2048,2048]{1,0:T(8,128)(2,1)} async-done(((bf16[512,2048]{1,0:T(8,128)(2,1)}), bf16[2048,2048]{1,0:T(8,128)(2,1)}) %all-gather.15.cloned.1.call-update) | async-done | bytes 8388624 | tf_op jit(solution)/shard_map/all_gather | solution.py:112
  100.2 6.7 convolution_convert_fusion.4
  107.1 8.0 all-gather.1
  115.1 7.1 all-gather.2
  122.2 8.0 all-gather.3
  130.2 7.1 all-gather.4
  138.4 51.5 %all-gather.19.cloned.1.call-done = bf16[2048,2048]{1,0:T(8,128)(2,1)} async-done(((bf16[512,2048]{1,0:T(8,128)(2,1)}), bf16[2048,2048]{1,0:T(8,128)(2,1)}) %all-gather.19.cloned.1.call-update) | async-done | bytes 8388624 | tf_op jit(solution)/shard_map/all_gather | solution.py:111
  189.9 5.8 multiply_reduce_fusion.10
  205.4 11.7 all-gather
  217.7 61.7 %all-gather.23.cloned.1.call-done = bf16[2048,2048]{1,0:T(8,128)(2,1)} async-done(((bf16[512,2048]{1,0:T(8,128)(2,1)}), bf16[2048,2048]{1,0:T(8,128)(2,1)}) %all-gather.23.cloned.1.call-update) | async-done | bytes 8388624 | tf_op jit(solution)/shard_map/all_gather | solution.py:110
  279.4 5.8 multiply_reduce_fusion.9
  291.6 71.9 %all-gather.17.cloned.1.call-done = bf16[2048,2048]{1,0:T(8,128)(2,1)} async-done(((bf16[256,2048]{1,0:T(8,128)(2,1)}), bf16[2048,2048]{1,0:T(8,128)(2,1)}) %all-gather.17.cloned.1.call-update) | async-done | bytes 8388624 | tf_op jit(solution)/shard_map/all_gather | solution.py:152
  363.5 12.3 copy.126
  375.9 70.7 %all-gather.21.cloned.1.call-done = bf16[2048,2048]{0,1:T(8,128)(2,1)} async-done(((bf16[256,2048]{0,1:T(8,128)(2,1)}), bf16[2048,2048]{0,1:T(8,128)(2,1)}) %all-gather.21.cloned.1.call-update) | async-done | bytes 8388624 | tf_op jit(solution)/shard_map/all_gather | solution.py:151
  446.6 51.6 %while.48 = (s32[]{:T(128)}, f32[16,256]{1,0:T(8,128)S(1)}, f32[16,256]{1,0:T(8,128)S(1)}, f32[256]{0:T(256)S(1)}, bf16[2048]{0:T(1024)(128)(2,1)S(1)}, /*index=...) while((s32[]{:T(128)}, f32[16,256]{1,0:T(8,128)S(1)}, ...), condition=%wide.region_5.6_spmd.clone, body=%wide.region_2.5_spmd.clone.sunk | while | flops 552229376 | bytes 24739520 | solution.py:174
  454.1 6.3 exponential_reduce_fusion.2
  498.2 42.5 %while.49 = (s32[]{:T(128)}, f32[256,16,128]{0,2,1:T(8,128)}, bf16[2048,2048]{0,1:T(8,128)(2,1)}, f32[256]{0:T(256)S(1)}, bf16[2048]{0:T(1024)(128)(2,1)S(1)}, /...) while((s32[]{:T(128)}, f32[256,16,128]{0,2,1:T(8,128)}, ...), condition=%wide.region_7.8_spmd.clone, body=%wide.region_6.7_spmd.clone.sunk | while | flops 1083836928 | bytes 18120392 | solution.py:195
  502.5 5.9 bitcast_add_fusion.4
  512.7 6.5 bitcast_add_fusion.4
  523.4 6.5 bitcast_add_fusion.4
  534.2 6.5 bitcast_add_fusion.4
  543.2 9.1 multiply_reduce_fusion.8
  554.1 279.1 %all-gather.27.cloned.1.call-done = bf16[2048,8192]{1,0:T(8,128)(2,1)} async-done(((bf16[512,8192]{1,0:T(8,128)(2,1)}), bf16[2048,8192]{1,0:T(8,128)(2,1)}) %all-gather.27.cloned.1.call-update) | async-done | bytes 33554448 | tf_op jit(solution)/shard_map/all_gather | solution.py:204
  833.2 22.2 fusion.92
  855.5 276.8 %all-gather.29.cloned.1.call-done = bf16[2048,8192]{1,0:T(8,128)(2,1)} async-done(((bf16[512,8192]{1,0:T(8,128)(2,1)}), bf16[2048,8192]{1,0:T(8,128)(2,1)}) %all-gather.29.cloned.1.call-update) | async-done | bytes 33554448 | tf_op jit(solution)/shard_map/all_gather | solution.py:205
  1132.3 26.9 multiply_convert_fusion.1
  1159.2 272.2 %all-gather.31.cloned.1.call-done = bf16[8192,2048]{1,0:T(8,128)(2,1)} async-done(((bf16[2048,2048]{1,0:T(8,128)(2,1)}), bf16[8192,2048]{1,0:T(8,128)(2,1)}) %all-gather.31.cloned.1.call-update) | async-done | bytes 33554448 | tf_op jit(solution)/shard_map/all_gather | solution.py:224
  1431.4 16.6 multiply_reduce_fusion.7
  1450.1 22.0 multiply_convert_fusion
  1472.1 17.1 fusion.93
  1489.2 20.5 multiply_reduce_fusion.1
  1531.4 106.4 %while.50 = (s32[]{:T(128)}, f32[256,16,128]{0,2,1:T(8,128)}, bf16[2048,2048]{0,1:T(8,128)(2,1)}, bf16[2048,2048]{1,0:T(8,128)(2,1)}, bf16[2048,2048]{0,1:T(8,12...) while((s32[]{:T(128)}, f32[256,16,128]{0,2,1:T(8,128)}, ...), condition=%wide.region_13.14_spmd.clone, body=%wide.region_12.13_spmd.clone.sunk | while | flops 2709129728 | bytes 103219016 | solution.py:303
  1639.7 16.4 convolution_convert_fusion.1
  1665.9 61.8 %reduce-scatter.10.cloned.1.call-done = bf16[256,2048]{0,1:T(8,128)(2,1)} async-done(((bf16[2048,2048]{0,1:T(8,128)(2,1)}), bf16[256,2048]{0,1:T(8,128)(2,1)}) %reduce-scatter.10.cloned.1.call-update) | async-done | bytes 1048592 | tf_op jit(solution)/shard_map/reduce_scatter | solution.py:310
  1741.6 76.9 %reduce-scatter.12.cloned.1.call-done = bf16[256,2048]{1,0:T(8,128)(2,1)} async-done(((bf16[2048,2048]{1,0:T(8,128)(2,1)}), bf16[256,2048]{1,0:T(8,128)(2,1)}) %reduce-scatter.12.cloned.1.call-update) | async-done | bytes 1048592 | tf_op jit(solution)/shard_map/reduce_scatter | solution.py:313
  1818.5 13.4 convert_bitcast_fusion
  1831.8 24.4 pad_maximum_fusion
  1857.4 29.1 convolution_convert_fusion
  1886.8 221.6 %reduce-scatter.18.cloned.1.call-done = bf16[2048,2048]{1,0:T(8,128)(2,1)} async-done(((bf16[8192,2048]{1,0:T(8,128)(2,1)}), bf16[2048,2048]{1,0:T(8,128)(2,1)}) %reduce-scatter.18.cloned.1.call-update) | async-done | bytes 8388624
  2108.4 292.0 %reduce-scatter.14.cloned.1.call-done = bf16[512,8192]{0,1:T(8,128)(2,1)} async-done(((bf16[2048,8192]{0,1:T(8,128)(2,1)}), bf16[512,8192]{0,1:T(8,128)(2,1)}) %reduce-scatter.14.cloned.1.call-update) | async-done | bytes 8388624 | tf_op jit(solution)/shard_map/reduce_scatter | solution.py:336
  2400.5 561.2 %reduce-scatter.16.cloned.1.call-done = bf16[512,16384]{1,0:T(8,128)(2,1)} async-done(((bf16[2048,16384]{1,0:T(8,128)(2,1)}), bf16[512,16384]{1,0:T(8,128)(2,1)}) %reduce-scatter.16.cloned.1.call-update) | async-done | bytes 16777232
  2965.6 41.1 %all-reduce.6 = (f32[4,2048]{1,0:T(4,128)S(1)}, f32[4]{0:T(128)S(1)}) all-reduce(f32[4,2048]{1,0:T(4,128)S(1)} %pad_maximum_fusion.2, f32[4]{0:T(128)S(1)} %pad_maximum_fusion.3), channel_id=1, replica_groups=mesh['replica'=8,'shard'=4] {'replica','shard'}, use_global_device_ids=true, to_apply=%region_28.29 | all-reduce | flops 8196 | bytes 65568 | tf_op jit(solution)/shard_map/psum | solution.py:360
  3009.2 5.9 fusion.94
  3015.1 6.1 convolution_add_fusion.2
  3025.0 591.2 %all-reduce.10.cloned.1.call-done = (bf16[512,8192]{0,1:T(8,128)(2,1)}, bf16[512,16384]{1,0:T(8,128)(2,1)}, bf16[2048,2048]{1,0:T(8,128)(2,1)}) async-done(((bf16[512,8192]{0,1:T(8,128)(2,1)}, bf16[512,16384]{1,0:T(8,128)(2,1)}, bf16[2048,2048]{1,0:T(8,128)(2,1)}), (bf16[512,8192]{0,1:T(8,128)(2,1)}, bf16[512,16384]{1,0:T(8,128)(2,1)}, bf16[2048,2048]{1,0:T(8,128)(2,1)})) %all-reduce.10.cloned.1.call-update) | async-done | bytes 33554448 | tf_op jit(solution)/shard_map/psum | solution.py:346
  3616.1 16.9 fusion.86
  3633.0 10.4 fusion.87
  3664.8 11.7 convert_element_type.207
  (396 shorter events, 273.2 us)
Async XLA Ops:
  7.2 93.0 %all-gather.15.cloned.1.call-start = ((), (), s32[]{:S(2)}) async-start(), calls=%async_computation.5 | async-start | bytes 10485760 | tf_op jit(solution)/shard_map/all_gather | solution.py:112
  7.9 92.3 %copy-start.22 = (bf16[1,256,2048]{2,1,0:T(8,128)(2,1)S(1)}, bf16[1,256,2048]{2,1,0:T(8,128)(2,1)}, u32[]{:S(2)}) copy-start(bf16[1,256,2048]{2,1,0:T(8,128)(2,1)} %param.21) | copy-start | bytes 3145732
  7.9 181.9 %all-gather.19.cloned.1.call-start = ((), (), s32[]{:S(2)}) async-start(), calls=%async_computation.7 | async-start | bytes 10485760 | tf_op jit(solution)/shard_map/all_gather | solution.py:111
  8.7 270.7 %all-gather.23.cloned.1.call-start = ((), (), s32[]{:S(2)}) async-start(), calls=%async_computation.9 | async-start | bytes 10485760 | tf_op jit(solution)/shard_map/all_gather | solution.py:110
  9.4 97.6 %copy-start.62 = (bf16[512]{0:T(512)(128)(2,1)S(1)}, bf16[512]{0:T(512)(128)(2,1)}, u32[]{:S(2)}) copy-start(bf16[512]{0:T(512)(128)(2,1)} %param.32) | copy-start | bytes 3076
  9.4 97.6 %copy-start.63 = (bf16[512]{0:T(512)(128)(2,1)S(1)}, bf16[512]{0:T(512)(128)(2,1)}, u32[]{:S(2)}) copy-start(bf16[512]{0:T(512)(128)(2,1)} %param.33) | copy-start | bytes 3076
  9.4 97.6 %copy-start.64 = (bf16[512]{0:T(512)(128)(2,1)S(1)}, bf16[512]{0:T(512)(128)(2,1)}, u32[]{:S(2)}) copy-start(bf16[512]{0:T(512)(128)(2,1)} %param.34) | copy-start | bytes 3076
  9.4 97.6 %copy-start.65 = (bf16[512]{0:T(512)(128)(2,1)S(1)}, bf16[512]{0:T(512)(128)(2,1)}, u32[]{:S(2)}) copy-start(bf16[512]{0:T(512)(128)(2,1)} %param.35) | copy-start | bytes 3076
  9.4 354.1 %all-gather.17.cloned.1.call-start = ((), (), s32[]{:S(2)}) async-start(), calls=%async_computation.6 | async-start | bytes 9437184 | tf_op jit(solution)/shard_map/all_gather | solution.py:152
  106.9 339.7 %all-gather.21.cloned.1.call-start = ((), (), s32[]{:S(2)}) async-start(), calls=%async_computation.8 | async-start | bytes 9437184 | tf_op jit(solution)/shard_map/all_gather | solution.py:151
  137.7 151.1 %copy-start.30 = (f32[256,64]{0,1:T(8,128)}, f32[256,64]{0,1:T(8,128)S(1)}, u32[]{:S(2)}) copy-start(f32[256,64]{0,1:T(8,128)S(1)} %get-tuple-element.949) | copy-start | bytes 196612
  137.7 151.1 %copy-start.32 = (f32[256,64]{0,1:T(8,128)}, f32[256,64]{0,1:T(8,128)S(1)}, u32[]{:S(2)}) copy-start(f32[256,64]{0,1:T(8,128)S(1)} %get-tuple-element.950) | copy-start | bytes 196612
  138.4 57.3 %copy-start.42 = (f32[1,2048]{1,0:T(1,128)}, f32[1,2048]{1,0:T(1,128)S(1)}, u32[]{:S(2)}) copy-start(f32[1,2048]{1,0:T(1,128)S(1)} %get-tuple-element.948) | copy-start | bytes 24580
  138.4 147.4 %copy-start.40 = (f32[1,2048]{1,0:T(1,128)}, f32[1,2048]{1,0:T(1,128)S(1)}, u32[]{:S(2)}) copy-start(f32[1,2048]{1,0:T(1,128)S(1)} %get-tuple-element.947) | copy-start | bytes 24580
  202.4 340.7 %all-gather.25.cloned.1.call-start = ((), (), s32[]{:S(2)}) async-start(), calls=%async_computation.10 | async-start | bytes 10485760 | tf_op jit(solution)/shard_map/all_gather | solution.py:113
  203.0 630.2 %all-gather.27.cloned.1.call-start = ((), (), s32[]{:S(2)}) async-start(), calls=%async_computation.11 | async-start | bytes 41943040 | tf_op jit(solution)/shard_map/all_gather | solution.py:204
  203.8 928.5 %all-gather.29.cloned.1.call-start = ((), (), s32[]{:S(2)}) async-start(), calls=%async_computation.12 | async-start | bytes 41943040 | tf_op jit(solution)/shard_map/all_gather | solution.py:205
  204.5 1226.8 %all-gather.31.cloned.1.call-start = ((), (), s32[]{:S(2)}) async-start(), calls=%async_computation.13 | async-start | bytes 41943040 | tf_op jit(solution)/shard_map/all_gather | solution.py:224
  205.3 1522.3 %reduce-scatter.10.cloned.1.call-start = ((), (), s32[]{:S(2)}) async-start(), calls=%async_computation.14 | async-start | bytes 9437184 | tf_op jit(solution)/shard_map/reduce_scatter | solution.py:310
  291.0 84.9 %copy-start.4 = (bf16[256,16,128]{0,2,1:T(8,128)(2,1)}, bf16[256,16,128]{0,2,1:T(8,128)(2,1)S(1)}, u32[]{:S(2)}) copy-start(bf16[256,16,128]{0,2,1:T(8,128)(2,1)S(1)} %maximum_convert_fusion) | copy-start | bytes 3145732
  540.7 11.6 copy-start.1
  540.7 11.6 copy-start.36
  540.7 11.6 copy-start.38
  540.7 11.6 copy-start.46
  543.1 9.2 copy-start.14
  543.2 10.5 copy-start.23
  554.1 578.2 %copy-start.20 = (bf16[256,2048]{1,0:T(8,128)(2,1)}, bf16[256,2048]{1,0:T(8,128)(2,1)S(1)}, u32[]{:S(2)}) copy-start(bf16[256,2048]{1,0:T(8,128)(2,1)S(1)} %fusion.71) | copy-start | bytes 3145732
  1431.4 16.6 copy-start.27
  1431.4 16.6 copy-start.44
  1431.4 16.6 copy-start.55
  1448.0 24.1 copy-start.16
  1450.1 22.0 copy-start.53
  1472.1 39.6 %slice-start = ((s8[8388608]{0:T(1024)(128)(4,1)}), s8[4194304]{0:T(1024)(128)(4,1)S(1)}, s32[]{:S(2)}) async-start(s8[8388608]{0:T(1024)(128)(4,1)} %bitcast.255), calls=%async_computation.20 | async-start | bytes 8388608
  1489.2 20.5 copy-start.13
  1489.2 22.5 slice-start.1
  1637.8 180.7 %reduce-scatter.12.cloned.1.call-start = ((), (), s32[]{:S(2)}) async-start(), calls=%async_computation.15 | async-start | bytes 9437184 | tf_op jit(solution)/shard_map/reduce_scatter | solution.py:313
  1638.6 469.9 %reduce-scatter.18.cloned.1.call-start = ((), (), s32[]{:S(2)}) async-start(), calls=%async_computation.18 | async-start | bytes 41943040
  1656.2 744.3 %reduce-scatter.14.cloned.1.call-start = ((), (), s32[]{:S(2)}) async-start(), calls=%async_computation.16 | async-start | bytes 41943040 | tf_op jit(solution)/shard_map/reduce_scatter | solution.py:336
  1665.8 63.2 %copy-start.19 = (f32[256,16,128]{0,2,1:T(8,128)S(1)}, f32[256,16,128]{0,2,1:T(8,128)}, u32[]{:S(2)}) copy-start(f32[256,16,128]{0,2,1:T(8,128)} %broadcast_multiply_fusion) | copy-start | bytes 6291460
  1665.8 63.2 %copy-start.31 = (f32[256,64]{0,1:T(8,128)S(1)}, f32[256,64]{0,1:T(8,128)}, u32[]{:S(2)}) copy-start(f32[256,64]{0,1:T(8,128)} %copy-done.30) | copy-start | bytes 196612
  1665.8 63.2 %copy-start.33 = (f32[256,64]{0,1:T(8,128)S(1)}, f32[256,64]{0,1:T(8,128)}, u32[]{:S(2)}) copy-start(f32[256,64]{0,1:T(8,128)} %copy-done.32) | copy-start | bytes 196612
  1741.1 77.4 %copy-start.24 = (bf16[1,256,2048]{2,1,0:T(8,128)(2,1)S(1)}, bf16[1,256,2048]{2,1,0:T(8,128)(2,1)}, u32[]{:S(2)}) copy-start(bf16[1,256,2048]{2,1,0:T(8,128)(2,1)} %param.21) | copy-start | bytes 3145732
  1856.3 1105.4 %reduce-scatter.16.cloned.1.call-start = ((), (), s32[]{:S(2)}) async-start(), calls=%async_computation.17 | async-start | bytes 83886080
  1886.5 1729.6 %all-reduce.10.cloned.1.call-start = ((), (), s32[]{:S(2)}) async-start(), calls=%async_computation.19 | async-start | bytes 67108864 | tf_op jit(solution)/shard_map/psum | solution.py:346
  3009.2 12.0 slice-start.2
  3015.1 6.1 copy-start.29
  3015.1 6.1 copy-start.34
  3015.1 6.1 slice-start.3
  (47 other events, 104.9 us)
Sparse Core Ops, SparseCore 0:
  9.9 90.2 all-gather.14
  102.0 87.7 all-gather.18
  191.7 87.6 all-gather.22
  281.4 82.0 all-gather.16
  365.5 81.0 all-gather.20
  448.3 85.7 all-gather.24
  536.0 297.2 all-gather.26
  835.1 297.2 all-gather.28
  1134.1 297.2 all-gather.30
  1638.0 89.6 reduce-scatter.9
  1730.5 87.9 reduce-scatter.11
  1821.4 286.9 reduce-scatter.17
  2111.8 288.6 reduce-scatter.13
  2403.4 558.2 reduce-scatter.15
  2964.4 651.7 all-reduce.9
where the time goes:
time: 3690 us; the launch traced here: 3680 us
  waiting for transfers between devices  2980 us (81%)
  matrix products  339 us (9%)
  local copies, waits for them, and re-layouts  166 us (4%)
  other arithmetic  92.9 us (3%)
  blocking collectives  83.1 us (2%)
    unnamed x17, waiting for transfers between devices  788 us
    psum x1, waiting for transfers between devices, per_device(): lax.psum(input_share.astype(jnp.bfloat16), 'replica').astype(jnp.float32)  591 us
    reduce_scatter x1, waiting for transfers between devices, per_device(): lax.psum_scatter(jnp.concatenate([contract_rows(tokens, grad_inputs), con...  292 us
    all_gather x1, waiting for transfers between devices, per_device(): lax.all_gather(gate_weight, 'shard', axis=0, tiled=True)  279 us
    all_gather x1, waiting for transfers between devices, per_device(): lax.all_gather(up_weight, 'shard', axis=0, tiled=True)  277 us
    all_gather x1, waiting for transfers between devices, per_device(): piece = lax.all_gather(down_weight, 'shard', axis=0, tiled=True)  272 us
    all_gather x1, waiting for transfers between devices, per_device(): piece_value = lax.all_gather(value_weight, 'shard', axis=0, tiled=True)  90.7 us
    dot_general x7, matrix products, contract_cols(): lax.dot_general(left, right, (((1,), (1,)), ((), ())), preferred_element_...  77.7 us
  transfers between devices with their start and end apart: 15, of which 14 were waited for; matrix products, arithmetic and copies ran while one was open for 9% of the time, Pallas kernels for 0%

commit v1 on v0

v1 whole, which is shorter than its diff:
```python
import jax
import jax.numpy as jnp
from jax import lax
from jax.experimental import pallas as pl
from jax.experimental.pallas import tpu as pltpu
from jax.sharding import Mesh, PartitionSpec as P

HEADS = 16
HEAD = 128
PIECE = 256

epsilon = 1e-06
theta_base = 500000.0
masked_score = -1e30
score_scale = HEAD ** (-0.5)

BF = jnp.bfloat16
F32 = jnp.float32


def mm(left, right):
    return jnp.dot(left, right, preferred_element_type=F32)


def contract_rows(left, right):
    return lax.dot_general(left, right, (((0,), (0,)), ((), ())), preferred_element_type=F32)


def contract_cols(left, right):
    return lax.dot_general(left, right, (((1,), (1,)), ((), ())), preferred_element_type=F32)


def send_core(values):
    return lax.ppermute(values, "core", [(0, 1), (1, 0)])


def send_shard(values, k):
    count = lax.axis_size("shard")
    return lax.ppermute(values, "shard", [(i, i ^ k) for i in range(count)])


def gather_shard(values):
    count = lax.axis_size("shard")
    if count != 4:
        return [values] + [send_shard(values, k) for k in range(1, count)]
    half = values.shape[0] // 2
    from_x = send_shard(values, 1)
    from_y = send_shard(values, 2)
    far_a = send_shard(from_x[:half], 2)
    far_b = send_shard(from_y[half:], 1)
    return [values, from_x, from_y, jnp.concatenate([far_a, far_b], 0)]


def gather_plane(values):
    mine = gather_shard(values)
    return [mine, [send_core(block) for block in mine]]


def reduce_plane(other, mine):
    count = lax.axis_size("shard")
    total = mine + send_core(other.astype(BF)).astype(F32)
    if count != 4:
        result = total[0]
        for k in range(1, count):
            result = result + send_shard(total[k].astype(BF), k).astype(F32)
        return result
    half = total.shape[1] // 2
    far = total[3].astype(BF)
    via_x = send_shard(far[:half], 1)
    via_y = send_shard(far[half:], 2)
    to_y = jnp.concatenate([total[2][:half] + via_x.astype(F32), total[2][half:]], 0).astype(BF)
    to_x = jnp.concatenate([total[1][:half], total[1][half:] + via_y.astype(F32)], 0).astype(BF)
    return total[0] + send_shard(to_x, 1).astype(F32) + send_shard(to_y, 2).astype(F32)


def sum_plane(values):
    count = lax.axis_size("shard")
    values = values + send_core(values)
    step = 1
    while step < count:
        values = values + send_shard(values, step)
        step *= 2
    return values


def forward_kernel(flags, queries, keys, values, key_bias, mixed, lse):
    rows = queries.shape[0]
    blocks = rows // PIECE
    place_key = lax.broadcasted_iota(jnp.int32, (PIECE, PIECE), 0)
    place_query = lax.broadcasted_iota(jnp.int32, (PIECE, PIECE), 1)
    causal = place_key <= place_query
    for b in range(blocks):
        here = pl.ds(b * PIECE, PIECE)
        whole = flags[b] > 0
        scores = contract_cols(keys[: (b + 1) * PIECE, :], queries[here, :]) * score_scale
        scores = scores + key_bias[: (b + 1) * PIECE, :]
        last = jnp.where(causal | whole, scores[b * PIECE :], masked_score)
        scores = jnp.concatenate([scores[: b * PIECE], last], 0) if b else last
        highest = jnp.max(scores, axis=0, keepdims=True)
        raised = jnp.exp(scores - highest)
        summed = jnp.sum(raised, axis=0, keepdims=True)
        lse[:, here] = highest + jnp.log(summed)
        probs = (raised * (1.0 / summed)).astype(BF)
        mixed[here, :] = contract_rows(probs, values[: (b + 1) * PIECE, :]).astype(mixed.dtype)


def attend_forward(queries, keys, values, key_bias, flags):
    rows, width = queries.shape
    heads = width // HEAD
    column = pl.BlockSpec((rows, HEAD), lambda h, f: (0, h))
    return pl.pallas_call(
        forward_kernel,
        grid_spec=pltpu.PrefetchScalarGridSpec(
            num_scalar_prefetch=1,
            grid=(heads,),
            in_specs=[column, column, column, pl.BlockSpec((rows, 1), lambda h, f: (0, 0))],
            out_specs=[column, pl.BlockSpec((None, 1, rows), lambda h, f: (h, 0, 0))],
        ),
        out_shape=[
            jax.ShapeDtypeStruct((rows, width), BF),
            jax.ShapeDtypeStruct((heads, 1, rows), F32),
        ],
        compiler_params=pltpu.CompilerParams(vmem_limit_bytes=48 * 1024 * 1024),
        name="attend_forward",
    )(flags, queries, keys, values, key_bias)


def backward_kernel(
    flags, queries, keys, values, grad_mixed, key_bias, lse, delta, grad_queries, grad_keys, grad_values, values_acc
):
    rows = queries.shape[0]
    blocks = rows // PIECE
    place_key = lax.broadcasted_iota(jnp.int32, (PIECE, PIECE), 0)
    place_query = lax.broadcasted_iota(jnp.int32, (PIECE, PIECE), 1)
    causal = place_key <= place_query
    grad_keys[...] = jnp.zeros_like(grad_keys)
    values_acc[...] = jnp.zeros_like(values_acc)
    for b in range(blocks):
        here = pl.ds(b * PIECE, PIECE)
        seen = pl.ds(0, (b + 1) * PIECE)
        whole = flags[b] > 0
        query_block = queries[here, :]
        grad_block = grad_mixed[here, :]
        scores = contract_cols(keys[seen, :], query_block) * score_scale + key_bias[seen, :]
        last = jnp.where(causal | whole, scores[b * PIECE :], masked_score)
        scores = jnp.concatenate([scores[: b * PIECE], last], 0) if b else last
        probs = jnp.exp(scores - lse[:, here])
        grad_probs = contract_cols(values[seen, :], grad_block)
        grad_scores = (probs * (grad_probs - delta[:, here])).astype(BF)
        values_acc[seen, :] += mm(probs.astype(BF), grad_block)
        grad_keys[seen, :] += mm(grad_scores, query_block) * score_scale
        grad_queries[here, :] = contract_rows(grad_scores, keys[seen, :]) * score_scale
    grad_values[...] = values_acc[...].astype(grad_values.dtype)


def attend_backward(queries, keys, values, grad_mixed, key_bias, flags, lse, delta):
    rows, width = queries.shape
    heads = width // HEAD
    column = pl.BlockSpec((rows, HEAD), lambda h, f: (0, h))
    line = pl.BlockSpec((None, 1, rows), lambda h, f: (h, 0, 0))
    return pl.pallas_call(
        backward_kernel,
        grid_spec=pltpu.PrefetchScalarGridSpec(
            num_scalar_prefetch=1,
            grid=(heads,),
            in_specs=[column] * 4 + [pl.BlockSpec((rows, 1), lambda h, f: (0, 0)), line, line],
            out_specs=[column] * 3,
            scratch_shapes=[pltpu.VMEM((rows, HEAD), F32)],
        ),
        out_shape=[
            jax.ShapeDtypeStruct((rows, width), F32),
            jax.ShapeDtypeStruct((rows, width), F32),
            jax.ShapeDtypeStruct((rows, width), BF),
        ],
        compiler_params=pltpu.CompilerParams(vmem_limit_bytes=56 * 1024 * 1024),
        name="attend_backward",
    )(flags, queries, keys, values, grad_mixed, key_bias, lse, delta)


def norm_factor(values):
    return lax.rsqrt(jnp.mean(values * values, axis=-1, keepdims=True) + epsilon)


def norm_back(values, factor, gain, cotangent):
    scaled = gain * cotangent
    inner = jnp.mean(values * scaled, axis=-1, keepdims=True)
    grad = factor * scaled - values * (factor * factor * factor) * inner
    return grad, jnp.sum(cotangent * values * factor, axis=0)


def rotate(values, cosine, sine):
    half = HEAD // 2
    first, second = values[..., :half], values[..., half:]
    cos_wide, sin_wide = cosine[:, None, :], sine[:, None, :]
    return jnp.concatenate(
        [first * cos_wide - second * sin_wide, second * cos_wide + first * sin_wide], axis=-1
    )


def rotate_back(values, cosine, sine):
    return rotate(values, cosine, -sine)


def per_device(
    hidden_in,
    piece_index,
    pad_flags,
    cotangent,
    query_weight,
    key_weight,
    value_weight,
    output_weight,
    gate_weight,
    up_weight,
    down_weight,
    query_gain,
    key_gain,
    attention_gain,
    feed_gain,
):
    shards = lax.axis_size("shard")
    planes = lax.axis_size("z")
    shard = lax.axis_index("shard")
    core = lax.axis_index("core")
    plane = lax.axis_index("z")
    tokens = hidden_in[0]
    rows, width = tokens.shape
    chunk = width // shards
    parts = 2 * shards
    head_cols = width // parts
    feed_cols = gate_weight.shape[1] // parts
    seq_len = rows * 2 * planes
    everything = 2 * rows * shards

    def swap_cores(values):
        return jnp.where(core == 0, values, values[::-1])

    def plane_relative(values):
        return jnp.stack(
            [
                lax.dynamic_index_in_dim(values, (shard ^ k) * 2 + (core ^ r), 0, keepdims=False)
                for r in range(2)
                for k in range(shards)
            ]
        )

    def plane_absolute(values):
        return jnp.stack(
            [
                lax.dynamic_index_in_dim(values, (core ^ r) * shards + (shard ^ j), 0, keepdims=False)
                for j in range(shards)
                for r in range(2)
            ]
        )

    by_chunk = tokens.reshape(rows, shards, chunk).transpose(1, 0, 2)
    by_seq = lax.all_to_all(by_chunk, "shard", 0, 0, tiled=True)
    mine = lax.all_to_all(by_seq, "z", 0, 0, tiled=True).reshape(planes * rows, chunk)

    def column_block(weight, k, cols):
        return lax.dynamic_slice_in_dim(weight, ((shard ^ k) * 2 + core) * cols, cols, 1)

    def input_block(k):
        return jnp.concatenate(
            [column_block(w, k, head_cols) for w in (query_weight, key_weight, value_weight)], 1
        )

    def feed_block(k):
        return jnp.concatenate([column_block(w, k, feed_cols) for w in (gate_weight, up_weight)], 1)

    input_blocks = [input_block(0)] + [send_shard(input_block(k), k) for k in range(1, shards)]
    whole_input = jnp.concatenate(input_blocks, 0)
    feed_blocks = [feed_block(0)] + [send_shard(feed_block(k), k) for k in range(1, shards)]
    whole_feed = jnp.zeros((width, 2 * feed_cols), BF)
    for k in range(shards):
        whole_feed = lax.dynamic_update_slice_in_dim(whole_feed, feed_blocks[k], (shard ^ k) * chunk, 0)
    out_block = lax.dynamic_slice_in_dim(output_weight, core * head_cols, head_cols, 0)
    down_block = lax.dynamic_slice_in_dim(down_weight, core * feed_cols, feed_cols, 0)
    gains = lax.all_gather(jnp.stack([attention_gain, feed_gain]), "shard", axis=1, tiled=True).astype(F32)
    query_gain_here = lax.dynamic_slice_in_dim(query_gain, core * head_cols, head_cols, 0).astype(F32)
    key_gain_here = lax.dynamic_slice_in_dim(key_gain, core * head_cols, head_cols, 0).astype(F32)
    info = jnp.stack([piece_index[0], pad_flags[0]]).astype(BF)
    info_all = lax.all_gather(info, ("z", "core", "shard"), axis=0)
    info_all = info_all.reshape(planes, 2, shards, 2, rows)
    info_seq = lax.dynamic_index_in_dim(info_all, plane, 2, keepdims=False).astype(F32)
    piece_seq = info_seq[:, :, 0].reshape(seq_len)
    pad_seq = info_seq[:, :, 1].reshape(seq_len)
    block_flags = (piece_seq.reshape(-1, PIECE)[:, 0] >= 0.0).astype(jnp.int32)
    key_bias = jnp.where(pad_seq > 0.0, masked_score, 0.0)[:, None]

    gathered = gather_plane(mine)
    inputs_here = jnp.concatenate([jnp.concatenate(blocks, 1) for blocks in gathered], 0)
    raw = mm(inputs_here, whole_input).reshape(2, planes, rows, 3 * head_cols)
    raw = swap_cores(raw).transpose(1, 0, 2, 3).reshape(seq_len, 3 * head_cols)
    query_raw = raw[:, :head_cols]
    key_raw = raw[:, head_cols : 2 * head_cols]
    value_low = raw[:, 2 * head_cols :].astype(BF)
    squares = sum_plane(
        jnp.stack([jnp.sum(query_raw * query_raw, -1), jnp.sum(key_raw * key_raw, -1)])
    )
    factors = lax.rsqrt(squares / width + epsilon)
    query_factor, key_factor = factors[0][:, None], factors[1][:, None]
    rates = theta_base ** (-jnp.arange(HEAD // 2).astype(F32) * (2.0 / HEAD))
    angles = jnp.arange(seq_len, dtype=jnp.int32).astype(F32)[:, None] * rates[None, :]
    cosine, sine = jnp.cos(angles), jnp.sin(angles)
    heads_here = head_cols // HEAD

    def turn(values, factor, gain):
        normed = (values * factor * gain).reshape(seq_len, heads_here, HEAD)
        return rotate(normed, cosine, sine).reshape(seq_len, head_cols).astype(BF)

    query_low = turn(query_raw, query_factor, query_gain_here)
    key_low = turn(key_raw, key_factor, key_gain_here)
    attended_seq, lse = attend_forward(query_low, key_low, value_low, key_bias, block_flags)

    attended = lax.all_to_all(
        attended_seq.reshape(planes, 2 * rows, head_cols), "z", 0, 0, tiled=True
    ).reshape(parts, rows, head_cols)
    attended = plane_relative(attended).reshape(everything, head_cols)
    half = everything // 2

    def blocks_of(values):
        return values.reshape(shards, rows, values.shape[-1])

    branch_attn = reduce_plane(
        blocks_of(mm(attended[half:], out_block)), blocks_of(mm(attended[:half], out_block))
    )
    attn_factor = norm_factor(branch_attn)
    residual = tokens.astype(F32) + branch_attn * attn_factor * gains[0]
    gathered = gather_plane(residual.astype(BF))
    residual_all = jnp.concatenate(gathered[0] + gathered[1], 0)
    gate = mm(residual_all, whole_feed[:, :feed_cols])
    up = mm(residual_all, whole_feed[:, feed_cols:])
    activated = (jax.nn.silu(gate) * up).astype(BF)
    branch_feed = reduce_plane(
        blocks_of(mm(activated[half:], down_block)), blocks_of(mm(activated[:half], down_block))
    )
    feed_factor = norm_factor(branch_feed)
    result = residual + branch_feed * feed_factor * gains[1]

    grad_out = cotangent[0].astype(F32)
    grad_feed, grad_feed_gain = norm_back(branch_feed, feed_factor, gains[1], grad_out)
    gathered = gather_plane(grad_feed.astype(BF))
    grad_feed_all = jnp.concatenate(gathered[0] + gathered[1], 0)
    grad_act = contract_cols(grad_feed_all, down_block)
    grad_down = contract_rows(activated, grad_feed_all).astype(BF)
    down_part = lax.psum_scatter(grad_down, "z", scatter_dimension=0, tiled=True)
    sigmoid = jax.nn.sigmoid(gate)
    grad_gate = (grad_act * up * sigmoid * (1.0 + gate * (1.0 - sigmoid))).astype(BF)
    grad_up = (grad_act * gate * sigmoid).astype(BF)
    grad_both = jnp.concatenate([grad_gate, grad_up], 1)
    grad_feed_in = reduce_plane(
        blocks_of(contract_cols(grad_both[half:], whole_feed)),
        blocks_of(contract_cols(grad_both[:half], whole_feed)),
    )

    def scatter_rows(term):
        cols = term.shape[1]
        term = term.astype(BF).reshape(shards, planes, chunk // planes, cols).transpose(1, 0, 2, 3)
        part = lax.psum_scatter(term.reshape(width, cols), "z", scatter_dimension=0, tiled=True)
        return part.reshape(shards, chunk // planes, cols)

    feed_part = scatter_rows(contract_rows(residual_all, grad_both))

    grad_resid = grad_out + grad_feed_in
    grad_branch, grad_attention_gain = norm_back(branch_attn, attn_factor, gains[0], grad_resid)
    gathered = gather_plane(grad_branch.astype(BF))
    grad_branch_all = jnp.concatenate(gathered[0] + gathered[1], 0)
    grad_mixed = contract_cols(grad_branch_all, out_block).astype(BF)
    grad_output = contract_rows(attended, grad_branch_all).astype(BF)
    grad_mixed = plane_absolute(grad_mixed.reshape(parts, rows, head_cols))
    grad_mixed = lax.all_to_all(
        grad_mixed.reshape(shards, 2 * rows, head_cols), "z", 0, 0, tiled=True
    ).reshape(seq_len, head_cols)
    delta = jnp.sum(
        (grad_mixed.astype(F32) * attended_seq.astype(F32)).reshape(seq_len, heads_here, HEAD), -1
    ).T.reshape(heads_here, 1, seq_len)
    grad_queries, grad_keys, grad_values = attend_backward(
        query_low, key_low, value_low, grad_mixed, key_bias, block_flags, lse, delta
    )

    def turn_back(grad, values, factor, gain):
        turned = rotate_back(grad.reshape(seq_len, heads_here, HEAD), cosine, sine)
        turned = turned.reshape(seq_len, head_cols)
        scaled = turned * gain
        return scaled, jnp.sum(values * scaled, -1), jnp.sum(turned * values * factor, 0)

    query_scaled, query_inner, grad_query_gain = turn_back(
        grad_queries, query_raw, query_factor, query_gain_here
    )
    key_scaled, key_inner, grad_key_gain = turn_back(grad_keys, key_raw, key_factor, key_gain_here)
    inner = sum_plane(jnp.stack([query_inner, key_inner])) / width

    def finish(scaled, values, factor, inner_row):
        return (factor * scaled - values * (factor * factor * factor) * inner_row[:, None]).astype(BF)

    grad_raw = jnp.concatenate(
        [
            finish(query_scaled, query_raw, query_factor, inner[0]),
            finish(key_scaled, key_raw, key_factor, inner[1]),
            grad_values,
        ],
        1,
    )
    grad_raw = grad_raw.reshape(planes, 2, rows, 3 * head_cols).transpose(1, 0, 2, 3)
    grad_raw = swap_cores(grad_raw).reshape(seq_len, 3 * head_cols)
    seq_half = seq_len // 2

    def chunks_of(values):
        return jnp.stack([contract_cols(values, block) for block in input_blocks])

    grad_chunk = reduce_plane(chunks_of(grad_raw[seq_half:]), chunks_of(grad_raw[:seq_half]))
    grad_chunk = grad_chunk.astype(BF).reshape(planes, rows, chunk)
    grad_chunk = lax.all_to_all(grad_chunk, "z", 0, 0, tiled=True)
    grad_chunk = lax.all_to_all(grad_chunk, "shard", 0, 0, tiled=True)
    grad_tokens = grad_resid + grad_chunk.transpose(1, 0, 2).reshape(rows, width).astype(F32)

    input_part = scatter_rows(contract_rows(inputs_here, grad_raw))
    output_part = lax.psum_scatter(grad_output, "z", scatter_dimension=0, tiled=True)

    def to_owner(part, is_relative):
        blocks = []
        for k in range(shards):
            block = part[k] if is_relative else lax.dynamic_index_in_dim(part, shard ^ k, 0, keepdims=False)
            blocks.append(send_shard(block, k) if k else block)
        stacked = jnp.stack(blocks)
        return jnp.stack(
            [lax.dynamic_index_in_dim(stacked, shard ^ j, 0, keepdims=False) for j in range(shards)]
        )

    def copies(values):
        return lax.all_gather(values, ("z", "core"), axis=0).reshape((planes, 2) + values.shape)

    down_all = copies(down_part)
    grad_down_weight = down_all.transpose(1, 0, 2, 3).reshape(down_weight.shape).astype(F32)
    feed_all = copies(to_owner(feed_part, False))

    def wide(values, weight):
        return values.transpose(0, 3, 2, 1, 4).reshape(weight.shape).astype(F32)

    grad_gate_weight = wide(feed_all[..., :feed_cols], gate_weight)
    grad_up_weight = wide(feed_all[..., feed_cols:], up_weight)
    output_all = copies(output_part)
    grad_output_weight = output_all.transpose(1, 0, 2, 3).reshape(output_weight.shape).astype(F32)
    input_all = copies(to_owner(input_part, True))
    grad_inputs = [
        wide(input_all[..., i * head_cols : (i + 1) * head_cols], query_weight) for i in range(3)
    ]

    valid = (pad_flags[0] == 0).astype(F32)[:, None]
    stat_terms = jnp.stack(
        [
            jnp.sum(valid * result * result),
            jnp.sum(valid * branch_attn * branch_attn),
            jnp.sum(valid * branch_feed * branch_feed),
            jnp.sum(valid),
        ]
    )
    place = (shard * 2 + core) * head_cols
    blank = jnp.zeros((2, width), F32)
    gain_heads = lax.dynamic_update_slice(
        blank, jnp.stack([grad_query_gain, grad_key_gain]), (jnp.int32(0), place)
    )
    terms = jnp.concatenate(
        [
            gain_heads.reshape(-1),
            grad_attention_gain,
            grad_feed_gain,
            stat_terms,
        ]
    )
    terms = lax.psum(terms, ("z", "core", "shard"))
    gain_terms = terms[: 4 * width].reshape(4, width)
    gain_width = query_gain.shape[0]
    gain_mine = lax.dynamic_slice_in_dim(gain_terms, shard * gain_width, gain_width, 1)
    stat_terms = terms[4 * width :]
    stats = jnp.sqrt(stat_terms[:3] / (stat_terms[3] * width))
    return (
        result[None],
        grad_tokens[None],
        grad_inputs[0],
        grad_inputs[1],
        grad_inputs[2],
        grad_output_weight,
        grad_gate_weight,
        grad_up_weight,
        grad_down_weight,
        gain_mine[0],
        gain_mine[1],
        gain_mine[2],
        gain_mine[3],
        stats,
    )


def solution(mesh):
    devices = mesh.devices.reshape(mesh.shape["replica"] // 2, 2, mesh.shape["shard"])
    split = Mesh(devices, ("z", "core", "shard"))
    tokens = ("z", "core")
    placed = (
        (P("shard", tokens, None), P("shard", tokens), P("shard", tokens), P("shard", tokens, None))
        + (P("shard", None),) * 7
        + (P("shard"),) * 4
    )
    return jax.shard_map(
        per_device,
        mesh=split,
        in_specs=placed,
        out_specs=(P("shard", tokens, None),) * 2
        + (P("shard", None),) * 7
        + (P("shard"),) * 4
        + (P(),),
        check_vma=False,
    )
```

time: 3690 us -> 1630 us (0.44)
  waiting for transfers between devices: 2980 us -> 613 us
  blocking collectives: 83.1 us -> 290 us
  matrix products: 339 us -> 193 us
  local copies, waits for them, and re-layouts: 166 us -> 256 us
  starting transfers between devices: 0.98 us -> 72.5 us
  other arithmetic: 92.9 us -> 155 us
    all_gather x9 -> x4, waiting for transfers between devices: 1170 us -> 104 us  [copies(): lax.all_gather(values, ('z', 'core'), axis=0)]
    unnamed x17 -> x8, waiting for transfers between devices: 788 us -> 1.1 us
    psum x1 -> x0, waiting for transfers between devices: 591 us -> none  [per_device(): lax.psum(input_share.astype(jnp.bfloat16), 'replica').astype(jnp.float32)]
    ppermute x0 -> x70, waiting for transfers between devices: none -> 293 us  [the longest x48 277 us: send_shard(): return lax.ppermute(values, 'shard', [(i, i ^ k) for i in range(count)])]
    reduce_scatter x3 -> x4, waiting for transfers between devices: 431 us -> 159 us  [the longest x2 159 us: scatter_rows(): lax.psum_scatter(term.reshape(width, cols), 'z', scatter_dimension=0, til...]
    convert_element_type x0 -> x13, local copies, waits for them, and re-layouts: none -> 147 us  [the longest x10 132 us: wide(): return values.transpose(0, 3, 2, 1, 4).reshape(weight.shape).astype(F32)]
    all_gather x5 -> x2, blocking collectives: 42 us -> 184 us  [the longest x1 108 us: per_device(): lax.all_gather(jnp.stack([attention_gain, feed_gain]), 'shard', axis=1, t...]
    dot_general x35 -> x7, matrix products: 197 us -> 66.5 us  [mm(): return jnp.dot(left, right, preferred_element_type=F32)]
  transfers between devices with their start and end apart: 15 -> 82, of which waited for: 14 -> 49; matrix products, arithmetic and copies ran while one was open for 9% -> 19% of each run, Pallas kernels for 0% -> 1%
where the time goes in v1:
time: 1630 us
  waiting for transfers between devices  613 us (38%)
  blocking collectives  290 us (18%)
  local copies, waits for them, and re-layouts  256 us (16%)
  matrix products  193 us (12%)
  other arithmetic  155 us (10%)
  starting transfers between devices  72.5 us (4%)
  Pallas kernels  28.9 us (2%)
  between operations  16.8 us (1%)
    ppermute x48, waiting for transfers between devices, send_shard(): return lax.ppermute(values, 'shard', [(i, i ^ k) for i in range(count)])  277 us
    reduce_scatter x2, waiting for transfers between devices, scatter_rows(): lax.psum_scatter(term.reshape(width, cols), 'z', scatter_dimension=0, til...  159 us
    convert_element_type x10, local copies, waits for them, and re-layouts, wide(): return values.transpose(0, 3, 2, 1, 4).reshape(weight.shape).astype(F32)  132 us
    all_gather x1, blocking collectives, per_device(): lax.all_gather(jnp.stack([attention_gain, feed_gain]), 'shard', axis=1, t...  108 us
    all_gather x4, waiting for transfers between devices, copies(): lax.all_gather(values, ('z', 'core'), axis=0)  104 us
    all_gather x1, blocking collectives, per_device(): info_all = lax.all_gather(info, ('z', 'core', 'shard'), axis=0)  75.5 us
    dot_general x7, matrix products, mm(): return jnp.dot(left, right, preferred_element_type=F32)  66.5 us
    dot_general x12, matrix products, contract_cols(): lax.dot_general(left, right, (((1,), (1,)), ((), ())), preferred_element_...  65 us
  transfers between devices with their start and end apart: 82, of which 49 were waited for; matrix products, arithmetic and copies ran while one was open for 19% of the time, Pallas kernels for 1%

profile of v1, /device:TPU:0, one launch (start us, length us, event | category | flops | bytes accessed | tf_op | source)
XLA Modules:
  0.0 1626.0 jit_solution(2661995967214960759)
XLA Ops:
  8.8 19.1 %all_to_all.30 = bf16[4,256,512]{1,2,0:T(8,128)(2,1)S(1)} all-to-all(bf16[4,256,512]{1,2,0:T(8,128)(2,1)S(1)} %bitcast.365), channel_id=1, replica_groups=mesh['z'=4,'core'=2,'shard'=4] {'shard'}, dimensions={0} | all-to-all | bytes 2097152 | tf_op jit(solution)/shard_map/all_to_all | solution.py:257
  27.9 28.8 %all_to_all.31 = bf16[4,256,512]{1,2,0:T(8,128)(2,1)S(1)} all-to-all(bf16[4,256,512]{1,2,0:T(8,128)(2,1)S(1)} %all_to_all.30), channel_id=1, replica_groups=mesh['z'=4,'core'=2,'shard'=4] {'z'}, dimensions={0} | all-to-all | bytes 2097152 | tf_op jit(solution)/shard_map/all_to_all | solution.py:258
  65.6 18.9 %collective-permute-done = bf16[1024,512]{1,0:T(8,128)(2,1)} collective-permute-done((bf16[1024,512]{1,0:T(8,128)(2,1)}, bf16[1024,512]{1,0:T(8,128)(2,1)}, u32[]{:S(2)}, u32[]{:S(2)}) %collective-permute-start) | collective-permute-done | bytes 1048608 | tf_op jit(solution)/shard_map/ppermute | solution.py:39
  86.9 13.0 collective-permute-done.1
  115.4 12.4 collective-permute-done.9
  128.7 75.5 %all_gather.31 = bf16[32,2,256]{2,1,0:T(2,128)(2,1)S(1)} all-gather(bf16[1,2,256]{2,1,0:T(2,128)(2,1)S(1)} %pad_maximum_fusion.37), channel_id=1, replica_groups=mesh['z'=4,'core'=2,'shard'=4] {'z','core','shard'}, dimensions={0}, use_global_device_ids=true | all-gather | bytes 33792 | tf_op jit(solution)/shard_map/all_gather | solution.py:283
  210.0 13.3 fusion.21
  252.0 9.1 subtract_convert_fusion.3
  267.3 11.4 attend_forward.1
  284.3 24.5 %all-to-all-done.2 = bf16[4,512,256]{2,1,0:T(8,128)(2,1)S(1)} async-done(((bf16[4,512,256]{2,1,0:T(8,128)(2,1)}), bf16[4,512,256]{2,1,0:T(8,128)(2,1)S(1)}, u32[]{:S(2)}, u32[]{:S(2)}) %all-to-all-start.2) | async-done | bytes 1048608 | tf_op jit(solution)/shard_map/all_to_all | solution.py:316
  350.3 108.4 %all_gather.32 = bf16[2,2048]{1,0:T(2,128)(2,1)S(1)} all-gather(bf16[2,512]{1,0:T(2,128)(2,1)S(1)} %pad_maximum_fusion.36), channel_id=1, replica_groups=mesh['z'=4,'core'=2,'shard'=4] {'shard'}, dimensions={1}, use_global_device_ids=true | all-gather | bytes 10240 | tf_op jit(solution)/shard_map/all_gather | solution.py:279
  469.9 14.2 collective-permute-done.19
  503.3 11.7 fusion.11
  515.0 16.9 %multiply_convert_fusion.2 = (bf16[2048,1024]{0,1:T(8,128)(2,1)S(1)}, f32[2048,1024]{0,1:T(8,128)}) fusion(f32[2048,1024]{0,1:T(8,128)} %fusion.11, bf16[2048,2048]{1,0:T(8,128)(2,1)} %copy-done.41, bf16[2048,2048]{1,0:T(8,128)(2,1)} %copy-done.21), kind=kOutput, calls=%fused_computation.16 | convolution fusion | flops 8602517504 | bytes 33554432 | tf_op jit(solution)/shard_map/dot_general | solution.py:22
  540.9 9.0 fusion.19
  551.9 10.2 fusion.126
  564.4 12.2 collective-permute-done.31
  581.1 22.1 %collective-permute-done.34 = bf16[256,2048]{1,0:T(8,128)(2,1)S(1)} collective-permute-done((bf16[256,2048]{1,0:T(8,128)(2,1)S(1)}, bf16[256,2048]{1,0:T(8,128)(2,1)S(1)}, u32[]{:S(2)}, u32[]{:S(2)}) %collective-permute-start.34) | collective-permute-done | bytes 1048608 | tf_op jit(solution)/shard_map/ppermute | solution.py:39
  611.4 21.1 %collective-permute-done.35 = bf16[256,2048]{1,0:T(8,128)(2,1)S(1)} collective-permute-done((bf16[256,2048]{1,0:T(8,128)(2,1)S(1)}, bf16[256,2048]{1,0:T(8,128)(2,1)S(1)}, u32[]{:S(2)}, u32[]{:S(2)}) %collective-permute-start.35) | collective-permute-done | bytes 1048608 | tf_op jit(solution)/shard_map/ppermute | solution.py:39
  650.4 21.2 %multiply_convert_fusion = (bf16[2048,1024]{0,1:T(8,128)(2,1)}, bf16[2048,1024]{0,1:T(8,128)(2,1)}) fusion(f32[2048,1024]{0,1:T(8,128)} %fusion.11, f32[2048,1024]{0,1:T(8,128)} %get-tuple-element.182, bf16[2048,2048]{1,0:T(8,128)(2,1)} %copy-done.42, bf16[2048,2048]{1,0:T(8,128)(2,1)} %param.25, s32[]{:T(128)S(6)} %select_n.187), kind=kOutput, calls=%fused_computation.13 | convolution fusion | flops 8617197568 | bytes 37748740 | tf_op jit(solution)/shard_map/dot_general | solution.py:30
  671.6 12.6 fusion.13
  684.4 14.8 fusion.4
  699.2 11.7 fusion.123
  714.6 12.2 collective-permute-done.44
  732.2 22.1 %collective-permute-done.47 = bf16[256,2048]{1,0:T(8,128)(2,1)S(1)} collective-permute-done((bf16[256,2048]{1,0:T(8,128)(2,1)S(1)}, bf16[256,2048]{1,0:T(8,128)(2,1)S(1)}, u32[]{:S(2)}, u32[]{:S(2)}) %collective-permute-start.47) | collective-permute-done | bytes 1048608 | tf_op jit(solution)/shard_map/ppermute | solution.py:39
  764.0 21.1 %collective-permute-done.48 = bf16[256,2048]{1,0:T(8,128)(2,1)S(1)} collective-permute-done((bf16[256,2048]{1,0:T(8,128)(2,1)S(1)}, bf16[256,2048]{1,0:T(8,128)(2,1)S(1)}, u32[]{:S(2)}, u32[]{:S(2)}) %collective-permute-start.48) | collective-permute-done | bytes 1048608 | tf_op jit(solution)/shard_map/ppermute | solution.py:39
  826.9 13.8 convolution_convert_fusion
  840.8 23.7 %all-to-all-done.3 = bf16[4,512,256]{2,1,0:T(8,128)(2,1)S(1)} async-done(((bf16[4,512,256]{2,1,0:T(8,128)(2,1)}), bf16[4,512,256]{2,1,0:T(8,128)(2,1)S(1)}, u32[]{:S(2)}, u32[]{:S(2)}) %all-to-all-start.3) | async-done | bytes 1048608 | tf_op jit(solution)/shard_map/all_to_all | solution.py:372
  875.4 17.5 %attend_backward.1 = (f32[2048,256]{1,0:T(8,128)}, f32[2048,256]{1,0:T(8,128)}, bf16[2048,256]{1,0:T(8,128)(2,1)}) custom-call(s32[8]{0:T(128)} %copy-done.9, bf16[2048,256]{1,0:T(8,128)(2,1)} %bitcast.324, bf16[2048,256]{1,0:T(8,128)(2,1)} %bitcast.326, bf16[2048,256]{1,0:T(8,128)(2,1)} %slice.726.values, bf16[2048,256]{1,0:T(8,128)(2,1)} %bitcast.346, ...), custom_call_target="tpu_custom_call" | custom-call | tf_op jit(solution)/shard_map/attend_backward/pallas_call | solution.py:161
  898.5 10.5 multiply_subtract_fusion.1
  931.3 20.1 %convolution_convert_fusion.3 = bf16[2048,768]{1,0:T(8,128)(2,1)} fusion(bf16[2048,768]{1,0:T(8,128)(2,1)} %bitcast.342, bf16[1024,512]{1,0:T(8,128)(2,1)} %collective-permute-done.7, bf16[1024,512]{1,0:T(8,128)(2,1)} %collective-permute-done.6, bf16[1024,512]{1,0:T(8,128)(2,1)} %collective-permute-done.5, bf16[1024,512]{1,0:T(8,128)(2,1)} %collective-permute-done.4, ...), kind=kOutput, calls=%fused_computation.39 | convolution fusion | flops 6511132672 | bytes 14680064 | tf_op jit(solution)/shard_map/dot_general | solution.py:26
  955.4 24.1 %fusion.1 = bf16[2048,2048]{1,0:T(8,128)(2,1)} fusion(bf16[2048,2048]{1,0:T(8,128)(2,1)} %copy-done.41, bf16[2048,1024]{0,1:T(8,128)(2,1)} %get-tuple-element.75, bf16[2048,1024]{0,1:T(8,128)(2,1)} %get-tuple-element.76), kind=kOutput, calls=%fused_computation.19 | convolution fusion | flops 17200840704 | bytes 25165824 | tf_op jit(solution)/shard_map/dot_general | solution.py:26
  989.2 25.5 %reduce-scatter.5.cloned.1.call-done = bf16[512,768]{1,0:T(8,128)(2,1)} async-done(((bf16[2048,768]{1,0:T(8,128)(2,1)}), bf16[512,768]{1,0:T(8,128)(2,1)}) %reduce-scatter.5.cloned.1.call-update) | async-done | bytes 786448 | tf_op jit(solution)/shard_map/reduce_scatter | solution.py:360
  1028.9 133.1 %reduce-scatter.9.cloned.1.call-done = bf16[512,2048]{1,0:T(8,128)(2,1)} async-done(((bf16[2048,2048]{1,0:T(8,128)(2,1)}), bf16[512,2048]{1,0:T(8,128)(2,1)}) %reduce-scatter.9.cloned.1.call-update) | async-done | bytes 2097168 | tf_op jit(solution)/shard_map/reduce_scatter | solution.py:360
  1167.3 12.3 collective-permute-done.69
  1179.6 9.9 collective-permute-done.68
  1211.4 11.7 collective-permute-done.60
  1227.1 21.9 %collective-permute-done.63 = bf16[1024,512]{1,0:T(8,128)(2,1)S(1)} collective-permute-done((bf16[1024,512]{1,0:T(8,128)(2,1)S(1)}, bf16[1024,512]{1,0:T(8,128)(2,1)S(1)}, u32[]{:S(2)}, u32[]{:S(2)}) %collective-permute-start.63) | collective-permute-done | bytes 1048608 | tf_op jit(solution)/shard_map/ppermute | solution.py:39
  1258.9 58.6 %psum.7 = f32[8196]{0:T(1024)S(1)} all-reduce(f32[8196]{0:T(1024)S(1)} %concatenate.158), channel_id=1, replica_groups=mesh['z'=4,'core'=2,'shard'=4] {'z','core','shard'}, use_global_device_ids=true, to_apply=%region_21.22 | all-reduce | flops 8196 | bytes 65568 | tf_op jit(solution)/shard_map/psum | solution.py:472
  1328.0 8.9 all-to-all-done.5
  1339.0 11.8 convert_bitcast_fusion
  1350.8 11.9 copy.76
  1410.6 103.5 %all-gather.13.cloned.1.call-done = bf16[32,128,2048]{2,1,0:T(8,128)(2,1)} async-done(((bf16[4,128,2048]{2,1,0:T(8,128)(2,1)}), bf16[32,128,2048]{2,1,0:T(8,128)(2,1)}) %all-gather.13.cloned.1.call-update) | async-done | bytes 16777232 | tf_op jit(solution)/shard_map/all_gather | solution.py:432
  1514.1 12.6 convert_bitcast_fusion.1
  1526.7 19.2 %copy.74 = f32[4,128,4,2,1024]{4,3,2,1,0:T(2,128)} copy(f32[4,128,4,2,1024]{4,1,2,3,0:T(8,128)S(1)} %get-tuple-element.74) | data formatting | bytes 33554432 | tf_op jit(solution)/shard_map/convert_element_type | solution.py:439
  1545.9 22.1 %reshape.490 = f32[512,8192]{1,0:T(8,128)} reshape(f32[4,128,4,2,1024]{4,3,2,1,0:T(2,128)} %copy.74) | data formatting | bytes 33554432 | tf_op jit(solution)/shard_map/convert_element_type | solution.py:439
  1568.0 28.7 %copy.75 = f32[4,128,4,2,1024]{4,3,2,1,0:T(2,128)} copy(f32[4,128,4,2,1024]{4,1,2,3,0:T(8,128)} %get-tuple-element.73) | data formatting | bytes 33554432 | tf_op jit(solution)/shard_map/convert_element_type | solution.py:439
  1596.7 22.3 %reshape.491 = f32[512,8192]{1,0:T(8,128)} reshape(f32[4,128,4,2,1024]{4,3,2,1,0:T(2,128)} %copy.75) | data formatting | bytes 33554432 | tf_op jit(solution)/shard_map/convert_element_type | solution.py:439
  (490 shorter events, 418.3 us)
Async XLA Ops:
  58.1 26.4 %collective-permute-start = (bf16[1024,512]{1,0:T(8,128)(2,1)}, bf16[1024,512]{1,0:T(8,128)(2,1)}, u32[]{:S(2)}, u32[]{:S(2)}) collective-permute-start(bf16[1024,512]{1,0:T(8,128)(2,1)} %bitcast.387), channel_id=1, source_target_pairs={{0,1},{1,0},{2,3},{3,2},{4,5},{5,4},{6,7},{7,6},{8,9},{9,8},{10,11... | collective-permute-start | bytes 3145736 | tf_op jit(solution)/shard_map/ppermute | solution.py:39
  59.4 40.5 %collective-permute-start.1 = (bf16[1024,512]{1,0:T(8,128)(2,1)}, bf16[1024,512]{1,0:T(8,128)(2,1)}, u32[]{:S(2)}, u32[]{:S(2)}) collective-permute-start(bf16[1024,512]{1,0:T(8,128)(2,1)} %bitcast.388), channel_id=1, source_target_pairs={{0,2},{1,3},{2,0},{3,1},{4,6},{5,7},{6,4},{7,5},{8,10},{9,11},{10,... | collective-permute-start | bytes 3145736 | tf_op jit(solution)/shard_map/ppermute | solution.py:39
  63.9 50.5 %collective-permute-start.10 = (bf16[512,768]{1,0:T(8,128)(2,1)S(1)}, bf16[512,768]{1,0:T(8,128)(2,1)S(1)}, u32[]{:S(2)}, u32[]{:S(2)}) collective-permute-start(bf16[512,768]{1,0:T(8,128)(2,1)S(1)} %pad_maximum_fusion.29), channel_id=1, source_target_pairs={{0,3},{1,2},{2,1},{3,0},{4,7},{5,6},{6,5},{7,4},{8,11},{9,10},{10,... | collective-permute-start | bytes 2359304 | tf_op jit(solution)/shard_map/ppermute | solution.py:39
  85.6 26.5 %collective-permute-start.2 = (bf16[512,512]{1,0:T(8,128)(2,1)S(1)}, bf16[512,512]{1,0:T(8,128)(2,1)S(1)}, u32[]{:S(2)}, u32[]{:S(2)}) collective-permute-start(bf16[512,512]{1,0:T(8,128)(2,1)S(1)} %slice.501), channel_id=1, source_target_pairs={{0,2},{1,3},{2,0},{3,1},{4,6},{5,7},{6,4},{7,5},{8,10},{9,11},{10,... | collective-permute-start | bytes 1572872 | tf_op jit(solution)/shard_map/ppermute | solution.py:39
  101.5 26.3 %collective-permute-start.9 = (bf16[512,768]{1,0:T(8,128)(2,1)S(1)}, bf16[512,768]{1,0:T(8,128)(2,1)S(1)}, u32[]{:S(2)}, u32[]{:S(2)}) collective-permute-start(bf16[512,768]{1,0:T(8,128)(2,1)S(1)} %pad_maximum_fusion.28), channel_id=1, source_target_pairs={{0,2},{1,3},{2,0},{3,1},{4,6},{5,7},{6,4},{7,5},{8,10},{9,11},{10,... | collective-permute-start | bytes 2359304 | tf_op jit(solution)/shard_map/ppermute | solution.py:39
  103.4 106.5 %collective-permute-start.4 = (bf16[1024,512]{1,0:T(8,128)(2,1)S(1)}, bf16[1024,512]{1,0:T(8,128)(2,1)}, u32[]{:S(2)}, u32[]{:S(2)}) collective-permute-start(bf16[1024,512]{1,0:T(8,128)(2,1)S(1)} %bitcast.389), channel_id=1, source_target_pairs={{0,4},{4,0},{1,5},{5,1},{2,6},{6,2},{3,7},{7,3},{8,12},{12,8},{9,1... | collective-permute-start | bytes 3145736 | tf_op jit(solution)/shard_map/ppermute | solution.py:34
  112.1 97.8 %collective-permute-start.6 = (bf16[1024,512]{1,0:T(8,128)(2,1)}, bf16[1024,512]{1,0:T(8,128)(2,1)}, u32[]{:S(2)}, u32[]{:S(2)}) collective-permute-start(bf16[1024,512]{1,0:T(8,128)(2,1)} %collective-permute-done.1), channel_id=1, source_target_pairs={{0,4},{4,0},{1,5},{5,1},{2,6},{6,2},{3,7},{7,3},{8,12},{12,8},{9,1... | collective-permute-start | bytes 3145736 | tf_op jit(solution)/shard_map/ppermute | solution.py:34
  113.0 97.0 %collective-permute-start.5 = (bf16[1024,512]{1,0:T(8,128)(2,1)}, bf16[1024,512]{1,0:T(8,128)(2,1)}, u32[]{:S(2)}, u32[]{:S(2)}) collective-permute-start(bf16[1024,512]{1,0:T(8,128)(2,1)} %collective-permute-done), channel_id=1, source_target_pairs={{0,4},{4,0},{1,5},{5,1},{2,6},{6,2},{3,7},{7,3},{8,12},{12,8},{9,1... | collective-permute-start | bytes 3145736 | tf_op jit(solution)/shard_map/ppermute | solution.py:34
  114.3 95.6 %collective-permute-start.7 = (bf16[1024,512]{1,0:T(8,128)(2,1)}, bf16[1024,512]{1,0:T(8,128)(2,1)}, u32[]{:S(2)}, u32[]{:S(2)}) collective-permute-start(bf16[1024,512]{1,0:T(8,128)(2,1)} %constant_dynamic-update-slice_fusion), channel_id=1, source_target_pairs={{0,4},{4,0},{1,5},{5,1},{2,6},{6,2},{3,7},{7,3},{8,12},{12,8},{9,1... | collective-permute-start | bytes 3145736 | tf_op jit(solution)/shard_map/ppermute | solution.py:34
  127.8 82.2 %collective-permute-start.8 = (bf16[512,768]{1,0:T(8,128)(2,1)}, bf16[512,768]{1,0:T(8,128)(2,1)}, u32[]{:S(2)}, u32[]{:S(2)}) collective-permute-start(bf16[512,768]{1,0:T(8,128)(2,1)} %pad_maximum_fusion.27), channel_id=1, source_target_pairs={{0,1},{1,0},{2,3},{3,2},{4,5},{5,4},{6,7},{7,6},{8,9},{9,8},{10,11... | collective-permute-start | bytes 2359304 | tf_op jit(solution)/shard_map/ppermute | solution.py:39
  280.3 28.5 %all-to-all-start.2 = ((bf16[4,512,256]{2,1,0:T(8,128)(2,1)}), bf16[4,512,256]{2,1,0:T(8,128)(2,1)S(1)}, u32[]{:S(2)}, u32[]{:S(2)}) async-start(bf16[4,512,256]{2,1,0:T(8,128)(2,1)} %bitcast.327), calls=%async_computation.2 | async-start | bytes 2097152 | tf_op jit(solution)/shard_map/all_to_all | solution.py:316
  283.8 704.2 %reduce-scatter.7.cloned.1.call-start = ((), (), s32[]{:S(2)}) async-start(), calls=%async_computation.11 | async-start | bytes 1310720 | tf_op jit(solution)/shard_map/reduce_scatter | solution.py:419
  326.9 14.9 collective-permute-start.17
  334.5 131.3 %collective-permute-start.27 = (bf16[512,2048]{1,0:T(8,128)(2,1)}, bf16[512,2048]{1,0:T(8,128)(2,1)}, u32[]{:S(2)}, u32[]{:S(2)}) collective-permute-start(bf16[512,2048]{1,0:T(8,128)(2,1)} %pad_maximum_fusion.6), channel_id=1, source_target_pairs={{0,1},{1,0},{2,3},{3,2},{4,5},{5,4},{6,7},{7,6},{8,9},{9,8},{10,11... | collective-permute-start | bytes 6291464 | tf_op jit(solution)/shard_map/ppermute | solution.py:39
  343.3 115.4 %collective-permute-start.18 = (bf16[256,2048]{1,0:T(8,128)(2,1)S(1)}, bf16[256,2048]{1,0:T(8,128)(2,1)S(1)}, u32[]{:S(2)}, u32[]{:S(2)}) collective-permute-start(bf16[256,2048]{1,0:T(8,128)(2,1)S(1)} %pad_maximum_fusion.16), channel_id=1, source_target_pairs={{0,2},{1,3},{2,0},{3,1},{4,6},{5,7},{6,4},{7,5},{8,10},{9,11},{10,... | collective-permute-start | bytes 3145736 | tf_op jit(solution)/shard_map/ppermute | solution.py:39
  343.8 114.9 %collective-permute-start.16 = (bf16[256,2048]{1,0:T(8,128)(2,1)S(1)}, bf16[256,2048]{1,0:T(8,128)(2,1)S(1)}, u32[]{:S(2)}, u32[]{:S(2)}) collective-permute-start(bf16[256,2048]{1,0:T(8,128)(2,1)S(1)} %pad_maximum_fusion.15), channel_id=1, source_target_pairs={{0,1},{1,0},{2,3},{3,2},{4,5},{5,4},{6,7},{7,6},{8,9},{9,8},{10,11... | collective-permute-start | bytes 3145736 | tf_op jit(solution)/shard_map/ppermute | solution.py:39
  346.0 121.8 %collective-permute-start.28 = (bf16[512,2048]{1,0:T(8,128)(2,1)}, bf16[512,2048]{1,0:T(8,128)(2,1)}, u32[]{:S(2)}, u32[]{:S(2)}) collective-permute-start(bf16[512,2048]{1,0:T(8,128)(2,1)} %pad_maximum_fusion.7), channel_id=1, source_target_pairs={{0,2},{1,3},{2,0},{3,1},{4,6},{5,7},{6,4},{7,5},{8,10},{9,11},{10,... | collective-permute-start | bytes 6291464 | tf_op jit(solution)/shard_map/ppermute | solution.py:39
  349.2 139.3 %collective-permute-start.29 = (bf16[512,2048]{1,0:T(8,128)(2,1)}, bf16[512,2048]{1,0:T(8,128)(2,1)}, u32[]{:S(2)}, u32[]{:S(2)}) collective-permute-start(bf16[512,2048]{1,0:T(8,128)(2,1)} %pad_maximum_fusion.8), channel_id=1, source_target_pairs={{0,3},{1,2},{2,1},{3,0},{4,7},{5,6},{6,5},{7,4},{8,11},{9,10},{10,... | collective-permute-start | bytes 6291464 | tf_op jit(solution)/shard_map/ppermute | solution.py:39
  462.3 21.8 %collective-permute-start.19 = (bf16[256,2048]{1,0:T(8,128)(2,1)}, bf16[256,2048]{1,0:T(8,128)(2,1)}, u32[]{:S(2)}, u32[]{:S(2)}) collective-permute-start(bf16[256,2048]{1,0:T(8,128)(2,1)} %get-tuple-element.70), channel_id=1, source_target_pairs={{0,1},{1,0},{2,3},{3,2},{4,5},{5,4},{6,7},{7,6},{8,9},{9,8},{10,11... | collective-permute-start | bytes 3145736 | tf_op jit(solution)/shard_map/ppermute | solution.py:39
  463.6 23.1 %collective-permute-start.20 = (bf16[256,2048]{1,0:T(8,128)(2,1)}, bf16[256,2048]{1,0:T(8,128)(2,1)}, u32[]{:S(2)}, u32[]{:S(2)}) collective-permute-start(bf16[256,2048]{1,0:T(8,128)(2,1)} %get-tuple-element.70), channel_id=1, source_target_pairs={{0,2},{1,3},{2,0},{3,1},{4,6},{5,7},{6,4},{7,5},{8,10},{9,11},{10,... | collective-permute-start | bytes 3145736 | tf_op jit(solution)/shard_map/ppermute | solution.py:39
  578.8 24.4 %collective-permute-start.34 = (bf16[256,2048]{1,0:T(8,128)(2,1)S(1)}, bf16[256,2048]{1,0:T(8,128)(2,1)S(1)}, u32[]{:S(2)}, u32[]{:S(2)}) collective-permute-start(bf16[256,2048]{1,0:T(8,128)(2,1)S(1)} %pad_maximum_fusion.19), channel_id=1, source_target_pairs={{0,2},{1,3},{2,0},{3,1},{4,6},{5,7},{6,4},{7,5},{8,10},{9,11},{10,... | collective-permute-start | bytes 3145736 | tf_op jit(solution)/shard_map/ppermute | solution.py:39
  580.4 24.1 %collective-permute-start.32 = (bf16[256,2048]{1,0:T(8,128)(2,1)S(1)}, bf16[256,2048]{1,0:T(8,128)(2,1)S(1)}, u32[]{:S(2)}, u32[]{:S(2)}) collective-permute-start(bf16[256,2048]{1,0:T(8,128)(2,1)S(1)} %pad_maximum_fusion.18), channel_id=1, source_target_pairs={{0,1},{1,0},{2,3},{3,2},{4,5},{5,4},{6,7},{7,6},{8,9},{9,8},{10,11... | collective-permute-start | bytes 3145736 | tf_op jit(solution)/shard_map/ppermute | solution.py:39
  609.3 23.2 %collective-permute-start.35 = (bf16[256,2048]{1,0:T(8,128)(2,1)S(1)}, bf16[256,2048]{1,0:T(8,128)(2,1)S(1)}, u32[]{:S(2)}, u32[]{:S(2)}) collective-permute-start(bf16[256,2048]{1,0:T(8,128)(2,1)S(1)} %get-tuple-element.64), channel_id=1, source_target_pairs={{0,1},{1,0},{2,3},{3,2},{4,5},{5,4},{6,7},{7,6},{8,9},{9,8},{10,11... | collective-permute-start | bytes 3145736 | tf_op jit(solution)/shard_map/ppermute | solution.py:39
  610.0 23.3 %collective-permute-start.36 = (bf16[256,2048]{1,0:T(8,128)(2,1)S(1)}, bf16[256,2048]{1,0:T(8,128)(2,1)S(1)}, u32[]{:S(2)}, u32[]{:S(2)}) collective-permute-start(bf16[256,2048]{1,0:T(8,128)(2,1)S(1)} %get-tuple-element.64), channel_id=1, source_target_pairs={{0,2},{1,3},{2,0},{3,1},{4,6},{5,7},{6,4},{7,5},{8,10},{9,11},{10,... | collective-permute-start | bytes 3145736 | tf_op jit(solution)/shard_map/ppermute | solution.py:39
  684.2 15.0 collective-permute-start.43
  712.5 14.3 collective-permute-start.44
  729.9 24.4 %collective-permute-start.47 = (bf16[256,2048]{1,0:T(8,128)(2,1)S(1)}, bf16[256,2048]{1,0:T(8,128)(2,1)S(1)}, u32[]{:S(2)}, u32[]{:S(2)}) collective-permute-start(bf16[256,2048]{1,0:T(8,128)(2,1)S(1)} %pad_maximum_fusion.22), channel_id=1, source_target_pairs={{0,2},{1,3},{2,0},{3,1},{4,6},{5,7},{6,4},{7,5},{8,10},{9,11},{10,... | collective-permute-start | bytes 3145736 | tf_op jit(solution)/shard_map/ppermute | solution.py:39
  730.8 24.1 %collective-permute-start.45 = (bf16[256,2048]{1,0:T(8,128)(2,1)S(1)}, bf16[256,2048]{1,0:T(8,128)(2,1)S(1)}, u32[]{:S(2)}, u32[]{:S(2)}) collective-permute-start(bf16[256,2048]{1,0:T(8,128)(2,1)S(1)} %pad_maximum_fusion.21), channel_id=1, source_target_pairs={{0,1},{1,0},{2,3},{3,2},{4,5},{5,4},{6,7},{7,6},{8,9},{9,8},{10,11... | collective-permute-start | bytes 3145736 | tf_op jit(solution)/shard_map/ppermute | solution.py:39
  762.0 23.1 %collective-permute-start.48 = (bf16[256,2048]{1,0:T(8,128)(2,1)S(1)}, bf16[256,2048]{1,0:T(8,128)(2,1)S(1)}, u32[]{:S(2)}, u32[]{:S(2)}) collective-permute-start(bf16[256,2048]{1,0:T(8,128)(2,1)S(1)} %get-tuple-element.59), channel_id=1, source_target_pairs={{0,1},{1,0},{2,3},{3,2},{4,5},{5,4},{6,7},{7,6},{8,9},{9,8},{10,11... | collective-permute-start | bytes 3145736 | tf_op jit(solution)/shard_map/ppermute | solution.py:39
  763.3 24.0 %collective-permute-start.49 = (bf16[256,2048]{1,0:T(8,128)(2,1)S(1)}, bf16[256,2048]{1,0:T(8,128)(2,1)S(1)}, u32[]{:S(2)}, u32[]{:S(2)}) collective-permute-start(bf16[256,2048]{1,0:T(8,128)(2,1)S(1)} %get-tuple-element.59), channel_id=1, source_target_pairs={{0,2},{1,3},{2,0},{3,1},{4,6},{5,7},{6,4},{7,5},{8,10},{9,11},{10,... | collective-permute-start | bytes 3145736 | tf_op jit(solution)/shard_map/ppermute | solution.py:39
  788.9 15.5 collective-permute-start.52
  788.9 16.6 %collective-permute-start.53 = (bf16[256,2048]{1,0:T(8,128)(2,1)}, bf16[256,2048]{1,0:T(8,128)(2,1)S(1)}, u32[]{:S(2)}, u32[]{:S(2)}) collective-permute-start(bf16[256,2048]{1,0:T(8,128)(2,1)} %copy-done.26), channel_id=1, source_target_pairs={{0,4},{4,0},{1,5},{5,1},{2,6},{6,2},{3,7},{7,3},{8,12},{12,8},{9,1... | collective-permute-start | bytes 3145736 | tf_op jit(solution)/shard_map/ppermute | solution.py:34
  789.4 17.1 %collective-permute-start.54 = (bf16[256,2048]{1,0:T(8,128)(2,1)S(1)}, bf16[256,2048]{1,0:T(8,128)(2,1)S(1)}, u32[]{:S(2)}, u32[]{:S(2)}) collective-permute-start(bf16[256,2048]{1,0:T(8,128)(2,1)S(1)} %collective-permute-done.49), channel_id=1, source_target_pairs={{0,4},{4,0},{1,5},{5,1},{2,6},{6,2},{3,7},{7,3},{8,12},{12,8},{9,1... | collective-permute-start | bytes 3145736 | tf_op jit(solution)/shard_map/ppermute | solution.py:34
  823.4 41.2 %all-to-all-start.3 = ((bf16[4,512,256]{2,1,0:T(8,128)(2,1)}), bf16[4,512,256]{2,1,0:T(8,128)(2,1)S(1)}, u32[]{:S(2)}, u32[]{:S(2)}) async-start(bf16[4,512,256]{2,1,0:T(8,128)(2,1)} %bitcast.51), calls=%async_computation.3 | async-start | bytes 2097152 | tf_op jit(solution)/shard_map/all_to_all | solution.py:372
  826.9 161.8 %reduce-scatter.11.cloned.1.call-start = ((), (), s32[]{:S(2)}) async-start(), calls=%async_computation.13 | async-start | bytes 5242880 | tf_op jit(solution)/shard_map/reduce_scatter | solution.py:347
  840.8 173.9 %reduce-scatter.5.cloned.1.call-start = ((), (), s32[]{:S(2)}) async-start(), calls=%async_computation.10 | async-start | bytes 3932160 | tf_op jit(solution)/shard_map/reduce_scatter | solution.py:360
  955.4 206.7 %reduce-scatter.9.cloned.1.call-start = ((), (), s32[]{:S(2)}) async-start(), calls=%async_computation.12 | async-start | bytes 10485760 | tf_op jit(solution)/shard_map/reduce_scatter | solution.py:360
  988.0 335.6 %all-gather.11.cloned.1.call-start = ((), (), s32[]{:S(2)}) async-start(), calls=%async_computation.15 | async-start | bytes 2359296 | tf_op jit(solution)/shard_map/all_gather | solution.py:432
  988.6 350.5 %all-gather.15.cloned.1.call-start = ((), (), s32[]{:S(2)}) async-start(), calls=%async_computation.17 | async-start | bytes 9437184 | tf_op jit(solution)/shard_map/all_gather | solution.py:432
  989.1 373.6 %all-gather.9.cloned.1.call-start = ((), (), s32[]{:S(2)}) async-start(), calls=%async_computation.14 | async-start | bytes 7077888 | tf_op jit(solution)/shard_map/all_gather | solution.py:432
  1028.9 485.2 %all-gather.13.cloned.1.call-start = ((), (), s32[]{:S(2)}) async-start(), calls=%async_computation.16 | async-start | bytes 18874368 | tf_op jit(solution)/shard_map/all_gather | solution.py:432
  1163.8 15.8 collective-permute-start.69
  1166.2 23.3 %collective-permute-start.68 = (bf16[128,2048]{1,0:T(8,128)(2,1)S(1)}, bf16[128,2048]{1,0:T(8,128)(2,1)S(1)}, u32[]{:S(2)}, u32[]{:S(2)}) collective-permute-start(bf16[128,2048]{1,0:T(8,128)(2,1)S(1)} %get-tuple-element.134), channel_id=1, source_target_pairs={{0,2},{1,3},{2,0},{3,1},{4,6},{5,7},{6,4},{7,5},{8,10},{9,11},{10,... | collective-permute-start | bytes 1572872 | tf_op jit(solution)/shard_map/ppermute | solution.py:39
  1166.7 22.8 %collective-permute-start.67 = (bf16[128,2048]{1,0:T(8,128)(2,1)S(1)}, bf16[128,2048]{1,0:T(8,128)(2,1)S(1)}, u32[]{:S(2)}, u32[]{:S(2)}) collective-permute-start(bf16[128,2048]{1,0:T(8,128)(2,1)S(1)} %get-tuple-element.135), channel_id=1, source_target_pairs={{0,1},{1,0},{2,3},{3,2},{4,5},{5,4},{6,7},{7,6},{8,9},{9,8},{10,11... | collective-permute-start | bytes 1572872 | tf_op jit(solution)/shard_map/ppermute | solution.py:39
  1224.8 24.2 %collective-permute-start.63 = (bf16[1024,512]{1,0:T(8,128)(2,1)S(1)}, bf16[1024,512]{1,0:T(8,128)(2,1)S(1)}, u32[]{:S(2)}, u32[]{:S(2)}) collective-permute-start(bf16[1024,512]{1,0:T(8,128)(2,1)S(1)} %pad_maximum_fusion.25), channel_id=1, source_target_pairs={{0,2},{1,3},{2,0},{3,1},{4,6},{5,7},{6,4},{7,5},{8,10},{9,11},{10,... | collective-permute-start | bytes 3145736 | tf_op jit(solution)/shard_map/ppermute | solution.py:39
  1225.5 24.0 %collective-permute-start.61 = (bf16[1024,512]{1,0:T(8,128)(2,1)S(1)}, bf16[1024,512]{1,0:T(8,128)(2,1)S(1)}, u32[]{:S(2)}, u32[]{:S(2)}) collective-permute-start(bf16[1024,512]{1,0:T(8,128)(2,1)S(1)} %pad_maximum_fusion.24), channel_id=1, source_target_pairs={{0,1},{1,0},{2,3},{3,2},{4,5},{5,4},{6,7},{7,6},{8,9},{9,8},{10,11... | collective-permute-start | bytes 3145736 | tf_op jit(solution)/shard_map/ppermute | solution.py:39
  1250.9 68.6 %all-to-all-start.4 = ((bf16[4,256,512]{2,1,0:T(8,128)(2,1)}), bf16[4,256,512]{2,1,0:T(8,128)(2,1)}, u32[]{:S(2)}, u32[]{:S(2)}) async-start(bf16[4,256,512]{2,1,0:T(8,128)(2,1)} %bitcast.77), calls=%async_computation.4 | async-start | bytes 2097152 | tf_op jit(solution)/shard_map/all_to_all | solution.py:414
  1319.5 17.4 %all-to-all-start.5 = ((bf16[4,256,512]{2,1,0:T(8,128)(2,1)}), bf16[4,256,512]{2,1,0:T(8,128)(2,1)S(1)}, u32[]{:S(2)}, u32[]{:S(2)}) async-start(bf16[4,256,512]{2,1,0:T(8,128)(2,1)} %all-to-all-done.4), calls=%async_computation.5 | async-start | bytes 2097152 | tf_op jit(solution)/shard_map/all_to_all | solution.py:415
  (103 other events, 1671.6 us)
Sparse Core Ops, SparseCore 0:
  818.1 35.7 reduce-scatter.6
  856.9 82.7 reduce-scatter.10
  955.5 59.1 reduce-scatter.4
  1017.5 144.4 reduce-scatter.8
  1163.5 29.8 all-gather.10
  1194.8 101.6 all-gather.14
  1298.6 63.4 all-gather.8
  1364.3 149.7 all-gather.12

commit v2 on v1

v2 whole, which is shorter than its diff:
```python
import functools

import jax
import jax.numpy as jnp
from jax import lax
from jax.experimental import pallas as pl
from jax.experimental.pallas import tpu as pltpu
from jax.sharding import Mesh, PartitionSpec as P

HEADS = 16
HEAD = 128
PIECE = 256

epsilon = 1e-06
theta_base = 500000.0
masked_score = -1e30
score_scale = HEAD ** (-0.5)

BF = jnp.bfloat16
F32 = jnp.float32


def mm(left, right):
    return jnp.dot(left, right, preferred_element_type=F32)


def contract_rows(left, right):
    return lax.dot_general(left, right, (((0,), (0,)), ((), ())), preferred_element_type=F32)


def contract_cols(left, right):
    return lax.dot_general(left, right, (((1,), (1,)), ((), ())), preferred_element_type=F32)


def send_core(values):
    return lax.ppermute(values, "core", [(0, 1), (1, 0)])


def send_shard(values, k):
    count = lax.axis_size("shard")
    return lax.ppermute(values, "shard", [(i, i ^ k) for i in range(count)])


def send_plane(values, k):
    count = lax.axis_size("z")
    return lax.ppermute(values, "z", [(i, i ^ k) for i in range(count)])


def gather_shard(values):
    count = lax.axis_size("shard")
    if count != 4:
        return [values] + [send_shard(values, k) for k in range(1, count)]
    half = values.shape[0] // 2
    from_x = send_shard(values, 1)
    from_y = send_shard(values, 2)
    far_a = send_shard(from_x[:half], 2)
    far_b = send_shard(from_y[half:], 1)
    return [values, from_x, from_y, jnp.concatenate([far_a, far_b], 0)]


def gather_plane(values):
    mine = gather_shard(values)
    return [mine, [send_core(block) for block in mine]]


def reduce_shard(term):
    count = lax.axis_size("shard")
    everything = slice(None)
    if count != 4:
        result = term(0, everything)
        for k in range(1, count):
            result = result + send_shard(term(k, everything).astype(BF), k).astype(F32)
        return result
    near, far = slice(0, term.rows // 2), slice(term.rows // 2, None)
    via_x = send_shard(term(3, near).astype(BF), 1)
    via_y = send_shard(term(3, far).astype(BF), 2)
    to_y = jnp.concatenate([(term(2, near) + via_x.astype(F32)).astype(BF), term(2, far).astype(BF)], 0)
    to_x = jnp.concatenate([term(1, near).astype(BF), (term(1, far) + via_y.astype(F32)).astype(BF)], 0)
    return term(0, everything) + send_shard(to_x, 1).astype(F32) + send_shard(to_y, 2).astype(F32)


def reduce_plane(other, mine):
    got = send_core(other.astype(BF))
    mine, got = lax.optimization_barrier((mine.astype(BF), got))

    def term(k, part):
        return mine[k, part].astype(F32) + got[k, part].astype(F32)

    term.rows = mine.shape[1]
    return reduce_shard(term)


def sum_over_planes(values):
    count = lax.axis_size("z")
    step = 1
    while step < count:
        values = values + lax.ppermute(values, "z", [(i, i ^ step) for i in range(count)])
        step *= 2
    return values


def sum_plane(values, swapped=False):
    count = lax.axis_size("shard")
    other = send_core(values)
    values = values + (other[:, ::-1] if swapped else other)
    step = 1
    while step < count:
        values = values + send_shard(values, step)
        step *= 2
    return values


def terms_kernel(tokens, grads, out):
    total = contract_rows(tokens[...], grads[...]).astype(BF)
    out[...] = total.reshape(out.shape)


def weight_terms(tokens, grads, shards, planes):
    rows, width = tokens.shape
    cols = grads.shape[1]
    chunk = width // shards
    return pl.pallas_call(
        terms_kernel,
        grid=(shards,),
        in_specs=[
            pl.BlockSpec((rows, chunk), lambda i: (0, i)),
            pl.BlockSpec((rows, cols), lambda i: (0, 0), pipeline_mode=pl.Buffered(1)),
        ],
        out_specs=pl.BlockSpec((planes, 1, chunk // planes, cols), lambda i: (0, i, 0, 0)),
        out_shape=jax.ShapeDtypeStruct((planes, shards, chunk // planes, cols), BF),
        compiler_params=pltpu.CompilerParams(vmem_limit_bytes=40 * 1024 * 1024),
        name="weight_terms",
    )(tokens, grads)


def columns_kernel(copies, *outs):
    _, cores, shards, rows, cols = copies.shape
    share = cols // len(outs)
    for n, out in enumerate(outs):
        for s in range(shards):
            for c in range(cores):
                at = (s * cores + c) * share
                out[:, at : at + share] = copies[0, c, s, :, n * share : (n + 1) * share].astype(F32)


def columns_out(copies, count):
    planes, cores, shards, rows, cols = copies.shape
    wide = shards * cores * cols // count
    return pl.pallas_call(
        columns_kernel,
        grid=(planes,),
        in_specs=[pl.BlockSpec((1,) + copies.shape[1:], lambda i: (i, 0, 0, 0, 0))],
        out_specs=[pl.BlockSpec((rows, wide), lambda i: (i, 0))] * count,
        out_shape=[jax.ShapeDtypeStruct((planes * rows, wide), F32)] * count,
        compiler_params=pltpu.CompilerParams(vmem_limit_bytes=40 * 1024 * 1024),
        name="columns_out",
    )(copies)


def rows_kernel(copies, out):
    out[...] = copies[0, 0].astype(F32)


def rows_out(copies):
    planes, cores, rows, cols = copies.shape
    return pl.pallas_call(
        rows_kernel,
        grid=(planes, cores),
        in_specs=[pl.BlockSpec((1, 1, rows, cols), lambda i, j: (i, j, 0, 0))],
        out_specs=pl.BlockSpec((rows, cols), lambda i, j: (j * planes + i, 0)),
        out_shape=jax.ShapeDtypeStruct((planes * cores * rows, cols), F32),
        name="rows_out",
    )(copies)


def project_kernel(count, *refs):
    tokens, weights, raw, squares = refs[: 2 * count], refs[2 * count : 3 * count], refs[-2], refs[-1]
    chunk = tokens[0].shape[1]
    third = raw.shape[1] // 3
    block = pl.program_id(0) * pl.num_programs(1) + pl.program_id(1)
    for r in range(2):

        @pl.when(pl.program_id(0) == r)
        def _():
            total = mm(tokens[r * count][...], weights[0][:chunk, :])
            for k in range(1, count):
                total += mm(tokens[r * count + k][...], weights[k][:chunk, :])
            raw[...] = total
            for n in range(2):
                squared = total[:, n * third : (n + 1) * third]
                squared = squared * squared
                folded = squared[:, :HEAD]
                for h in range(1, third // HEAD):
                    folded += squared[:, h * HEAD : (h + 1) * HEAD]
                squares[n, pl.ds(block, 1), :] = as_row(folded)


def project(pieces, weights):
    count = len(weights)
    rows, chunk = pieces[0][0].shape
    cols = weights[0].shape[1]
    steps = rows // PIECE

    def spec(r):
        return pl.BlockSpec((PIECE, chunk), lambda a, i: (jnp.where(a == r, i, (steps - 1) * (a > r)), 0))

    return pl.pallas_call(
        functools.partial(project_kernel, count),
        grid=(2, steps),
        in_specs=[spec(r) for r in range(2) for _ in range(count)]
        + [pl.BlockSpec(w.shape, lambda a, i: (0, 0), pipeline_mode=pl.Buffered(1)) for w in weights],
        out_specs=[
            pl.BlockSpec((PIECE, cols), lambda a, i: (a * steps + i, 0)),
            pl.BlockSpec((2, 2 * steps, PIECE), lambda a, i: (0, 0, 0)),
        ],
        out_shape=[
            jax.ShapeDtypeStruct((2 * rows, cols), F32),
            jax.ShapeDtypeStruct((2, 2 * steps, PIECE), F32),
        ],
        compiler_params=pltpu.CompilerParams(vmem_limit_bytes=40 * 1024 * 1024),
        name="project",
    )(*pieces[0], *pieces[1], *weights)


def input_terms_kernel(count, *refs):
    tokens, grads, out = refs[: 2 * count], refs[2 * count], refs[2 * count + 1]
    rows = tokens[0].shape[0]
    planes, _, share, cols = out.shape
    for k in range(count):
        total = contract_rows(tokens[k][...], grads[:rows, :]) + contract_rows(tokens[count + k][...], grads[rows:, :])
        out[:, k] = total.astype(BF).reshape(planes, share, cols)


def input_terms(pieces, grads, planes):
    count = len(pieces[0])
    chunk = pieces[0][0].shape[1]
    return pl.pallas_call(
        functools.partial(input_terms_kernel, count),
        out_shape=jax.ShapeDtypeStruct((planes, count, chunk // planes, grads.shape[1]), BF),
        compiler_params=pltpu.CompilerParams(vmem_limit_bytes=56 * 1024 * 1024),
        name="input_terms",
    )(*pieces[0], *pieces[1], grads)


def memory_block(block, where, blocks, per_device):
    core, here = where
    plane, rest = divmod(block, 2 * per_device)
    which, inside = divmod(rest, per_device)
    return (which ^ core) * (blocks // 2) + (plane ^ here) * per_device + inside


def as_columns(row):
    return jnp.broadcast_to(row, (HEAD, PIECE)).T


def as_row(values):
    return jnp.sum(values.T, axis=0, keepdims=True)


def factor_of(squares):
    return lax.rsqrt(squares * (1.0 / (HEADS * HEAD)) + epsilon)


def forward_kernel(
    per_device, flags, raw_q, raw_k, raw_v, squares, gain_q, gain_k, cosine, sine, key_bias,
    mixed, queries, keys, values, lse,
):
    rows = queries.shape[0]
    blocks = rows // PIECE
    core = (flags[blocks], flags[blocks + 1])
    place_key = lax.broadcasted_iota(jnp.int32, (PIECE, PIECE), 0)
    place_query = lax.broadcasted_iota(jnp.int32, (PIECE, PIECE), 1)
    causal = place_key <= place_query
    for b in range(blocks):
        here = pl.ds(b * PIECE, PIECE)
        from_block = memory_block(b, core, blocks, per_device)
        there = pl.ds(pl.multiple_of(from_block * PIECE, PIECE), PIECE)
        for n, (raw, gain, turned) in enumerate(((raw_q, gain_q, queries), (raw_k, gain_k, keys))):
            factor = as_columns(factor_of(squares[n, pl.ds(from_block, 1), :]))
            normed = raw[there, :] * factor * gain[...]
            turned[here, :] = (
                normed * cosine[here, :] + pltpu.roll(normed, HEAD // 2, 1) * sine[here, :]
            ).astype(BF)
        values[here, :] = raw_v[there, :].astype(BF)
    for b in range(blocks):
        here = pl.ds(b * PIECE, PIECE)
        seen = pl.ds(0, (b + 1) * PIECE)
        whole = flags[b] > 0
        scores = contract_cols(keys[seen, :], queries[here, :]) * score_scale + key_bias[seen, :]
        last = jnp.where(causal | whole, scores[b * PIECE :], masked_score)
        scores = jnp.concatenate([scores[: b * PIECE], last], 0) if b else last
        highest = jnp.max(scores, axis=0, keepdims=True)
        raised = jnp.exp(scores - highest)
        summed = jnp.sum(raised, axis=0, keepdims=True)
        lse[:, here] = highest + jnp.log(summed)
        probs = (raised * (1.0 / summed)).astype(BF)
        mixed[here, :] = contract_rows(probs, values[seen, :]).astype(mixed.dtype)


def attend_forward(raw, squares, gain_q, gain_k, cosine, sine, key_bias, flags, per_device):
    rows = raw.shape[0]
    heads = raw.shape[1] // (3 * HEAD)
    blocks = rows // PIECE
    column = pl.BlockSpec((rows, HEAD), lambda h, f: (0, h))
    table = pl.BlockSpec((rows, HEAD), lambda h, f: (0, 0), pipeline_mode=pl.Buffered(1))
    gain = pl.BlockSpec((1, HEAD), lambda h, f: (0, h))
    turned = jax.ShapeDtypeStruct((rows, heads * HEAD), BF)
    return pl.pallas_call(
        functools.partial(forward_kernel, per_device),
        grid_spec=pltpu.PrefetchScalarGridSpec(
            num_scalar_prefetch=1,
            grid=(heads,),
            in_specs=[
                column,
                pl.BlockSpec((rows, HEAD), lambda h, f: (0, heads + h)),
                pl.BlockSpec((rows, HEAD), lambda h, f: (0, 2 * heads + h)),
                pl.BlockSpec((2, blocks, PIECE), lambda h, f: (0, 0, 0)),
                gain,
                gain,
                table,
                table,
                pl.BlockSpec((rows, 1), lambda h, f: (0, 0), pipeline_mode=pl.Buffered(1)),
            ],
            out_specs=[column] * 4 + [pl.BlockSpec((None, 1, rows), lambda h, f: (h, 0, 0))],
        ),
        out_shape=[turned] * 4 + [jax.ShapeDtypeStruct((heads, 1, rows), F32)],
        compiler_params=pltpu.CompilerParams(vmem_limit_bytes=52 * 1024 * 1024),
        name="attend_forward",
    )(flags, raw, raw, raw, squares, gain_q, gain_k, cosine, sine, key_bias)


def backward_kernel(
    per_device, flags, queries, keys, values, grad_mixed, mixed, raw_q, raw_k, squares, gain_q, gain_k,
    cosine, sine, key_bias, lse,
    scaled_q, scaled_k, grad_values, inner, grad_gains, keys_acc, values_acc,
):
    rows = queries.shape[0]
    blocks = rows // PIECE
    core = (flags[blocks], flags[blocks + 1])
    place_key = lax.broadcasted_iota(jnp.int32, (PIECE, PIECE), 0)
    place_query = lax.broadcasted_iota(jnp.int32, (PIECE, PIECE), 1)
    causal = place_key <= place_query
    keys_acc[...] = jnp.zeros_like(keys_acc)
    values_acc[...] = jnp.zeros_like(values_acc)
    grad_gains[...] = jnp.zeros_like(grad_gains)

    def turn_back(n, b, grad, raw, gain, scaled_out):
        here = pl.ds(b * PIECE, PIECE)
        block = memory_block(b, core, blocks, per_device)
        there = pl.ds(pl.multiple_of(block * PIECE, PIECE), PIECE)
        turned = grad * cosine[here, :] - pltpu.roll(grad, HEAD // 2, 1) * sine[here, :]
        raw_block = raw[there, :]
        scaled = turned * gain[...]
        scaled_out[there, :] = scaled
        inner[n, pl.ds(block, 1), :] = as_row(raw_block * scaled)
        factor = as_columns(factor_of(squares[n, pl.ds(block, 1), :]))
        grad_gains[n : n + 1, :] += jnp.sum(turned * raw_block * factor, axis=0, keepdims=True)

    for b in range(blocks):
        here = pl.ds(b * PIECE, PIECE)
        whole = flags[b] > 0
        query_block = queries[here, :]
        grad_block = grad_mixed[here, :]
        delta = as_row(grad_block.astype(F32) * mixed[here, :].astype(F32))
        grad_query = jnp.zeros((PIECE, HEAD), F32)
        for first in range(0, b + 1, 8):
            last = min(first + 8, b + 1)
            seen = pl.ds(first * PIECE, (last - first) * PIECE)
            scores = contract_cols(keys[seen, :], query_block) * score_scale + key_bias[seen, :]
            if last == b + 1:
                edge = (b - first) * PIECE
                final = jnp.where(causal | whole, scores[edge:], masked_score)
                scores = jnp.concatenate([scores[:edge], final], 0) if edge else final
            probs = jnp.exp(scores - lse[:, here])
            grad_probs = contract_cols(values[seen, :], grad_block)
            grad_scores = (probs * (grad_probs - delta)).astype(BF)
            values_acc[seen, :] += mm(probs.astype(BF), grad_block)
            keys_acc[seen, :] += mm(grad_scores, query_block)
            grad_query += contract_rows(grad_scores, keys[seen, :])
        turn_back(0, b, grad_query * score_scale, raw_q, gain_q, scaled_q)
    for b in range(blocks):
        here = pl.ds(b * PIECE, PIECE)
        turn_back(1, b, keys_acc[here, :] * score_scale, raw_k, gain_k, scaled_k)
        block = memory_block(b, core, blocks, per_device)
        there = pl.ds(pl.multiple_of(block * PIECE, PIECE), PIECE)
        grad_values[there, :] = values_acc[here, :].astype(BF)


def attend_backward(
    queries, keys, values, grad_mixed, mixed, raw, squares, gain_q, gain_k, cosine, sine, key_bias, flags, lse,
    per_device,
):
    rows, width = queries.shape
    heads = width // HEAD
    blocks = rows // PIECE
    column = pl.BlockSpec((rows, HEAD), lambda h, f: (0, h))
    table = pl.BlockSpec((rows, HEAD), lambda h, f: (0, 0), pipeline_mode=pl.Buffered(1))
    gain = pl.BlockSpec((1, HEAD), lambda h, f: (0, h))
    return pl.pallas_call(
        functools.partial(backward_kernel, per_device),
        grid_spec=pltpu.PrefetchScalarGridSpec(
            num_scalar_prefetch=1,
            grid=(heads,),
            in_specs=[column] * 5
            + [
                column,
                pl.BlockSpec((rows, HEAD), lambda h, f: (0, heads + h)),
                pl.BlockSpec((2, blocks, PIECE), lambda h, f: (0, 0, 0)),
                gain,
                gain,
                table,
                table,
                pl.BlockSpec((rows, 1), lambda h, f: (0, 0), pipeline_mode=pl.Buffered(1)),
                pl.BlockSpec((None, 1, rows), lambda h, f: (h, 0, 0)),
            ],
            out_specs=[column] * 3
            + [
                pl.BlockSpec((None, 2, blocks, PIECE), lambda h, f: (h, 0, 0, 0)),
                pl.BlockSpec((None, 2, HEAD), lambda h, f: (h, 0, 0)),
            ],
            scratch_shapes=[pltpu.VMEM((rows, HEAD), F32)] * 2,
        ),
        out_shape=[
            jax.ShapeDtypeStruct((rows, width), F32),
            jax.ShapeDtypeStruct((rows, width), F32),
            jax.ShapeDtypeStruct((rows, width), BF),
            jax.ShapeDtypeStruct((heads, 2, blocks, PIECE), F32),
            jax.ShapeDtypeStruct((heads, 2, HEAD), F32),
        ],
        compiler_params=pltpu.CompilerParams(vmem_limit_bytes=56 * 1024 * 1024),
        name="attend_backward",
    )(
        flags, queries, keys, values, grad_mixed, mixed, raw, raw, squares, gain_q, gain_k, cosine, sine,
        key_bias, lse,
    )


def finish_kernel(scaled_q, scaled_k, grad_values, raw, squares, inner, out):
    block = pl.program_id(0)
    width = scaled_q.shape[1]
    for n, scaled in enumerate((scaled_q, scaled_k)):
        factor_row = factor_of(squares[n, pl.ds(block, 1), :])
        inner_row = inner[n, pl.ds(block, 1), :] * (1.0 / (HEADS * HEAD))
        factor = as_columns(factor_row)
        slope = as_columns(factor_row * factor_row * factor_row * inner_row)
        for h in range(width // HEAD):
            at = n * width + h * HEAD
            out[:, at : at + HEAD] = (
                factor * scaled[:, h * HEAD : (h + 1) * HEAD] - raw[:, at : at + HEAD] * slope
            ).astype(BF)
    out[:, 2 * width :] = grad_values[...]


def finish(scaled_q, scaled_k, grad_values, raw, squares, inner):
    rows, width = scaled_q.shape
    blocks = rows // PIECE
    part = pl.BlockSpec((PIECE, width), lambda i: (i, 0))
    wide = pl.BlockSpec((PIECE, 3 * width), lambda i: (i, 0))
    row = pl.BlockSpec((2, blocks, PIECE), lambda i: (0, 0, 0))
    return pl.pallas_call(
        finish_kernel,
        grid=(blocks,),
        in_specs=[part, part, part, wide, row, row],
        out_specs=wide,
        out_shape=jax.ShapeDtypeStruct((rows, 3 * width), BF),
        name="finish",
    )(scaled_q, scaled_k, grad_values, raw, squares, inner)


def norm_factor(values):
    return lax.rsqrt(jnp.mean(values * values, axis=-1, keepdims=True) + epsilon)


def norm_back(values, factor, gain, cotangent):
    scaled = gain * cotangent
    inner = jnp.mean(values * scaled, axis=-1, keepdims=True)
    grad = factor * scaled - values * (factor * factor * factor) * inner
    return grad, jnp.sum(cotangent * values * factor, axis=0)


def per_device(
    hidden_in,
    piece_index,
    pad_flags,
    cotangent,
    query_weight,
    key_weight,
    value_weight,
    output_weight,
    gate_weight,
    up_weight,
    down_weight,
    query_gain,
    key_gain,
    attention_gain,
    feed_gain,
):
    shards = lax.axis_size("shard")
    planes = lax.axis_size("z")
    shard = lax.axis_index("shard")
    core = lax.axis_index("core")
    plane = lax.axis_index("z")
    tokens = hidden_in[0]
    rows, width = tokens.shape
    chunk = width // shards
    parts = 2 * shards
    head_cols = width // parts
    feed_cols = gate_weight.shape[1] // parts
    seq_len = rows * 2 * planes
    everything = 2 * rows * shards

    tie = lax.optimization_barrier

    def plane_relative(values):
        return jnp.stack(
            [
                lax.dynamic_index_in_dim(values, (shard ^ k) * 2 + (core ^ r), 0, keepdims=False)
                for r in range(2)
                for k in range(shards)
            ]
        )

    def plane_absolute(values):
        return jnp.stack(
            [
                lax.dynamic_index_in_dim(values, (core ^ r) * shards + (shard ^ j), 0, keepdims=False)
                for j in range(shards)
                for r in range(2)
            ]
        )

    def absolute_shards(blocks):
        stacked = jnp.stack(blocks)
        return jnp.stack(
            [lax.dynamic_index_in_dim(stacked, shard ^ j, 0, keepdims=False) for j in range(shards)]
        )

    info_rows = 2 * rows // chunk
    info = jnp.stack([piece_index[0], pad_flags[0]]).astype(BF).reshape(info_rows, chunk)
    info = jnp.pad(info, ((0, 16 - info_rows), (0, 0)))

    def chunk_of(k):
        return jnp.concatenate([lax.dynamic_slice_in_dim(tokens, (shard ^ k) * chunk, chunk, 1), info], 0)

    by_seq = jnp.stack([send_shard(chunk_of(k), k) if k else chunk_of(k) for k in range(shards)])
    by_plane = [
        lax.dynamic_index_in_dim(by_seq, shard ^ plane ^ k, 0, keepdims=False) for k in range(planes)
    ]
    by_plane = jnp.stack([send_plane(by_plane[k], k) if k else by_plane[k] for k in range(planes)])
    mine = by_plane[:, :rows].reshape(planes * rows, chunk)
    info_mine = by_plane[:, rows : rows + info_rows].reshape(planes, 2, rows)
    info_mine = jnp.stack(
        [lax.dynamic_index_in_dim(info_mine, plane ^ j, 0, keepdims=False) for j in range(planes)]
    )
    info_both = jnp.stack([info_mine, send_core(info_mine)], 1)
    info_seq = jnp.where(core == 0, info_both, info_both[:, ::-1]).astype(F32)
    piece_seq = info_seq[:, :, 0].reshape(seq_len)
    pad_seq = info_seq[:, :, 1].reshape(seq_len)
    block_flags = (piece_seq.reshape(-1, PIECE)[:, 0] >= 0.0).astype(jnp.int32)
    block_flags = jnp.concatenate([block_flags, core[None], plane[None]])
    key_bias = jnp.where(pad_seq > 0.0, masked_score, 0.0)[:, None]

    def column_block(weight, k, cols):
        return lax.dynamic_slice_in_dim(weight, ((shard ^ k) * 2 + core) * cols, cols, 1)

    gain_rows = jnp.pad(
        jnp.stack([attention_gain, feed_gain]), ((0, 14), (0, 3 * head_cols - attention_gain.shape[0]))
    )

    def input_block(k):
        block = [column_block(w, k, head_cols) for w in (query_weight, key_weight, value_weight)]
        return jnp.concatenate([jnp.concatenate(block, 1), gain_rows], 0)

    input_blocks = [input_block(0)] + [send_shard(input_block(k), k) for k in range(1, shards)]
    gains = absolute_shards([b[chunk : chunk + 2, : attention_gain.shape[0]] for b in input_blocks])
    gains = gains.transpose(1, 0, 2).reshape(2, width).astype(F32)
    out_block = lax.dynamic_slice_in_dim(output_weight, core * head_cols, head_cols, 0)
    down_block = lax.dynamic_slice_in_dim(down_weight, core * feed_cols, feed_cols, 0)
    query_gain_here = lax.dynamic_slice_in_dim(query_gain, core * head_cols, head_cols, 0).astype(F32)[None]
    key_gain_here = lax.dynamic_slice_in_dim(key_gain, core * head_cols, head_cols, 0).astype(F32)[None]
    rates = theta_base ** (-jnp.arange(HEAD // 2).astype(F32) * (2.0 / HEAD))
    angles = jnp.arange(seq_len, dtype=jnp.int32).astype(F32)[:, None] * rates[None, :]
    cosine, sine = jnp.cos(angles), jnp.sin(angles)
    cosine = jnp.concatenate([cosine, cosine], 1)
    sine = jnp.concatenate([-sine, sine], 1)

    gathered = gather_shard(mine)
    gate_weight, up_weight, gathered = tie((gate_weight, up_weight, gathered))
    gathered = [gathered, [send_core(block) for block in gathered]]

    def feed_block(k):
        return jnp.concatenate([column_block(w, k, feed_cols) for w in (gate_weight, up_weight)], 1)

    feed_blocks = [feed_block(0)] + [send_shard(feed_block(k), k) for k in range(1, shards - 1)]
    inputs_here = gathered
    raw, squares = project(inputs_here, input_blocks)
    squares = sum_plane(squares.reshape(2, 2, seq_len // 2), True)
    squares, feed_blocks, gate_weight, up_weight = tie((squares, feed_blocks, gate_weight, up_weight))
    feed_blocks.append(send_shard(feed_block(shards - 1), shards - 1))
    squares = squares.reshape(2, seq_len // PIECE, PIECE)
    per_block = rows // PIECE
    attended_seq, query_low, key_low, value_low, lse = attend_forward(
        raw, squares, query_gain_here, key_gain_here, cosine, sine, key_bias, block_flags, per_block
    )

    attended = lax.all_to_all(
        attended_seq.reshape(planes, 2 * rows, head_cols), "z", 0, 0, tiled=True
    ).reshape(parts, rows, head_cols)
    attended, feed_blocks = tie((attended, feed_blocks))
    attended = plane_relative(attended).reshape(everything, head_cols)
    half = everything // 2
    whole_feed = jnp.zeros((width, 2 * feed_cols), BF)
    for k in range(shards):
        whole_feed = lax.dynamic_update_slice_in_dim(whole_feed, feed_blocks[k], (shard ^ k) * chunk, 0)

    def blocks_of(values):
        return values.reshape(shards, rows, values.shape[-1])

    branch_attn = reduce_plane(
        blocks_of(mm(attended[half:], out_block)), blocks_of(mm(attended[:half], out_block))
    )
    attn_factor = norm_factor(branch_attn)
    residual = tokens.astype(F32) + branch_attn * attn_factor * gains[0]
    gathered = gather_plane(residual.astype(BF))
    residual_all = jnp.concatenate(gathered[0] + gathered[1], 0)
    gate = mm(residual_all, whole_feed[:, :feed_cols])
    up = mm(residual_all, whole_feed[:, feed_cols:])
    activated = (jax.nn.silu(gate) * up).astype(BF)
    branch_feed = reduce_plane(
        blocks_of(mm(activated[half:], down_block)), blocks_of(mm(activated[:half], down_block))
    )
    feed_factor = norm_factor(branch_feed)
    result = residual + branch_feed * feed_factor * gains[1]

    grad_out = cotangent[0].astype(F32)
    grad_feed, grad_feed_gain = norm_back(branch_feed, feed_factor, gains[1], grad_out)
    gathered = gather_plane(grad_feed.astype(BF))
    grad_feed_all = jnp.concatenate(gathered[0] + gathered[1], 0)
    grad_down = contract_rows(activated, grad_feed_all).astype(BF)
    grad_down, grad_feed_all = tie((grad_down, grad_feed_all))

    def plane_share(terms):
        flat = terms.reshape(-1, terms.shape[-1])
        share = lax.psum_scatter(flat, "z", scatter_dimension=0, tiled=True)
        return share.reshape((1,) + terms.shape[1:])[0]

    def to_owner(share, relative):
        blocks = []
        for k in range(shards):
            block = share[k] if relative else lax.dynamic_index_in_dim(share, shard ^ k, 0, keepdims=False)
            blocks.append(send_shard(block, k) if k else block)
        return absolute_shards(blocks)

    def copies(values):
        whole = lax.all_gather(values, ("z", "core"), axis=0)
        return whole.reshape((planes, 2) + values.shape)

    down_share = plane_share(grad_down.reshape(planes, feed_cols // planes, width))
    grad_act = contract_cols(grad_feed_all, down_block)
    sigmoid = jax.nn.sigmoid(gate)
    grad_gate = (grad_act * up * sigmoid * (1.0 + gate * (1.0 - sigmoid))).astype(BF)
    grad_up = (grad_act * gate * sigmoid).astype(BF)

    def feed_back(part):
        return contract_cols(grad_gate[part], whole_feed[:, :feed_cols]) + contract_cols(
            grad_up[part], whole_feed[:, feed_cols:]
        )

    got_core = send_core(feed_back(slice(half, None)).astype(BF))
    gate_terms = weight_terms(residual_all, grad_gate, shards, planes)
    gate_terms, grad_gate, grad_up, got_core = tie((gate_terms, grad_gate, grad_up, got_core))
    gate_share = plane_share(gate_terms)
    to_mine = feed_back(slice(None, half)).astype(BF)
    to_mine, got_core, grad_up = tie((to_mine, got_core, grad_up))
    up_terms = weight_terms(residual_all, grad_up, shards, planes)
    up_share = plane_share(up_terms)

    def feed_term(k, part):
        return blocks_of(to_mine)[k, part].astype(F32) + blocks_of(got_core)[k, part].astype(F32)

    feed_term.rows = rows
    grad_feed_in = reduce_shard(feed_term)
    grad_feed_in, down_share, up_terms = tie((grad_feed_in, down_share, up_terms))

    grad_resid = grad_out + grad_feed_in
    grad_branch, grad_attention_gain = norm_back(branch_attn, attn_factor, gains[0], grad_resid)
    gathered = gather_plane(grad_branch.astype(BF))
    grad_branch_all = jnp.concatenate(gathered[0] + gathered[1], 0)
    grad_mixed = contract_cols(grad_branch_all, out_block).astype(BF)
    grad_mixed = plane_absolute(grad_mixed.reshape(parts, rows, head_cols))
    grad_mixed = lax.all_to_all(
        grad_mixed.reshape(shards, 2 * rows, head_cols), "z", 0, 0, tiled=True
    ).reshape(seq_len, head_cols)
    grad_output = contract_rows(attended, grad_branch_all).astype(BF)
    grad_output, grad_mixed, gate_share = tie((grad_output, grad_mixed, gate_share))
    output_share = plane_share(grad_output.reshape(planes, head_cols // planes, width))
    scaled_q, scaled_k, grad_values, inner, grad_gains = attend_backward(
        query_low, key_low, value_low, grad_mixed, attended_seq, raw, squares, query_gain_here, key_gain_here,
        cosine, sine, key_bias, block_flags, lse, per_block,
    )
    inner, up_share = tie((inner, up_share))
    inner = sum_plane(jnp.sum(inner, 0).reshape(2, 2, seq_len // 2), True).reshape(squares.shape)
    grad_raw = finish(scaled_q, scaled_k, grad_values, raw, squares, inner)
    input_part = input_terms(inputs_here, grad_raw, planes)
    grad_raw, input_part = tie((grad_raw, input_part))
    input_share = plane_share(input_part)
    seq_half = seq_len // 2

    def chunks_of(values):
        return jnp.stack([contract_cols(values, block[:chunk]) for block in input_blocks])

    grad_chunk = reduce_plane(chunks_of(grad_raw[seq_half:]), chunks_of(grad_raw[:seq_half]))
    grad_chunk = grad_chunk.astype(BF).reshape(planes, rows, chunk)
    grad_chunk = jnp.stack([send_plane(grad_chunk[k], k) if k else grad_chunk[k] for k in range(planes)])
    by_shard = [
        lax.dynamic_index_in_dim(grad_chunk, shard ^ plane ^ k, 0, keepdims=False) for k in range(shards)
    ]
    by_shard = [send_shard(by_shard[k], k) if k else by_shard[k] for k in range(shards)]
    grad_chunk = absolute_shards(by_shard)
    grad_tokens = grad_resid + grad_chunk.transpose(1, 0, 2).reshape(rows, width).astype(F32)

    grad_down_weight = rows_out(copies(down_share))
    (grad_gate_weight,) = columns_out(copies(to_owner(gate_share, False)), 1)
    (grad_up_weight,) = columns_out(copies(to_owner(up_share, False)), 1)
    grad_output_weight = rows_out(copies(output_share))
    grad_query_weight, grad_key_weight, grad_value_weight = columns_out(copies(to_owner(input_share, True)), 3)

    valid = (pad_flags[0] == 0).astype(F32)[:, None]
    stat_terms = jnp.stack(
        [
            jnp.sum(valid * result * result),
            jnp.sum(valid * branch_attn * branch_attn),
            jnp.sum(valid * branch_feed * branch_feed),
            jnp.sum(valid),
        ]
    )
    terms = jnp.concatenate([grad_attention_gain, grad_feed_gain, jnp.pad(stat_terms, (0, 124))])
    terms = sum_over_planes(sum_plane(terms.reshape(-1, 128))).reshape(-1)
    gain_width = query_gain.shape[0]
    gain_full = terms[: 2 * width].reshape(2, width)
    gain_full = lax.dynamic_slice_in_dim(gain_full, shard * gain_width, gain_width, 1)
    stat_terms = terms[2 * width :]
    stats = jnp.sqrt(stat_terms[:3] / (stat_terms[3] * width))
    gain_heads = sum_over_planes(grad_gains.transpose(1, 0, 2).reshape(2, head_cols))
    gain_other = send_core(gain_heads)
    gain_heads = jnp.where(
        core == 0,
        jnp.concatenate([gain_heads, gain_other], 1),
        jnp.concatenate([gain_other, gain_heads], 1),
    )
    return (
        result[None],
        grad_tokens[None],
        grad_query_weight,
        grad_key_weight,
        grad_value_weight,
        grad_output_weight,
        grad_gate_weight,
        grad_up_weight,
        grad_down_weight,
        gain_heads[0],
        gain_heads[1],
        gain_full[0],
        gain_full[1],
        stats,
    )


def solution(mesh):
    devices = mesh.devices.reshape(mesh.shape["replica"] // 2, 2, mesh.shape["shard"])
    split = Mesh(devices, ("z", "core", "shard"))
    tokens = ("z", "core")
    placed = (
        (P("shard", tokens, None), P("shard", tokens), P("shard", tokens), P("shard", tokens, None))
        + (P("shard", None),) * 7
        + (P("shard"),) * 4
    )
    return jax.shard_map(
        per_device,
        mesh=split,
        in_specs=placed,
        out_specs=(P("shard", tokens, None),) * 2
        + (P("shard", None),) * 7
        + (P("shard"),) * 4
        + (P(),),
        check_vma=False,
    )
```

time: 1630 us -> 1230 us (0.75)
  blocking collectives: 290 us -> 0 us
  local copies, waits for them, and re-layouts: 256 us -> 80.9 us
  Pallas kernels: 28.9 us -> 131 us
  other arithmetic: 155 us -> 75 us
  waiting for transfers between devices: 613 us -> 674 us
  matrix products: 193 us -> 145 us
  starting transfers between devices: 72.5 us -> 92.4 us
    all_gather x2 -> x0, blocking collectives: 184 us -> none  [the longest x1 108 us: per_device(): lax.all_gather(jnp.stack([attention_gain, feed_gain]), 'shard', axis=1, t...]
    convert_element_type x12 -> x0, local copies, waits for them, and re-layouts: 147 us -> none  [the longest x10 132 us: wide(): return values.transpose(0, 3, 2, 1, 4).reshape(weight.shape).astype(F32)]
    reduce_scatter x4 -> x5, waiting for transfers between devices: 159 us -> 22.5 us  [plane_share(): share = lax.psum_scatter(flat, 'z', scatter_dimension=0, tiled=True)]
    pallas_call x2 -> x12, Pallas kernels: 28.9 us -> 131 us  [the longest x2 22.5 us: weight_terms(): pl.pallas_call(terms_kernel, grid=(shards,), in_specs=[pl.BlockSpec((rows...]
    all_gather x4 -> x5, waiting for transfers between devices: 104 us -> 177 us  [copies(): whole = lax.all_gather(values, ('z', 'core'), axis=0)]
    ppermute x0 -> x10, waiting for transfers between devices: none -> 64.3 us  [the longest x4 41.3 us: sum_over_planes(): lax.ppermute(values, 'z', [(i, i ^ step) for i in range(count)])]
    psum x1 -> x0, blocking collectives: 58.6 us -> none  [per_device(): terms = lax.psum(terms, ('z', 'core', 'shard'))]
    all_to_all x2 -> x0, blocking collectives: 47.9 us -> none  [the longest x1 28.8 us: per_device(): lax.all_to_all(by_seq, 'z', 0, 0, tiled=True).reshape(planes * rows, chunk)]
  transfers between devices with their start and end apart: 82 -> 106, of which waited for: 49 -> 64; matrix products, arithmetic and copies ran while one was open for 19% -> 17% of each run, Pallas kernels for 1% -> 10%
where the time goes in v2:
time: 1230 us; the launch traced here: 1220 us
  waiting for transfers between devices  674 us (55%)
  matrix products  145 us (12%)
  Pallas kernels  131 us (11%)
  starting transfers between devices  92.4 us (8%)
  local copies, waits for them, and re-layouts  80.9 us (7%)
  other arithmetic  75 us (6%)
  between operations  17 us (1%)
    ppermute x59, waiting for transfers between devices, send_shard(): return lax.ppermute(values, 'shard', [(i, i ^ k) for i in range(count)])  321 us
    all_gather x5, waiting for transfers between devices, copies(): whole = lax.all_gather(values, ('z', 'core'), axis=0)  177 us
    dot_general x14, matrix products, contract_cols(): lax.dot_general(left, right, (((1,), (1,)), ((), ())), preferred_element_...  83.9 us
    ppermute x59, starting transfers between devices, send_shard(): return lax.ppermute(values, 'shard', [(i, i ^ k) for i in range(count)])  65.5 us
    all_to_all x1, waiting for transfers between devices, per_device(): lax.all_to_all(grad_mixed.reshape(shards, 2 * rows, head_cols), 'z', 0, 0...  49.7 us
    dot_general x6, matrix products, mm(): return jnp.dot(left, right, preferred_element_type=F32)  43.6 us
    unnamed x170, local copies, waits for them, and re-layouts  41.9 us
    ppermute x4, waiting for transfers between devices, sum_over_planes(): lax.ppermute(values, 'z', [(i, i ^ step) for i in range(count)])  41.3 us
  transfers between devices with their start and end apart: 106, of which 64 were waited for; matrix products, arithmetic and copies ran while one was open for 17% of the time, Pallas kernels for 10%

profile of v2, /device:TPU:0, one launch (start us, length us, event | category | flops | bytes accessed | tf_op | source)
XLA Modules:
  0.0 1216.6 jit_solution(9998209397105120679)
XLA Ops:
  14.8 6.9 collective-permute-done.2
  32.9 7.1 collective-permute-done.5
  39.9 16.0 %collective-permute-done.4 = bf16[272,512]{1,0:T(8,128)(2,1)S(1)} collective-permute-done((bf16[272,512]{1,0:T(8,128)(2,1)S(1)}, bf16[272,512]{1,0:T(8,128)(2,1)S(1)}, u32[]{:S(2)}, u32[]{:S(2)}) %collective-permute-start.4) | collective-permute-done | bytes 278560 | tf_op jit(solution)/shard_map/ppermute | solution.py:46
  59.7 20.7 %collective-permute-done.8.refs_2_ = bf16[1024,512]{1,0:T(8,128)(2,1)} collective-permute-done((bf16[1024,512]{1,0:T(8,128)(2,1)S(1)}, bf16[1024,512]{1,0:T(8,128)(2,1)}, u32[]{:S(2)}, u32[]{:S(2)}) %collective-permute-start.8) | collective-permute-done | bytes 1048608 | tf_op jit(solution)/shard_map/ppermute | solution.py:41
  97.5 20.7 %collective-permute-done.9 = bf16[512,512]{1,0:T(8,128)(2,1)} collective-permute-done((bf16[512,512]{1,0:T(8,128)(2,1)}, bf16[512,512]{1,0:T(8,128)(2,1)}, u32[]{:S(2)}, u32[]{:S(2)}) %collective-permute-start.9) | collective-permute-done | bytes 524320 | tf_op jit(solution)/shard_map/ppermute | solution.py:41
  142.2 12.9 %project.1 = (f32[2048,768]{1,0:T(8,128)}, f32[2,8,256]{2,1,0:T(8,128)S(1)}) custom-call(bf16[1024,512]{1,0:T(8,128)(2,1)S(1)} %bitcast.272, bf16[1024,512]{1,0:T(8,128)(2,1)} %collective-permute-done.7.refs_1_, bf16[1024,512]{1,0:T(8,128)(2,1)} %collective-permute-done.8.refs_2_, bf16[1024,512]{1,0:T(8,128)(2,1)S(1)} %copy-done.4, ...), custom_call_target="tpu_custom_call" | custom-call | tf_op jit(solution)/shard_map/project/pallas_call | solution.py:207
  156.8 18.6 %collective-permute-done.19 = f32[2,2,1024]{2,1,0:T(2,128)S(1)} collective-permute-done((f32[2,2,1024]{2,1,0:T(2,128)S(1)}, f32[2,2,1024]{2,1,0:T(2,128)S(1)}, u32[]{:S(2)}, u32[]{:S(2)}) %collective-permute-start.19) | collective-permute-done | bytes 16416 | tf_op jit(solution)/shard_map/ppermute | solution.py:41
  187.2 19.5 %attend_forward.1 = (bf16[2048,256]{1,0:T(8,128)(2,1)}, bf16[2048,256]{1,0:T(8,128)(2,1)}, bf16[2048,256]{1,0:T(8,128)(2,1)}, bf16[2048,256]{1,0:T(8,128)(2,1)}, f32[2,1,2048]{2,1,0:T(1,128)S(1)}) custom-call(s32[10]{0:T(128)S(1)} %pad_add_fusion.flags, f32[2048,768]{1,0:T(8,128)} %get-tuple-element.74.raw_q.raw_k.raw_v.raw, ...), custom_call_target="tpu_custom_call" | custom-call | tf_op jit(solution)/shard_map/attend_forward/pallas_call | solution.py:308
  211.5 24.8 %all-to-all-done = bf16[4,512,256]{2,1,0:T(8,128)(2,1)S(1)} async-done(((bf16[4,512,256]{2,1,0:T(8,128)(2,1)}), bf16[4,512,256]{2,1,0:T(8,128)(2,1)S(1)}, u32[]{:S(2)}, u32[]{:S(2)}) %all-to-all-start) | async-done | bytes 1048608 | tf_op jit(solution)/shard_map/all_to_all | solution.py:606
  250.4 12.2 %collective-permute-done.25 = bf16[128,2048]{1,0:T(8,128)(2,1)} collective-permute-done((bf16[128,2048]{1,0:T(8,128)(2,1)}, bf16[128,2048]{1,0:T(8,128)(2,1)}, u32[]{:S(2)}, u32[]{:S(2)}) %collective-permute-start.25) | collective-permute-done | bytes 524320 | tf_op jit(solution)/shard_map/ppermute | solution.py:41
  270.5 19.7 %collective-permute-done.28 = bf16[256,2048]{1,0:T(8,128)(2,1)S(1)} collective-permute-done((bf16[256,2048]{1,0:T(8,128)(2,1)S(1)}, bf16[256,2048]{1,0:T(8,128)(2,1)S(1)}, u32[]{:S(2)}, u32[]{:S(2)}) %collective-permute-start.28) | collective-permute-done | bytes 1048608 | tf_op jit(solution)/shard_map/ppermute | solution.py:41
  304.1 15.2 %collective-permute-done.29 = bf16[256,2048]{1,0:T(8,128)(2,1)} collective-permute-done((bf16[256,2048]{1,0:T(8,128)(2,1)}, bf16[256,2048]{1,0:T(8,128)(2,1)}, u32[]{:S(2)}, u32[]{:S(2)}) %collective-permute-start.29) | collective-permute-done | bytes 1048608 | tf_op jit(solution)/shard_map/ppermute | solution.py:41
  336.2 11.7 fusion.8
  347.9 14.6 %multiply_convert_fusion.2 = (bf16[2048,1024]{1,0:T(8,128)(2,1)}, f32[2048,1024]{1,0:T(8,128)}) fusion(f32[2048,1024]{1,0:T(8,128)} %fusion.8, bf16[2048,2048]{1,0:T(8,128)(2,1)S(1)} %constant_dynamic-update-slice_fusion.tokens, bf16[2048,2048]{1,0:T(8,128)(2,1)S(1)} %constant_dynamic-update-slice_fusion.35), kind=kOutput, calls=%fused_computation.4 | convolution fusion | flops 8602517504 | bytes 33554432 | tf_op jit(solution)/shard_map/dot_general | solution.py:24
  362.5 7.5 convolution_convert_fusion.3
  370.2 7.3 convolution_convert_fusion.4
  380.4 12.2 %collective-permute-done.38 = bf16[128,2048]{1,0:T(8,128)(2,1)S(1)} collective-permute-done((bf16[128,2048]{1,0:T(8,128)(2,1)S(1)}, bf16[128,2048]{1,0:T(8,128)(2,1)S(1)}, u32[]{:S(2)}, u32[]{:S(2)}) %collective-permute-start.38) | collective-permute-done | bytes 524320 | tf_op jit(solution)/shard_map/ppermute | solution.py:41
  396.0 22.1 %collective-permute-done.41 = bf16[256,2048]{1,0:T(8,128)(2,1)S(1)} collective-permute-done((bf16[256,2048]{1,0:T(8,128)(2,1)S(1)}, bf16[256,2048]{1,0:T(8,128)(2,1)S(1)}, u32[]{:S(2)}, u32[]{:S(2)}) %collective-permute-start.41) | collective-permute-done | bytes 1048608 | tf_op jit(solution)/shard_map/ppermute | solution.py:41
  426.2 21.1 %collective-permute-done.42 = bf16[256,2048]{1,0:T(8,128)(2,1)S(1)} collective-permute-done((bf16[256,2048]{1,0:T(8,128)(2,1)S(1)}, bf16[256,2048]{1,0:T(8,128)(2,1)S(1)}, u32[]{:S(2)}, u32[]{:S(2)}) %collective-permute-start.42) | collective-permute-done | bytes 1048608 | tf_op jit(solution)/shard_map/ppermute | solution.py:41
  450.9 8.1 collective-permute-done.44
  465.2 10.9 convolution_convert_fusion
  476.2 22.1 %multiply_convert_fusion = (bf16[2048,1024]{1,0:T(8,128)(2,1)S(1)}, bf16[2048,1024]{1,0:T(8,128)(2,1)}) fusion(f32[2048,1024]{1,0:T(8,128)} %fusion.8, f32[2048,1024]{1,0:T(8,128)} %get-tuple-element.280, bf16[2048,2048]{1,0:T(8,128)(2,1)} %copy-done.55, bf16[2048,2048]{1,0:T(8,128)(2,1)} %param.25, s32[]{:T(128)S(6)} %select_n.247), kind=kOutput, calls=%fused_computation.2 | convolution fusion | flops 8617197568 | bytes 37748740 | tf_op jit(solution)/shard_map/dot_general | solution.py:32
  498.3 12.3 %fusion.6 = f32[1024,2048]{1,0:T(8,128)} fusion(bf16[2048,2048]{1,0:T(8,128)(2,1)} %copy-done.30, bf16[2048,1024]{1,0:T(8,128)(2,1)} %get-tuple-element.95.grads), kind=kOutput, calls=%fused_computation.19 | convolution fusion | flops 4294967296 | bytes 14680064 | tf_op jit(solution)/shard_map/dot_general | solution.py:32
  510.6 8.4 add_convert_fusion.1
  519.2 11.3 weight_terms.2
  532.6 11.0 fusion
  543.6 8.7 add_convert_fusion
  558.2 12.3 %collective-permute-done.51 = bf16[128,2048]{1,0:T(8,128)(2,1)S(1)} collective-permute-done((bf16[128,2048]{1,0:T(8,128)(2,1)S(1)}, bf16[128,2048]{1,0:T(8,128)(2,1)S(1)}, u32[]{:S(2)}, u32[]{:S(2)}) %collective-permute-start.51) | collective-permute-done | bytes 524320 | tf_op jit(solution)/shard_map/ppermute | solution.py:41
  577.3 11.3 weight_terms.3
  590.7 8.4 collective-permute-done.54
  612.7 21.2 %collective-permute-done.55 = bf16[256,2048]{1,0:T(8,128)(2,1)S(1)} collective-permute-done((bf16[256,2048]{1,0:T(8,128)(2,1)S(1)}, bf16[256,2048]{1,0:T(8,128)(2,1)S(1)}, u32[]{:S(2)}, u32[]{:S(2)}) %collective-permute-start.55) | collective-permute-done | bytes 1048608 | tf_op jit(solution)/shard_map/ppermute | solution.py:41
  669.9 7.0 convolution_convert_fusion.6
  676.9 49.7 %all-to-all-done.1 = bf16[4,512,256]{2,1,0:T(8,128)(2,1)} async-done(((bf16[4,512,256]{2,1,0:T(8,128)(2,1)}), bf16[4,512,256]{2,1,0:T(8,128)(2,1)}, u32[]{:S(2)}, u32[]{:S(2)}) %all-to-all-start.1) | async-done | bytes 1048608 | tf_op jit(solution)/shard_map/all_to_all | solution.py:691
  726.7 20.2 %attend_backward.1 = (f32[2048,256]{1,0:T(8,128)}, f32[2048,256]{1,0:T(8,128)}, bf16[2048,256]{1,0:T(8,128)(2,1)}, f32[2,2,8,256]{3,2,1,0:T(8,128)}, f32[2,2,128]{2,1,0:T(2,128)}) custom-call(s32[10]{0:T(128)} %copy-done.17, bf16[2048,256]{1,0:T(8,128)(2,1)} %get-tuple-element.103.queries, bf16[2048,256]{1,0:T(8,128)(2,1)} %get-tuple-element.104.keys, ...), custom_call_target="tpu_custom_call" | custom-call | tf_op jit(solution)/shard_map/attend_backward/pallas_call | solution.py:399
  757.5 8.8 finish.1.refs_8_
  766.3 12.8 %input_terms.1 = bf16[4,4,128,768]{3,2,1,0:T(8,128)(2,1)} custom-call(bf16[1024,512]{1,0:T(8,128)(2,1)} %bitcast.273, bf16[1024,512]{1,0:T(8,128)(2,1)} %collective-permute-done.7.refs_1_, bf16[1024,512]{1,0:T(8,128)(2,1)} %collective-permute-done.8.refs_2_, bf16[1024,512]{1,0:T(8,128)(2,1)} %pad_maximum_fusion.10.refs_3_, ...), custom_call_target="tpu_custom_call" | custom-call | tf_op jit(solution)/shard_map/input_terms/pallas_call | solution.py:237
  785.3 6.7 collective-permute-done.82
  801.5 6.6 collective-permute-done.85
  814.3 22.5 %reduce-scatter.12.cloned.1.call-done = bf16[512,768]{1,0:T(8,128)(2,1)} async-done(((bf16[2048,768]{1,0:T(8,128)(2,1)}), bf16[512,768]{1,0:T(8,128)(2,1)}) %reduce-scatter.12.cloned.1.call-update) | async-done | bytes 786448 | tf_op jit(solution)/shard_map/reduce_scatter | solution.py:644
  871.2 12.1 collective-permute-done.67
  894.2 18.3 %collective-permute-done.90 = f32[33,128]{1,0:T(8,128)S(1)} collective-permute-done((f32[33,128]{1,0:T(8,128)S(1)}, f32[33,128]{1,0:T(8,128)S(1)}, u32[]{:S(2)}, u32[]{:S(2)}) %collective-permute-start.90) | collective-permute-done | bytes 16928 | tf_op jit(solution)/shard_map/ppermute | solution.py:41
  940.8 31.8 %collective-permute-done.87 = f32[2,256]{1,0:T(2,128)S(1)} collective-permute-done((f32[2,256]{1,0:T(2,128)S(1)}, f32[2,256]{1,0:T(2,128)S(1)}, u32[]{:S(2)}, u32[]{:S(2)}) %collective-permute-start.87) | collective-permute-done | bytes 2080 | tf_op jit(solution)/shard_map/ppermute | solution.py:97
  994.0 10.4 rows_out.3
  1004.4 50.3 %all-gather.15.cloned.1.call-done = bf16[32,128,1024]{2,1,0:T(8,128)(2,1)} async-done(((bf16[4,128,1024]{2,1,0:T(8,128)(2,1)}), bf16[32,128,1024]{2,1,0:T(8,128)(2,1)}) %all-gather.15.cloned.1.call-update) | async-done | bytes 8388624 | tf_op jit(solution)/shard_map/all_gather | solution.py:655
  1058.1 6.8 columns_out.4
  1065.0 72.0 %all-gather.17.cloned.1.call-done = bf16[32,128,1024]{2,1,0:T(8,128)(2,1)} async-done(((bf16[4,128,1024]{2,1,0:T(8,128)(2,1)}), bf16[32,128,1024]{2,1,0:T(8,128)(2,1)}) %all-gather.17.cloned.1.call-update) | async-done | bytes 8388624 | tf_op jit(solution)/shard_map/all_gather | solution.py:655
  1140.4 6.5 columns_out.5
  1146.9 54.9 %all-gather.11.cloned.1.call-done = bf16[32,128,768]{2,1,0:T(8,128)(2,1)} async-done(((bf16[4,128,768]{2,1,0:T(8,128)(2,1)}), bf16[32,128,768]{2,1,0:T(8,128)(2,1)}) %all-gather.11.cloned.1.call-update) | async-done | bytes 6291472 | tf_op jit(solution)/shard_map/all_gather | solution.py:655
  (531 shorter events, 365.3 us)
Async XLA Ops:
  32.1 23.8 %collective-permute-start.4 = (bf16[272,512]{1,0:T(8,128)(2,1)S(1)}, bf16[272,512]{1,0:T(8,128)(2,1)S(1)}, u32[]{:S(2)}, u32[]{:S(2)}) collective-permute-start(bf16[272,512]{1,0:T(8,128)(2,1)S(1)} %get-tuple-element.206), channel_id=1, source_target_pairs={{0,16},{8,24},{16,0},{24,8},{1,17},{9,25},{17,1},{25,9},{2,18},{10... | collective-permute-start | bytes 835592 | tf_op jit(solution)/shard_map/ppermute | solution.py:46
  32.1 23.8 %collective-permute-start.3 = (bf16[272,512]{1,0:T(8,128)(2,1)S(1)}, bf16[272,512]{1,0:T(8,128)(2,1)S(1)}, u32[]{:S(2)}, u32[]{:S(2)}) collective-permute-start(bf16[272,512]{1,0:T(8,128)(2,1)S(1)} %get-tuple-element.207), channel_id=1, source_target_pairs={{0,8},{8,0},{16,24},{24,16},{1,9},{9,1},{17,25},{25,17},{2,10},{10... | collective-permute-start | bytes 835592 | tf_op jit(solution)/shard_map/ppermute | solution.py:46
  56.0 24.4 %collective-permute-start.8 = (bf16[1024,512]{1,0:T(8,128)(2,1)S(1)}, bf16[1024,512]{1,0:T(8,128)(2,1)}, u32[]{:S(2)}, u32[]{:S(2)}) collective-permute-start(bf16[1024,512]{1,0:T(8,128)(2,1)S(1)} %bitcast.269), channel_id=1, source_target_pairs={{0,2},{1,3},{2,0},{3,1},{4,6},{5,7},{6,4},{7,5},{8,10},{9,11},{10,... | collective-permute-start | bytes 3145736 | tf_op jit(solution)/shard_map/ppermute | solution.py:41
  57.6 26.2 %collective-permute-start.7 = (bf16[1024,512]{1,0:T(8,128)(2,1)S(1)}, bf16[1024,512]{1,0:T(8,128)(2,1)}, u32[]{:S(2)}, u32[]{:S(2)}) collective-permute-start(bf16[1024,512]{1,0:T(8,128)(2,1)S(1)} %bitcast.270), channel_id=1, source_target_pairs={{0,1},{1,0},{2,3},{3,2},{4,5},{5,4},{6,7},{7,6},{8,9},{9,8},{10,11... | collective-permute-start | bytes 3145736 | tf_op jit(solution)/shard_map/ppermute | solution.py:41
  82.3 15.2 %collective-permute-start.10 = (bf16[512,512]{1,0:T(8,128)(2,1)}, bf16[512,512]{1,0:T(8,128)(2,1)}, u32[]{:S(2)}, u32[]{:S(2)}) collective-permute-start(bf16[512,512]{1,0:T(8,128)(2,1)} %slice.452), channel_id=1, source_target_pairs={{0,1},{1,0},{2,3},{3,2},{4,5},{5,4},{6,7},{7,6},{8,9},{9,8},{10,11... | collective-permute-start | bytes 1572872 | tf_op jit(solution)/shard_map/ppermute | solution.py:41
  85.7 32.6 %collective-permute-start.9 = (bf16[512,512]{1,0:T(8,128)(2,1)}, bf16[512,512]{1,0:T(8,128)(2,1)}, u32[]{:S(2)}, u32[]{:S(2)}) collective-permute-start(bf16[512,512]{1,0:T(8,128)(2,1)} %slice.451), channel_id=1, source_target_pairs={{0,2},{1,3},{2,0},{3,1},{4,6},{5,7},{6,4},{7,5},{8,10},{9,11},{10,... | collective-permute-start | bytes 1572872 | tf_op jit(solution)/shard_map/ppermute | solution.py:41
  88.5 40.4 %collective-permute-start.17 = (bf16[528,768]{1,0:T(8,128)(2,1)}, bf16[528,768]{1,0:T(8,128)(2,1)}, u32[]{:S(2)}, u32[]{:S(2)}) collective-permute-start(bf16[528,768]{1,0:T(8,128)(2,1)} %get-tuple-element.270), channel_id=1, source_target_pairs={{0,3},{1,2},{2,1},{3,0},{4,7},{5,6},{6,5},{7,4},{8,11},{9,10},{10,... | collective-permute-start | bytes 2433032 | tf_op jit(solution)/shard_map/ppermute | solution.py:41
  90.2 42.7 %collective-permute-start.16 = (bf16[528,768]{1,0:T(8,128)(2,1)}, bf16[528,768]{1,0:T(8,128)(2,1)}, u32[]{:S(2)}, u32[]{:S(2)}) collective-permute-start(bf16[528,768]{1,0:T(8,128)(2,1)} %get-tuple-element.269), channel_id=1, source_target_pairs={{0,2},{1,3},{2,0},{3,1},{4,6},{5,7},{6,4},{7,5},{8,10},{9,11},{10,... | collective-permute-start | bytes 2433032 | tf_op jit(solution)/shard_map/ppermute | solution.py:41
  91.8 41.2 %collective-permute-start.15 = (bf16[528,768]{1,0:T(8,128)(2,1)}, bf16[528,768]{1,0:T(8,128)(2,1)}, u32[]{:S(2)}, u32[]{:S(2)}) collective-permute-start(bf16[528,768]{1,0:T(8,128)(2,1)} %get-tuple-element.268), channel_id=1, source_target_pairs={{0,1},{1,0},{2,3},{3,2},{4,5},{5,4},{6,7},{7,6},{8,9},{9,8},{10,11... | collective-permute-start | bytes 2433032 | tf_op jit(solution)/shard_map/ppermute | solution.py:41
  126.8 52.6 %collective-permute-start.21 = (bf16[512,2048]{1,0:T(8,128)(2,1)}, bf16[512,2048]{1,0:T(8,128)(2,1)}, u32[]{:S(2)}, u32[]{:S(2)}) collective-permute-start(bf16[512,2048]{1,0:T(8,128)(2,1)} %pad_maximum_fusion.3), channel_id=1, source_target_pairs={{0,1},{1,0},{2,3},{3,2},{4,5},{5,4},{6,7},{7,6},{8,9},{9,8},{10,11... | collective-permute-start | bytes 6291464 | tf_op jit(solution)/shard_map/ppermute | solution.py:41
  128.9 50.5 %collective-permute-start.22 = (bf16[512,2048]{1,0:T(8,128)(2,1)}, bf16[512,2048]{1,0:T(8,128)(2,1)}, u32[]{:S(2)}, u32[]{:S(2)}) collective-permute-start(bf16[512,2048]{1,0:T(8,128)(2,1)} %pad_maximum_fusion.4), channel_id=1, source_target_pairs={{0,2},{1,3},{2,0},{3,1},{4,6},{5,7},{6,4},{7,5},{8,10},{9,11},{10,... | collective-permute-start | bytes 6291464 | tf_op jit(solution)/shard_map/ppermute | solution.py:41
  139.3 17.5 %collective-permute-start.6 = (bf16[4,2,256]{2,1,0:T(2,128)(2,1)S(1)}, bf16[4,2,256]{2,1,0:T(2,128)(2,1)S(1)}, u32[]{:S(2)}, u32[]{:S(2)}) collective-permute-start(bf16[4,2,256]{2,1,0:T(2,128)(2,1)S(1)} %pad_maximum_fusion.37), channel_id=1, source_target_pairs={{0,4},{4,0},{1,5},{5,1},{2,6},{6,2},{3,7},{7,3},{8,12},{12,8},{9,1... | collective-permute-start | bytes 12296 | tf_op jit(solution)/shard_map/ppermute | solution.py:36
  156.6 18.8 %collective-permute-start.19 = (f32[2,2,1024]{2,1,0:T(2,128)S(1)}, f32[2,2,1024]{2,1,0:T(2,128)S(1)}, u32[]{:S(2)}, u32[]{:S(2)}) collective-permute-start(f32[2,2,1024]{2,1,0:T(2,128)S(1)} %add.552), channel_id=1, source_target_pairs={{0,1},{1,0},{2,3},{3,2},{4,5},{5,4},{6,7},{7,6},{8,9},{9,8},{10,11... | collective-permute-start | bytes 49160 | tf_op jit(solution)/shard_map/ppermute | solution.py:41
  183.5 52.8 %collective-permute-start.23 = (bf16[512,2048]{1,0:T(8,128)(2,1)}, bf16[512,2048]{1,0:T(8,128)(2,1)}, u32[]{:S(2)}, u32[]{:S(2)}) collective-permute-start(bf16[512,2048]{1,0:T(8,128)(2,1)} %pad_maximum_fusion.5), channel_id=1, source_target_pairs={{0,3},{1,2},{2,1},{3,0},{4,7},{5,6},{6,5},{7,4},{8,11},{9,10},{10,... | collective-permute-start | bytes 6291464 | tf_op jit(solution)/shard_map/ppermute | solution.py:41
  207.3 29.0 %all-to-all-start = ((bf16[4,512,256]{2,1,0:T(8,128)(2,1)}), bf16[4,512,256]{2,1,0:T(8,128)(2,1)S(1)}, u32[]{:S(2)}, u32[]{:S(2)}) async-start(bf16[4,512,256]{2,1,0:T(8,128)(2,1)} %bitcast.22), calls=%async_computation | async-start | bytes 2097152 | tf_op jit(solution)/shard_map/all_to_all | solution.py:606
  211.1 393.8 %reduce-scatter.6.cloned.1.call-start = ((), (), s32[]{:S(2)}) async-start(), calls=%async_computation.7 | async-start | bytes 5242880 | tf_op jit(solution)/shard_map/reduce_scatter | solution.py:644
  266.1 24.1 %collective-permute-start.28 = (bf16[256,2048]{1,0:T(8,128)(2,1)S(1)}, bf16[256,2048]{1,0:T(8,128)(2,1)S(1)}, u32[]{:S(2)}, u32[]{:S(2)}) collective-permute-start(bf16[256,2048]{1,0:T(8,128)(2,1)S(1)} %pad_maximum_fusion.14), channel_id=1, source_target_pairs={{0,2},{1,3},{2,0},{3,1},{4,6},{5,7},{6,4},{7,5},{8,10},{9,11},{10,... | collective-permute-start | bytes 3145736 | tf_op jit(solution)/shard_map/ppermute | solution.py:41
  267.0 23.8 %collective-permute-start.26 = (bf16[256,2048]{1,0:T(8,128)(2,1)S(1)}, bf16[256,2048]{1,0:T(8,128)(2,1)S(1)}, u32[]{:S(2)}, u32[]{:S(2)}) collective-permute-start(bf16[256,2048]{1,0:T(8,128)(2,1)S(1)} %pad_maximum_fusion.13), channel_id=1, source_target_pairs={{0,1},{1,0},{2,3},{3,2},{4,5},{5,4},{6,7},{7,6},{8,9},{9,8},{10,11... | collective-permute-start | bytes 3145736 | tf_op jit(solution)/shard_map/ppermute | solution.py:41
  296.2 23.2 %collective-permute-start.29 = (bf16[256,2048]{1,0:T(8,128)(2,1)}, bf16[256,2048]{1,0:T(8,128)(2,1)}, u32[]{:S(2)}, u32[]{:S(2)}) collective-permute-start(bf16[256,2048]{1,0:T(8,128)(2,1)} %get-tuple-element.157), channel_id=1, source_target_pairs={{0,1},{1,0},{2,3},{3,2},{4,5},{5,4},{6,7},{7,6},{8,9},{9,8},{10,11... | collective-permute-start | bytes 3145736 | tf_op jit(solution)/shard_map/ppermute | solution.py:41
  297.4 24.4 %collective-permute-start.30 = (bf16[256,2048]{1,0:T(8,128)(2,1)}, bf16[256,2048]{1,0:T(8,128)(2,1)}, u32[]{:S(2)}, u32[]{:S(2)}) collective-permute-start(bf16[256,2048]{1,0:T(8,128)(2,1)} %get-tuple-element.157), channel_id=1, source_target_pairs={{0,2},{1,3},{2,0},{3,1},{4,6},{5,7},{6,4},{7,5},{8,10},{9,11},{10,... | collective-permute-start | bytes 3145736 | tf_op jit(solution)/shard_map/ppermute | solution.py:41
  393.7 24.4 %collective-permute-start.41 = (bf16[256,2048]{1,0:T(8,128)(2,1)S(1)}, bf16[256,2048]{1,0:T(8,128)(2,1)S(1)}, u32[]{:S(2)}, u32[]{:S(2)}) collective-permute-start(bf16[256,2048]{1,0:T(8,128)(2,1)S(1)} %pad_maximum_fusion.17), channel_id=1, source_target_pairs={{0,2},{1,3},{2,0},{3,1},{4,6},{5,7},{6,4},{7,5},{8,10},{9,11},{10,... | collective-permute-start | bytes 3145736 | tf_op jit(solution)/shard_map/ppermute | solution.py:41
  395.2 24.1 %collective-permute-start.39 = (bf16[256,2048]{1,0:T(8,128)(2,1)S(1)}, bf16[256,2048]{1,0:T(8,128)(2,1)S(1)}, u32[]{:S(2)}, u32[]{:S(2)}) collective-permute-start(bf16[256,2048]{1,0:T(8,128)(2,1)S(1)} %pad_maximum_fusion.16), channel_id=1, source_target_pairs={{0,1},{1,0},{2,3},{3,2},{4,5},{5,4},{6,7},{7,6},{8,9},{9,8},{10,11... | collective-permute-start | bytes 3145736 | tf_op jit(solution)/shard_map/ppermute | solution.py:41
  424.1 23.2 %collective-permute-start.42 = (bf16[256,2048]{1,0:T(8,128)(2,1)S(1)}, bf16[256,2048]{1,0:T(8,128)(2,1)S(1)}, u32[]{:S(2)}, u32[]{:S(2)}) collective-permute-start(bf16[256,2048]{1,0:T(8,128)(2,1)S(1)} %get-tuple-element.136), channel_id=1, source_target_pairs={{0,1},{1,0},{2,3},{3,2},{4,5},{5,4},{6,7},{7,6},{8,9},{9,8},{10,11... | collective-permute-start | bytes 3145736 | tf_op jit(solution)/shard_map/ppermute | solution.py:41
  424.9 23.4 %collective-permute-start.43 = (bf16[256,2048]{1,0:T(8,128)(2,1)S(1)}, bf16[256,2048]{1,0:T(8,128)(2,1)S(1)}, u32[]{:S(2)}, u32[]{:S(2)}) collective-permute-start(bf16[256,2048]{1,0:T(8,128)(2,1)S(1)} %get-tuple-element.136), channel_id=1, source_target_pairs={{0,2},{1,3},{2,0},{3,1},{4,6},{5,7},{6,4},{7,5},{8,10},{9,11},{10,... | collective-permute-start | bytes 3145736 | tf_op jit(solution)/shard_map/ppermute | solution.py:41
  476.1 200.8 %reduce-scatter.8.cloned.1.call-start = ((), (), s32[]{:S(2)}) async-start(), calls=%async_computation.8 | async-start | bytes 5242880 | tf_op jit(solution)/shard_map/reduce_scatter | solution.py:644
  532.5 214.4 %reduce-scatter.10.cloned.1.call-start = ((), (), s32[]{:S(2)}) async-start(), calls=%async_computation.9 | async-start | bytes 5242880 | tf_op jit(solution)/shard_map/reduce_scatter | solution.py:644
  574.2 24.8 %collective-permute-start.54 = (bf16[256,2048]{1,0:T(8,128)(2,1)}, bf16[256,2048]{1,0:T(8,128)(2,1)}, u32[]{:S(2)}, u32[]{:S(2)}) collective-permute-start(bf16[256,2048]{1,0:T(8,128)(2,1)} %pad_maximum_fusion.20), channel_id=1, source_target_pairs={{0,2},{1,3},{2,0},{3,1},{4,6},{5,7},{6,4},{7,5},{8,10},{9,11},{10,... | collective-permute-start | bytes 3145736 | tf_op jit(solution)/shard_map/ppermute | solution.py:41
  576.1 24.5 %collective-permute-start.52 = (bf16[256,2048]{1,0:T(8,128)(2,1)}, bf16[256,2048]{1,0:T(8,128)(2,1)}, u32[]{:S(2)}, u32[]{:S(2)}) collective-permute-start(bf16[256,2048]{1,0:T(8,128)(2,1)} %pad_maximum_fusion.19), channel_id=1, source_target_pairs={{0,1},{1,0},{2,3},{3,2},{4,5},{5,4},{6,7},{7,6},{8,9},{9,8},{10,11... | collective-permute-start | bytes 3145736 | tf_op jit(solution)/shard_map/ppermute | solution.py:41
  610.7 23.2 %collective-permute-start.55 = (bf16[256,2048]{1,0:T(8,128)(2,1)S(1)}, bf16[256,2048]{1,0:T(8,128)(2,1)S(1)}, u32[]{:S(2)}, u32[]{:S(2)}) collective-permute-start(bf16[256,2048]{1,0:T(8,128)(2,1)S(1)} %get-tuple-element.134), channel_id=1, source_target_pairs={{0,1},{1,0},{2,3},{3,2},{4,5},{5,4},{6,7},{7,6},{8,9},{9,8},{10,11... | collective-permute-start | bytes 3145736 | tf_op jit(solution)/shard_map/ppermute | solution.py:41
  612.0 24.0 %collective-permute-start.56 = (bf16[256,2048]{1,0:T(8,128)(2,1)S(1)}, bf16[256,2048]{1,0:T(8,128)(2,1)S(1)}, u32[]{:S(2)}, u32[]{:S(2)}) collective-permute-start(bf16[256,2048]{1,0:T(8,128)(2,1)S(1)} %get-tuple-element.134), channel_id=1, source_target_pairs={{0,2},{1,3},{2,0},{3,1},{4,6},{5,7},{6,4},{7,5},{8,10},{9,11},{10,... | collective-permute-start | bytes 3145736 | tf_op jit(solution)/shard_map/ppermute | solution.py:41
  638.7 15.4 %collective-permute-start.59 = (bf16[256,2048]{1,0:T(8,128)(2,1)}, bf16[256,2048]{1,0:T(8,128)(2,1)S(1)}, u32[]{:S(2)}, u32[]{:S(2)}) collective-permute-start(bf16[256,2048]{1,0:T(8,128)(2,1)} %copy-done.45), channel_id=1, source_target_pairs={{0,4},{4,0},{1,5},{5,1},{2,6},{6,2},{3,7},{7,3},{8,12},{12,8},{9,1... | collective-permute-start | bytes 3145736 | tf_op jit(solution)/shard_map/ppermute | solution.py:36
  638.7 16.5 %collective-permute-start.60 = (bf16[256,2048]{1,0:T(8,128)(2,1)}, bf16[256,2048]{1,0:T(8,128)(2,1)S(1)}, u32[]{:S(2)}, u32[]{:S(2)}) collective-permute-start(bf16[256,2048]{1,0:T(8,128)(2,1)} %copy-done.37), channel_id=1, source_target_pairs={{0,4},{4,0},{1,5},{5,1},{2,6},{6,2},{3,7},{7,3},{8,12},{12,8},{9,1... | collective-permute-start | bytes 3145736 | tf_op jit(solution)/shard_map/ppermute | solution.py:36
  639.2 17.1 %collective-permute-start.61 = (bf16[256,2048]{1,0:T(8,128)(2,1)}, bf16[256,2048]{1,0:T(8,128)(2,1)S(1)}, u32[]{:S(2)}, u32[]{:S(2)}) collective-permute-start(bf16[256,2048]{1,0:T(8,128)(2,1)} %copy-done.36), channel_id=1, source_target_pairs={{0,4},{4,0},{1,5},{5,1},{2,6},{6,2},{3,7},{7,3},{8,12},{12,8},{9,1... | collective-permute-start | bytes 3145736 | tf_op jit(solution)/shard_map/ppermute | solution.py:36
  665.4 61.2 %all-to-all-start.1 = ((bf16[4,512,256]{2,1,0:T(8,128)(2,1)}), bf16[4,512,256]{2,1,0:T(8,128)(2,1)}, u32[]{:S(2)}, u32[]{:S(2)}) async-start(bf16[4,512,256]{2,1,0:T(8,128)(2,1)} %bitcast.302), calls=%async_computation.2 | async-start | bytes 2097152 | tf_op jit(solution)/shard_map/all_to_all | solution.py:691
  669.8 109.3 %reduce-scatter.14.cloned.1.call-start = ((), (), s32[]{:S(2)}) async-start(), calls=%async_computation.11 | async-start | bytes 1310720 | tf_op jit(solution)/shard_map/reduce_scatter | solution.py:644
  726.6 110.1 %reduce-scatter.12.cloned.1.call-start = ((), (), s32[]{:S(2)}) async-start(), calls=%async_computation.10 | async-start | bytes 3932160 | tf_op jit(solution)/shard_map/reduce_scatter | solution.py:644
  779.1 198.7 %all-gather.13.cloned.1.call-start = ((), (), s32[]{:S(2)}) async-start(), calls=%async_computation.13 | async-start | bytes 2359296 | tf_op jit(solution)/shard_map/all_gather | solution.py:655
  779.7 214.4 %all-gather.19.cloned.1.call-start = ((), (), s32[]{:S(2)}) async-start(), calls=%async_computation.16 | async-start | bytes 9437184 | tf_op jit(solution)/shard_map/all_gather | solution.py:655
  780.4 274.3 %all-gather.15.cloned.1.call-start = ((), (), s32[]{:S(2)}) async-start(), calls=%async_computation.14 | async-start | bytes 9437184 | tf_op jit(solution)/shard_map/all_gather | solution.py:655
  796.6 340.4 %all-gather.17.cloned.1.call-start = ((), (), s32[]{:S(2)}) async-start(), calls=%async_computation.15 | async-start | bytes 9437184 | tf_op jit(solution)/shard_map/all_gather | solution.py:655
  814.2 387.6 %all-gather.11.cloned.1.call-start = ((), (), s32[]{:S(2)}) async-start(), calls=%async_computation.12 | async-start | bytes 7077888 | tf_op jit(solution)/shard_map/all_gather | solution.py:655
  886.0 43.5 %collective-permute-start.70 = (bf16[1024,512]{1,0:T(8,128)(2,1)}, bf16[1024,512]{1,0:T(8,128)(2,1)}, u32[]{:S(2)}, u32[]{:S(2)}) collective-permute-start(bf16[1024,512]{1,0:T(8,128)(2,1)} %pad_maximum_fusion.23), channel_id=1, source_target_pairs={{0,2},{1,3},{2,0},{3,1},{4,6},{5,7},{6,4},{7,5},{8,10},{9,11},{10,... | collective-permute-start | bytes 3145736 | tf_op jit(solution)/shard_map/ppermute | solution.py:41
  887.6 41.9 %collective-permute-start.68 = (bf16[1024,512]{1,0:T(8,128)(2,1)}, bf16[1024,512]{1,0:T(8,128)(2,1)}, u32[]{:S(2)}, u32[]{:S(2)}) collective-permute-start(bf16[1024,512]{1,0:T(8,128)(2,1)} %pad_maximum_fusion.22), channel_id=1, source_target_pairs={{0,1},{1,0},{2,3},{3,2},{4,5},{5,4},{6,7},{7,6},{8,9},{9,8},{10,11... | collective-permute-start | bytes 3145736 | tf_op jit(solution)/shard_map/ppermute | solution.py:41
  893.6 18.9 %collective-permute-start.90 = (f32[33,128]{1,0:T(8,128)S(1)}, f32[33,128]{1,0:T(8,128)S(1)}, u32[]{:S(2)}, u32[]{:S(2)}) collective-permute-start(f32[33,128]{1,0:T(8,128)S(1)} %fusion.126), channel_id=1, source_target_pairs={{0,1},{1,0},{2,3},{3,2},{4,5},{5,4},{6,7},{7,6},{8,9},{9,8},{10,11... | collective-permute-start | bytes 50696 | tf_op jit(solution)/shard_map/ppermute | solution.py:41
  932.4 40.3 %collective-permute-start.73 = (bf16[256,512]{1,0:T(8,128)(2,1)S(1)}, bf16[256,512]{1,0:T(8,128)(2,1)S(1)}, u32[]{:S(2)}, u32[]{:S(2)}) collective-permute-start(bf16[256,512]{1,0:T(8,128)(2,1)S(1)} %get-tuple-element.233), channel_id=1, source_target_pairs={{0,24},{8,16},{16,8},{24,0},{1,25},{9,17},{17,9},{25,1},{2,26},{10... | collective-permute-start | bytes 786440 | tf_op jit(solution)/shard_map/ppermute | solution.py:46
  936.1 36.5 %collective-permute-start.72 = (bf16[256,512]{1,0:T(8,128)(2,1)S(1)}, bf16[256,512]{1,0:T(8,128)(2,1)S(1)}, u32[]{:S(2)}, u32[]{:S(2)}) collective-permute-start(bf16[256,512]{1,0:T(8,128)(2,1)S(1)} %get-tuple-element.234), channel_id=1, source_target_pairs={{0,16},{8,24},{16,0},{24,8},{1,17},{9,25},{17,1},{25,9},{2,18},{10... | collective-permute-start | bytes 786440 | tf_op jit(solution)/shard_map/ppermute | solution.py:46
  936.8 35.9 %collective-permute-start.71 = (bf16[256,512]{1,0:T(8,128)(2,1)S(1)}, bf16[256,512]{1,0:T(8,128)(2,1)S(1)}, u32[]{:S(2)}, u32[]{:S(2)}) collective-permute-start(bf16[256,512]{1,0:T(8,128)(2,1)S(1)} %get-tuple-element.235), channel_id=1, source_target_pairs={{0,8},{8,0},{16,24},{24,16},{1,9},{9,1},{17,25},{25,17},{2,10},{10... | collective-permute-start | bytes 786440 | tf_op jit(solution)/shard_map/ppermute | solution.py:46
  937.3 35.4 %collective-permute-start.87 = (f32[2,256]{1,0:T(2,128)S(1)}, f32[2,256]{1,0:T(2,128)S(1)}, u32[]{:S(2)}, u32[]{:S(2)}) collective-permute-start(f32[2,256]{1,0:T(2,128)S(1)} %bitcast_add_fusion.11), channel_id=1, source_target_pairs={{0,16},{8,24},{16,0},{24,8},{1,17},{9,25},{17,1},{25,9},{2,18},{10... | collective-permute-start | bytes 6152 | tf_op jit(solution)/shard_map/ppermute | solution.py:97
  (125 other events, 1746.8 us)
Sparse Core Ops, SparseCore 0:
  476.3 74.8 reduce-scatter.5
  554.1 77.2 reduce-scatter.7
  634.3 94.0 reduce-scatter.9
  731.3 31.8 reduce-scatter.13
  779.2 57.4 reduce-scatter.11
  838.2 29.5 all-gather.12
  869.4 101.6 all-gather.18
  973.3 81.4 all-gather.14
  1056.4 80.5 all-gather.16
  1138.5 63.2 all-gather.10

commit v3 on v2

--- a/solution.py
+++ b/solution.py
@@ -63,40 +63,50 @@
     return [mine, [send_core(block) for block in mine]]
 
 
-def reduce_shard(term):
+def reduce_steps(term):
     count = lax.axis_size("shard")
     everything = slice(None)
     if count != 4:
+        got = yield [send_shard(term(k, everything).astype(BF), k) for k in range(1, count)]
         result = term(0, everything)
-        for k in range(1, count):
-            result = result + send_shard(term(k, everything).astype(BF), k).astype(F32)
+        for values in got:
+            result = result + values.astype(F32)
         return result
     near, far = slice(0, term.rows // 2), slice(term.rows // 2, None)
-    via_x = send_shard(term(3, near).astype(BF), 1)
-    via_y = send_shard(term(3, far).astype(BF), 2)
+    via_x, via_y = yield (send_shard(term(3, near).astype(BF), 1), send_shard(term(3, far).astype(BF), 2))
     to_y = jnp.concatenate([(term(2, near) + via_x.astype(F32)).astype(BF), term(2, far).astype(BF)], 0)
     to_x = jnp.concatenate([term(1, near).astype(BF), (term(1, far) + via_y.astype(F32)).astype(BF)], 0)
-    return term(0, everything) + send_shard(to_x, 1).astype(F32) + send_shard(to_y, 2).astype(F32)
-
-
-def reduce_plane(other, mine):
+    from_x, from_y = yield (send_shard(to_x, 1), send_shard(to_y, 2))
+    return term(0, everything) + from_x.astype(F32) + from_y.astype(F32)
+
+
+def run_steps(steps, between=lambda values: values):
+    values = next(steps)
+    while True:
+        try:
+            values = steps.send(between(values))
+        except StopIteration as stop:
+            return stop.value
+
+
+def reduce_shard(term):
+    return run_steps(reduce_steps(term))
+
+
+def reduce_plane(other, mine, also):
     got = send_core(other.astype(BF))
-    mine, got = lax.optimization_barrier((mine.astype(BF), got))
+    mine, got, also = lax.optimization_barrier((mine.astype(BF), got, also))
 
     def term(k, part):
         return mine[k, part].astype(F32) + got[k, part].astype(F32)
 
     term.rows = mine.shape[1]
-    return reduce_shard(term)
+    return reduce_shard(term), also
 
 
 def sum_over_planes(values):
-    count = lax.axis_size("z")
-    step = 1
-    while step < count:
-        values = values + lax.ppermute(values, "z", [(i, i ^ step) for i in range(count)])
-        step *= 2
-    return values
+    parts = [send_plane(values, k) for k in range(1, lax.axis_size("z"))]
+    return sum(parts, values)
 
 
 def sum_plane(values, swapped=False):
@@ -225,10 +235,11 @@
 def input_terms_kernel(count, *refs):
     tokens, grads, out = refs[: 2 * count], refs[2 * count], refs[2 * count + 1]
     rows = tokens[0].shape[0]
-    planes, _, share, cols = out.shape
+    planes, _, _, share, third = out.shape
     for k in range(count):
         total = contract_rows(tokens[k][...], grads[:rows, :]) + contract_rows(tokens[count + k][...], grads[rows:, :])
-        out[:, k] = total.astype(BF).reshape(planes, share, cols)
+        for n in range(3):
+            out[:, k, n] = total[:, n * third : (n + 1) * third].astype(BF).reshape(planes, share, third)
 
 
 def input_terms(pieces, grads, planes):
@@ -236,10 +247,43 @@
     chunk = pieces[0][0].shape[1]
     return pl.pallas_call(
         functools.partial(input_terms_kernel, count),
-        out_shape=jax.ShapeDtypeStruct((planes, count, chunk // planes, grads.shape[1]), BF),
+        out_shape=jax.ShapeDtypeStruct((planes, count, 3, chunk // planes, grads.shape[1] // 3), BF),
         compiler_params=pltpu.CompilerParams(vmem_limit_bytes=56 * 1024 * 1024),
         name="input_terms",
     )(*pieces[0], *pieces[1], grads)
+
+
+def attention_out_kernel(shards, share, copies, query, key, value, output):
+    _, cores, _, cols = copies.shape
+    for n, out in enumerate((query, key, value)):
+        for s in range(shards):
+            for c in range(cores):
+                at = (s * cores + c) * cols
+                row = (s * 3 + n) * share
+                out[:, at : at + cols] = copies[0, c, row : row + share, :].astype(F32)
+    first = shards * 3 * share
+    rows = output.shape[1]
+    for c in range(cores):
+        for j in range(output.shape[2] // cols):
+            row = first + j * rows
+            output[c, :, j * cols : (j + 1) * cols] = copies[0, c, row : row + rows, :].astype(F32)
+
+
+def attention_out(copies, shards, share):
+    planes, cores, total, cols = copies.shape
+    wide = shards * cores * cols
+    rows = (total - shards * 3 * share) * cols // wide
+    return pl.pallas_call(
+        functools.partial(attention_out_kernel, shards, share),
+        grid=(planes,),
+        in_specs=[pl.BlockSpec((1, cores, total, cols), lambda i: (i, 0, 0, 0))],
+        out_specs=[pl.BlockSpec((share, wide), lambda i: (i, 0))] * 3
+        + [pl.BlockSpec((cores, rows, wide), lambda i: (0, i, 0))],
+        out_shape=[jax.ShapeDtypeStruct((planes * share, wide), F32)] * 3
+        + [jax.ShapeDtypeStruct((cores, planes * rows, wide), F32)],
+        compiler_params=pltpu.CompilerParams(vmem_limit_bytes=40 * 1024 * 1024),
+        name="attention_out",
+    )(copies)
 
 
 def memory_block(block, where, blocks, per_device):
@@ -535,6 +579,18 @@
             [lax.dynamic_index_in_dim(stacked, shard ^ j, 0, keepdims=False) for j in range(shards)]
         )
 
+    def column_block(weight, k, cols):
+        return lax.dynamic_slice_in_dim(weight, ((shard ^ k) * 2 + core) * cols, cols, 1)
+
+    gain_rows = jnp.pad(
+        jnp.stack([attention_gain, feed_gain]), ((0, 14), (0, 3 * head_cols - attention_gain.shape[0]))
+    )
+
+    def input_block(k):
+        block = [column_block(w, k, head_cols) for w in (query_weight, key_weight, value_weight)]
+        return jnp.concatenate([jnp.concatenate(block, 1), gain_rows], 0)
+
+    input_blocks = [input_block(0)] + [send_shard(input_block(k), k) for k in range(1, shards)]
     info_rows = 2 * rows // chunk
     info = jnp.stack([piece_index[0], pad_flags[0]]).astype(BF).reshape(info_rows, chunk)
     info = jnp.pad(info, ((0, 16 - info_rows), (0, 0)))
@@ -547,6 +603,12 @@
         lax.dynamic_index_in_dim(by_seq, shard ^ plane ^ k, 0, keepdims=False) for k in range(planes)
     ]
     by_plane = jnp.stack([send_plane(by_plane[k], k) if k else by_plane[k] for k in range(planes)])
+    rates = theta_base ** (-jnp.arange(HEAD // 2).astype(F32) * (2.0 / HEAD))
+    angles = jnp.arange(seq_len, dtype=jnp.int32).astype(F32)[:, None] * rates[None, :]
+    cosine, sine = jnp.cos(angles), jnp.sin(angles)
+    cosine = jnp.concatenate([cosine, cosine], 1)
+    sine = jnp.concatenate([-sine, sine], 1)
+    by_plane, input_blocks, cosine, sine = tie((by_plane, input_blocks, cosine, sine))
     mine = by_plane[:, :rows].reshape(planes * rows, chunk)
     info_mine = by_plane[:, rows : rows + info_rows].reshape(planes, 2, rows)
     info_mine = jnp.stack(
@@ -560,43 +622,30 @@
     block_flags = jnp.concatenate([block_flags, core[None], plane[None]])
     key_bias = jnp.where(pad_seq > 0.0, masked_score, 0.0)[:, None]
 
-    def column_block(weight, k, cols):
-        return lax.dynamic_slice_in_dim(weight, ((shard ^ k) * 2 + core) * cols, cols, 1)
-
-    gain_rows = jnp.pad(
-        jnp.stack([attention_gain, feed_gain]), ((0, 14), (0, 3 * head_cols - attention_gain.shape[0]))
-    )
-
-    def input_block(k):
-        block = [column_block(w, k, head_cols) for w in (query_weight, key_weight, value_weight)]
-        return jnp.concatenate([jnp.concatenate(block, 1), gain_rows], 0)
-
-    input_blocks = [input_block(0)] + [send_shard(input_block(k), k) for k in range(1, shards)]
     gains = absolute_shards([b[chunk : chunk + 2, : attention_gain.shape[0]] for b in input_blocks])
     gains = gains.transpose(1, 0, 2).reshape(2, width).astype(F32)
     out_block = lax.dynamic_slice_in_dim(output_weight, core * head_cols, head_cols, 0)
     down_block = lax.dynamic_slice_in_dim(down_weight, core * feed_cols, feed_cols, 0)
     query_gain_here = lax.dynamic_slice_in_dim(query_gain, core * head_cols, head_cols, 0).astype(F32)[None]
     key_gain_here = lax.dynamic_slice_in_dim(key_gain, core * head_cols, head_cols, 0).astype(F32)[None]
-    rates = theta_base ** (-jnp.arange(HEAD // 2).astype(F32) * (2.0 / HEAD))
-    angles = jnp.arange(seq_len, dtype=jnp.int32).astype(F32)[:, None] * rates[None, :]
-    cosine, sine = jnp.cos(angles), jnp.sin(angles)
-    cosine = jnp.concatenate([cosine, cosine], 1)
-    sine = jnp.concatenate([-sine, sine], 1)
-
+
+    def feed_block(k):
+        return [column_block(w, k, feed_cols) for w in (gate_weight, up_weight)]
+
+    last = shards - 1
+    feed_own = [jnp.concatenate(feed_block(k), 1) for k in range(last)]
+    feed_last = feed_block(last)
     gathered = gather_shard(mine)
-    gate_weight, up_weight, gathered = tie((gate_weight, up_weight, gathered))
+    feed_own, feed_last, gathered = tie((feed_own, feed_last, gathered))
     gathered = [gathered, [send_core(block) for block in gathered]]
-
-    def feed_block(k):
-        return jnp.concatenate([column_block(w, k, feed_cols) for w in (gate_weight, up_weight)], 1)
-
-    feed_blocks = [feed_block(0)] + [send_shard(feed_block(k), k) for k in range(1, shards - 1)]
+    gate_last = send_shard(feed_last[0], last)
+
     inputs_here = gathered
     raw, squares = project(inputs_here, input_blocks)
     squares = sum_plane(squares.reshape(2, 2, seq_len // 2), True)
-    squares, feed_blocks, gate_weight, up_weight = tie((squares, feed_blocks, gate_weight, up_weight))
-    feed_blocks.append(send_shard(feed_block(shards - 1), shards - 1))
+    squares, gate_last, feed_own, feed_last = tie((squares, gate_last, feed_own, feed_last))
+    feed_blocks = feed_own[:1] + [send_shard(feed_own[k], k) for k in range(1, last)]
+    up_last = send_shard(feed_last[1], last)
     squares = squares.reshape(2, seq_len // PIECE, PIECE)
     per_block = rows // PIECE
     attended_seq, query_low, key_low, value_low, lse = attend_forward(
@@ -609,16 +658,17 @@
     attended, feed_blocks = tie((attended, feed_blocks))
     attended = plane_relative(attended).reshape(everything, head_cols)
     half = everything // 2
+
+    def blocks_of(values):
+        return values.reshape(shards, rows, values.shape[-1])
+
+    branch_attn, up_last = reduce_plane(
+        blocks_of(mm(attended[half:], out_block)), blocks_of(mm(attended[:half], out_block)), up_last
+    )
+    feed_blocks.append(jnp.concatenate([gate_last, up_last], 1))
     whole_feed = jnp.zeros((width, 2 * feed_cols), BF)
     for k in range(shards):
         whole_feed = lax.dynamic_update_slice_in_dim(whole_feed, feed_blocks[k], (shard ^ k) * chunk, 0)
-
-    def blocks_of(values):
-        return values.reshape(shards, rows, values.shape[-1])
-
-    branch_attn = reduce_plane(
-        blocks_of(mm(attended[half:], out_block)), blocks_of(mm(attended[:half], out_block))
-    )
     attn_factor = norm_factor(branch_attn)
     residual = tokens.astype(F32) + branch_attn * attn_factor * gains[0]
     gathered = gather_plane(residual.astype(BF))
@@ -626,8 +676,8 @@
     gate = mm(residual_all, whole_feed[:, :feed_cols])
     up = mm(residual_all, whole_feed[:, feed_cols:])
     activated = (jax.nn.silu(gate) * up).astype(BF)
-    branch_feed = reduce_plane(
-        blocks_of(mm(activated[half:], down_block)), blocks_of(mm(activated[:half], down_block))
+    branch_feed, _ = reduce_plane(
+        blocks_of(mm(activated[half:], down_block)), blocks_of(mm(activated[:half], down_block)), ()
     )
     feed_factor = norm_factor(branch_feed)
     result = residual + branch_feed * feed_factor * gains[1]
@@ -692,24 +742,33 @@
         grad_mixed.reshape(shards, 2 * rows, head_cols), "z", 0, 0, tiled=True
     ).reshape(seq_len, head_cols)
     grad_output = contract_rows(attended, grad_branch_all).astype(BF)
-    grad_output, grad_mixed, gate_share = tie((grad_output, grad_mixed, gate_share))
-    output_share = plane_share(grad_output.reshape(planes, head_cols // planes, width))
+    output_rows = head_cols // planes
+    output_part = grad_output.reshape(planes, output_rows, width // head_cols, head_cols).transpose(0, 2, 1, 3)
+    output_part, grad_mixed, gate_share = tie((output_part, grad_mixed, gate_share))
+    down_all = copies(down_share)
     scaled_q, scaled_k, grad_values, inner, grad_gains = attend_backward(
         query_low, key_low, value_low, grad_mixed, attended_seq, raw, squares, query_gain_here, key_gain_here,
         cosine, sine, key_bias, block_flags, lse, per_block,
     )
-    inner, up_share = tie((inner, up_share))
+    inner, up_share, down_share = tie((inner, up_share, down_share))
     inner = sum_plane(jnp.sum(inner, 0).reshape(2, 2, seq_len // 2), True).reshape(squares.shape)
     grad_raw = finish(scaled_q, scaled_k, grad_values, raw, squares, inner)
     input_part = input_terms(inputs_here, grad_raw, planes)
-    grad_raw, input_part = tie((grad_raw, input_part))
-    input_share = plane_share(input_part)
+    heads_part = jnp.concatenate(
+        [input_part.reshape(planes, -1, head_cols), output_part.reshape(planes, -1, head_cols)], 1
+    )
+    grad_raw, heads_part = tie((grad_raw, heads_part))
+    heads_part, down_all = tie((heads_part, down_all))
+    heads_share = plane_share(heads_part)
+    share = chunk // planes
+    input_share = heads_share[: shards * 3 * share].reshape(shards, 3 * share, head_cols)
+    output_share = heads_share[shards * 3 * share :]
     seq_half = seq_len // 2
 
     def chunks_of(values):
-        return jnp.stack([contract_cols(values, block[:chunk]) for block in input_blocks])
-
-    grad_chunk = reduce_plane(chunks_of(grad_raw[seq_half:]), chunks_of(grad_raw[:seq_half]))
+        return jnp.stack([contract_cols(values, block[:chunk]) for block in input_blocks]).astype(BF)
+
+    grad_chunk, _ = reduce_plane(chunks_of(grad_raw[seq_half:]), chunks_of(grad_raw[:seq_half]), ())
     grad_chunk = grad_chunk.astype(BF).reshape(planes, rows, chunk)
     grad_chunk = jnp.stack([send_plane(grad_chunk[k], k) if k else grad_chunk[k] for k in range(planes)])
     by_shard = [
@@ -719,11 +778,13 @@
     grad_chunk = absolute_shards(by_shard)
     grad_tokens = grad_resid + grad_chunk.transpose(1, 0, 2).reshape(rows, width).astype(F32)
 
-    grad_down_weight = rows_out(copies(down_share))
+    grad_down_weight = rows_out(down_all)
     (grad_gate_weight,) = columns_out(copies(to_owner(gate_share, False)), 1)
     (grad_up_weight,) = columns_out(copies(to_owner(up_share, False)), 1)
-    grad_output_weight = rows_out(copies(output_share))
-    grad_query_weight, grad_key_weight, grad_value_weight = columns_out(copies(to_owner(input_share, True)), 3)
+    input_share = to_owner(input_share, True).reshape(-1, head_cols)
+    heads_all = copies(jnp.concatenate([input_share, output_share], 0))
+    grad_query_weight, grad_key_weight, grad_value_weight, grad_output_weight = attention_out(heads_all, shards, share)
+    grad_output_weight = grad_output_weight.reshape(output_weight.shape)
 
     valid = (pad_flags[0] == 0).astype(F32)[:, None]
     stat_terms = jnp.stack(

time: 1230 us -> 1170 us (0.951)
  waiting for transfers between devices: 674 us -> 614 us
  starting transfers between devices: 92.4 us -> 109 us
    all_gather x5 -> x4, waiting for transfers between devices: 177 us -> 108 us  [copies(): whole = lax.all_gather(values, ('z', 'core'), axis=0)]
    ppermute x4 -> x0, waiting for transfers between devices: 41.3 us -> none  [sum_over_planes(): lax.ppermute(values, 'z', [(i, i ^ step) for i in range(count)])]
    ppermute x6 -> x12, waiting for transfers between devices: 23 us -> 54.7 us  [send_plane(): return lax.ppermute(values, 'z', [(i, i ^ k) for i in range(count)])]
    reduce_scatter x5 -> x4, waiting for transfers between devices: 22.5 us -> 44.9 us  [plane_share(): share = lax.psum_scatter(flat, 'z', scatter_dimension=0, tiled=True)]
    ppermute x6 -> x12, starting transfers between devices: 9.34 us -> 29.3 us  [send_plane(): return lax.ppermute(values, 'z', [(i, i ^ k) for i in range(count)])]
    ppermute x59 -> x60, waiting for transfers between devices: 321 us -> 325 us  [send_shard(): return lax.ppermute(values, 'shard', [(i, i ^ k) for i in range(count)])]
    unnamed x170 -> x175, local copies, waits for them, and re-layouts: 41.9 us -> 45.4 us
    ppermute x59 -> x60, starting transfers between devices: 65.5 us -> 67.5 us  [send_shard(): return lax.ppermute(values, 'shard', [(i, i ^ k) for i in range(count)])]
  transfers between devices with their start and end apart: 106 -> 107, of which waited for: 64 -> 70; matrix products, arithmetic and copies ran while one was open for 17% -> 17% of each run, Pallas kernels for 10% -> 10%
where the time goes in v3:
time: 1170 us; the launch traced here: 1160 us
  waiting for transfers between devices  614 us (52%)
  matrix products  140 us (12%)
  Pallas kernels  125 us (11%)
  starting transfers between devices  109 us (9%)
  local copies, waits for them, and re-layouts  81.4 us (7%)
  other arithmetic  71.5 us (6%)
  between operations  17.1 us (1%)
    ppermute x60, waiting for transfers between devices, send_shard(): return lax.ppermute(values, 'shard', [(i, i ^ k) for i in range(count)])  325 us
    all_gather x4, waiting for transfers between devices, copies(): whole = lax.all_gather(values, ('z', 'core'), axis=0)  108 us
    dot_general x14, matrix products, contract_cols(): lax.dot_general(left, right, (((1,), (1,)), ((), ())), preferred_element_...  79.3 us
    ppermute x60, starting transfers between devices, send_shard(): return lax.ppermute(values, 'shard', [(i, i ^ k) for i in range(count)])  67.5 us
    ppermute x12, waiting for transfers between devices, send_plane(): return lax.ppermute(values, 'z', [(i, i ^ k) for i in range(count)])  54.7 us
    unnamed x175, local copies, waits for them, and re-layouts  45.4 us
    reduce_scatter x4, waiting for transfers between devices, plane_share(): share = lax.psum_scatter(flat, 'z', scatter_dimension=0, tiled=True)  44.9 us
    all_to_all x1, waiting for transfers between devices, per_device(): lax.all_to_all(grad_mixed.reshape(shards, 2 * rows, head_cols), 'z', 0, 0...  44.5 us
  transfers between devices with their start and end apart: 107, of which 70 were waited for; matrix products, arithmetic and copies ran while one was open for 17% of the time, Pallas kernels for 10%

profile of v3, /device:TPU:0, one launch (start us, length us, event | category | flops | bytes accessed | tf_op | source)
XLA Modules:
  0.0 1158.4 jit_solution(12970268372811204670)
XLA Ops:
  40.2 12.3 %collective-permute-start.3 = (bf16[272,512]{1,0:T(8,128)(2,1)S(1)}, bf16[272,512]{1,0:T(8,128)(2,1)S(1)}, u32[]{:S(2)}, u32[]{:S(2)}) collective-permute-start(bf16[272,512]{1,0:T(8,128)(2,1)S(1)} %get-tuple-element.235), channel_id=1, source_target_pairs={{0,8},{8,0},{16,24},{24,16},{1,9},{9,1},{17,25},{25,17},{2,10},{10... | collective-permute-start | bytes 835592 | tf_op jit(solution)/shard_map/ppermute | solution.py:46
  62.9 10.2 collective-permute-done.7.refs_10_
  83.4 14.5 %collective-permute-done.11.refs_2_ = bf16[1024,512]{1,0:T(8,128)(2,1)} collective-permute-done((bf16[1024,512]{1,0:T(8,128)(2,1)S(1)}, bf16[1024,512]{1,0:T(8,128)(2,1)}, u32[]{:S(2)}, u32[]{:S(2)}) %collective-permute-start.11) | collective-permute-done | bytes 1048608 | tf_op jit(solution)/shard_map/ppermute | solution.py:41
  124.9 12.3 %project.1 = (f32[2048,768]{1,0:T(8,128)}, f32[2,8,256]{2,1,0:T(8,128)S(1)}) custom-call(bf16[1024,512]{1,0:T(8,128)(2,1)S(1)} %bitcast.282, bf16[1024,512]{1,0:T(8,128)(2,1)} %collective-permute-done.10.refs_1_, bf16[1024,512]{1,0:T(8,128)(2,1)} %collective-permute-done.11.refs_2_, bf16[1024,512]{1,0:T(8,128)(2,1)} %pad_maximum_fusion.14.refs_3_, ...), custom_call_target="tpu_custom_call" | custom-call | tf_op jit(solution)/shard_map/project/pallas_call | solution.py:217
  150.7 19.7 %attend_forward.1 = (bf16[2048,256]{1,0:T(8,128)(2,1)}, bf16[2048,256]{1,0:T(8,128)(2,1)}, bf16[2048,256]{1,0:T(8,128)(2,1)}, bf16[2048,256]{1,0:T(8,128)(2,1)}, f32[2,1,2048]{2,1,0:T(1,128)S(1)}) custom-call(s32[10]{0:T(128)S(1)} %pad_add_fusion.flags, f32[2048,768]{1,0:T(8,128)} %get-tuple-element.92.raw_q.raw_k.raw_v.raw, ...), custom_call_target="tpu_custom_call" | custom-call | tf_op jit(solution)/shard_map/attend_forward/pallas_call | solution.py:352
  174.9 23.2 %all-to-all-done = bf16[4,512,256]{2,1,0:T(8,128)(2,1)S(1)} async-done(((bf16[4,512,256]{2,1,0:T(8,128)(2,1)}), bf16[4,512,256]{2,1,0:T(8,128)(2,1)S(1)}, u32[]{:S(2)}, u32[]{:S(2)}) %all-to-all-start) | async-done | bytes 1048608 | tf_op jit(solution)/shard_map/all_to_all | solution.py:655
  203.4 23.7 %collective-permute-done.25 = bf16[512,1024]{1,0:T(8,128)(2,1)S(1)} collective-permute-done((bf16[512,1024]{1,0:T(8,128)(2,1)S(1)}, bf16[512,1024]{1,0:T(8,128)(2,1)S(1)}, u32[]{:S(2)}, u32[]{:S(2)}) %collective-permute-start.25) | collective-permute-done | bytes 1048608 | tf_op jit(solution)/shard_map/ppermute | solution.py:41
  232.5 11.1 collective-permute-done.26
  251.6 19.4 %collective-permute-done.29 = bf16[256,2048]{1,0:T(8,128)(2,1)S(1)} collective-permute-done((bf16[256,2048]{1,0:T(8,128)(2,1)S(1)}, bf16[256,2048]{1,0:T(8,128)(2,1)S(1)}, u32[]{:S(2)}, u32[]{:S(2)}) %collective-permute-start.29) | collective-permute-done | bytes 1048608 | tf_op jit(solution)/shard_map/ppermute | solution.py:41
  284.5 15.0 %collective-permute-done.30 = bf16[256,2048]{1,0:T(8,128)(2,1)} collective-permute-done((bf16[256,2048]{1,0:T(8,128)(2,1)}, bf16[256,2048]{1,0:T(8,128)(2,1)}, u32[]{:S(2)}, u32[]{:S(2)}) %collective-permute-start.30) | collective-permute-done | bytes 1048608 | tf_op jit(solution)/shard_map/ppermute | solution.py:41
  315.9 11.7 %fusion.8 = f32[2048,1024]{1,0:T(8,128)} fusion(bf16[2048,2048]{1,0:T(8,128)(2,1)S(1)} %constant_dynamic-update-slice_fusion.tokens, bf16[2048,2048]{1,0:T(8,128)(2,1)S(1)} %maximum_dynamic-update-slice_fusion), kind=kOutput, calls=%fused_computation.22 | convolution fusion | flops 8589934592 | bytes 20971520 | tf_op jit(solution)/shard_map/dot_general | solution.py:24
  327.6 14.6 %multiply_convert_fusion.2 = (bf16[2048,1024]{1,0:T(8,128)(2,1)}, f32[2048,1024]{1,0:T(8,128)}) fusion(f32[2048,1024]{1,0:T(8,128)} %fusion.8, bf16[2048,2048]{1,0:T(8,128)(2,1)S(1)} %constant_dynamic-update-slice_fusion.tokens, bf16[2048,2048]{1,0:T(8,128)(2,1)S(1)} %maximum_dynamic-update-slice_fusion), kind=kOutput, calls=%fused_computation.4 | convolution fusion | flops 8602517504 | bytes 33554432 | tf_op jit(solution)/shard_map/dot_general | solution.py:24
  342.2 7.5 convolution_convert_fusion.3
  349.8 7.3 convolution_convert_fusion.4
  359.8 12.5 %collective-permute-done.39 = bf16[128,2048]{1,0:T(8,128)(2,1)S(1)} collective-permute-done((bf16[128,2048]{1,0:T(8,128)(2,1)S(1)}, bf16[128,2048]{1,0:T(8,128)(2,1)S(1)}, u32[]{:S(2)}, u32[]{:S(2)}) %collective-permute-start.39) | collective-permute-done | bytes 524320 | tf_op jit(solution)/shard_map/ppermute | solution.py:41
  375.3 22.6 %collective-permute-done.42 = bf16[256,2048]{1,0:T(8,128)(2,1)S(1)} collective-permute-done((bf16[256,2048]{1,0:T(8,128)(2,1)S(1)}, bf16[256,2048]{1,0:T(8,128)(2,1)S(1)}, u32[]{:S(2)}, u32[]{:S(2)}) %collective-permute-start.42) | collective-permute-done | bytes 1048608 | tf_op jit(solution)/shard_map/ppermute | solution.py:41
  405.5 21.4 %collective-permute-done.43 = bf16[256,2048]{1,0:T(8,128)(2,1)S(1)} collective-permute-done((bf16[256,2048]{1,0:T(8,128)(2,1)S(1)}, bf16[256,2048]{1,0:T(8,128)(2,1)S(1)}, u32[]{:S(2)}, u32[]{:S(2)}) %collective-permute-start.43) | collective-permute-done | bytes 1048608 | tf_op jit(solution)/shard_map/ppermute | solution.py:41
  430.9 7.3 collective-permute-done.45
  444.8 10.9 convolution_convert_fusion
  455.9 22.1 %multiply_convert_fusion = (bf16[2048,1024]{1,0:T(8,128)(2,1)S(1)}, bf16[2048,1024]{1,0:T(8,128)(2,1)}) fusion(f32[2048,1024]{1,0:T(8,128)} %fusion.8, f32[2048,1024]{1,0:T(8,128)} %get-tuple-element.308, bf16[2048,2048]{1,0:T(8,128)(2,1)} %copy-done.57, bf16[2048,2048]{1,0:T(8,128)(2,1)} %param.25, s32[]{:T(128)S(6)} %select_n.247), kind=kOutput, calls=%fused_computation.2 | convolution fusion | flops 8617197568 | bytes 37748740 | tf_op jit(solution)/shard_map/dot_general | solution.py:32
  478.0 12.3 %fusion.6 = f32[1024,2048]{1,0:T(8,128)} fusion(bf16[2048,2048]{1,0:T(8,128)(2,1)} %copy-done.40, bf16[2048,1024]{1,0:T(8,128)(2,1)} %get-tuple-element.118.grads), kind=kOutput, calls=%fused_computation.20 | convolution fusion | flops 4294967296 | bytes 14680064 | tf_op jit(solution)/shard_map/dot_general | solution.py:32
  490.3 8.4 add_convert_fusion.1
  498.8 11.5 weight_terms.2
  512.5 11.0 fusion
  523.5 9.8 add_convert_fusion
  533.3 11.3 weight_terms.3
  552.4 12.2 %collective-permute-done.52 = bf16[128,2048]{1,0:T(8,128)(2,1)S(1)} collective-permute-done((bf16[128,2048]{1,0:T(8,128)(2,1)S(1)}, bf16[128,2048]{1,0:T(8,128)(2,1)S(1)}, u32[]{:S(2)}, u32[]{:S(2)}) %collective-permute-start.52) | collective-permute-done | bytes 524320 | tf_op jit(solution)/shard_map/ppermute | solution.py:41
  569.6 22.3 %collective-permute-done.55 = bf16[256,2048]{1,0:T(8,128)(2,1)S(1)} collective-permute-done((bf16[256,2048]{1,0:T(8,128)(2,1)S(1)}, bf16[256,2048]{1,0:T(8,128)(2,1)S(1)}, u32[]{:S(2)}, u32[]{:S(2)}) %collective-permute-start.55) | collective-permute-done | bytes 1048608 | tf_op jit(solution)/shard_map/ppermute | solution.py:41
  603.6 21.4 %collective-permute-done.56 = bf16[256,2048]{1,0:T(8,128)(2,1)S(1)} collective-permute-done((bf16[256,2048]{1,0:T(8,128)(2,1)S(1)}, bf16[256,2048]{1,0:T(8,128)(2,1)S(1)}, u32[]{:S(2)}, u32[]{:S(2)}) %collective-permute-start.56) | collective-permute-done | bytes 1048608 | tf_op jit(solution)/shard_map/ppermute | solution.py:41
  659.5 6.2 convolution_convert_fusion.6
  667.0 44.5 %all-to-all-done.1 = bf16[4,512,256]{2,1,0:T(8,128)(2,1)S(1)} async-done(((bf16[4,512,256]{2,1,0:T(8,128)(2,1)}), bf16[4,512,256]{2,1,0:T(8,128)(2,1)S(1)}, u32[]{:S(2)}, u32[]{:S(2)}) %all-to-all-start.1) | async-done | bytes 1048608 | tf_op jit(solution)/shard_map/all_to_all | solution.py:741
  712.5 20.1 %attend_backward.1 = (f32[2048,256]{1,0:T(8,128)}, f32[2048,256]{1,0:T(8,128)}, bf16[2048,256]{1,0:T(8,128)(2,1)}, f32[2,2,8,256]{3,2,1,0:T(8,128)}, f32[2,2,128]{2,1,0:T(2,128)}) custom-call(s32[10]{0:T(128)} %copy-done.26, bf16[2048,256]{1,0:T(8,128)(2,1)} %get-tuple-element.126.queries, bf16[2048,256]{1,0:T(8,128)(2,1)} %get-tuple-element.127.keys, ...), custom_call_target="tpu_custom_call" | custom-call | tf_op jit(solution)/shard_map/attend_backward/pallas_call | solution.py:443
  743.2 8.7 finish.1.refs_8_
  751.9 12.8 %input_terms.1 = bf16[4,4,3,128,256]{4,3,2,1,0:T(8,128)(2,1)} custom-call(bf16[1024,512]{1,0:T(8,128)(2,1)} %bitcast.283, bf16[1024,512]{1,0:T(8,128)(2,1)} %collective-permute-done.10.refs_1_, bf16[1024,512]{1,0:T(8,128)(2,1)} %collective-permute-done.11.refs_2_, bf16[1024,512]{1,0:T(8,128)(2,1)} %pad_maximum_fusion.14.refs_3_, ...), custom_call_target="tpu_custom_call" | custom-call | tf_op jit(solution)/shard_map/input_terms/pallas_call | solution.py:248
  768.9 27.7 %all-gather.9.cloned.1.call-done = bf16[2048,2048]{1,0:T(8,128)(2,1)} async-done(((bf16[256,2048]{1,0:T(8,128)(2,1)}), bf16[2048,2048]{1,0:T(8,128)(2,1)}) %all-gather.9.cloned.1.call-update) | async-done | bytes 8388624 | tf_op jit(solution)/shard_map/all_gather | solution.py:705
  800.3 6.6 collective-permute-done.83
  817.0 6.6 collective-permute-done.86
  829.8 44.9 %reduce-scatter.11.cloned.1.call-done = bf16[2048,256]{1,0:T(8,128)(2,1)} async-done(((bf16[8192,256]{1,0:T(8,128)(2,1)}), bf16[2048,256]{1,0:T(8,128)(2,1)}) %reduce-scatter.11.cloned.1.call-update) | async-done | bytes 1048592 | tf_op jit(solution)/shard_map/reduce_scatter | solution.py:694
  909.5 8.6 collective-permute-done.68
  925.6 21.7 %collective-permute-done.92 = f32[33,128]{1,0:T(8,128)S(1)} collective-permute-done((f32[33,128]{1,0:T(8,128)S(1)}, f32[33,128]{1,0:T(8,128)S(1)}, u32[]{:S(2)}, u32[]{:S(2)}) %collective-permute-start.92) | collective-permute-done | bytes 16928 | tf_op jit(solution)/shard_map/ppermute | solution.py:41
  972.9 10.8 collective-permute-done.74
  983.8 34.1 %collective-permute-done.73 = bf16[256,512]{1,0:T(8,128)(2,1)S(1)} collective-permute-done((bf16[256,512]{1,0:T(8,128)(2,1)S(1)}, bf16[256,512]{1,0:T(8,128)(2,1)S(1)}, u32[]{:S(2)}, u32[]{:S(2)}) %collective-permute-start.73) | collective-permute-done | bytes 262176 | tf_op jit(solution)/shard_map/ppermute | solution.py:46
  1032.2 10.3 rows_out.1
  1045.9 6.2 columns_out.2
  1052.1 7.0 all-gather.15.cloned.1.call-done
  1062.4 6.5 columns_out.3
  1068.9 72.9 %all-gather.11.cloned.1.call-done = bf16[16384,256]{1,0:T(8,128)(2,1)} async-done(((bf16[2048,256]{1,0:T(8,128)(2,1)}), bf16[16384,256]{1,0:T(8,128)(2,1)}) %all-gather.11.cloned.1.call-update) | async-done | bytes 8388624 | tf_op jit(solution)/shard_map/all_gather | solution.py:705
  1145.1 6.0 attention_out.1
  (537 shorter events, 359.6 us)
Async XLA Ops:
  34.9 28.0 %collective-permute-start.6 = (bf16[528,768]{1,0:T(8,128)(2,1)S(1)}, bf16[528,768]{1,0:T(8,128)(2,1)S(1)}, u32[]{:S(2)}, u32[]{:S(2)}) collective-permute-start(bf16[528,768]{1,0:T(8,128)(2,1)S(1)} %get-tuple-element.277), channel_id=1, source_target_pairs={{0,1},{1,0},{2,3},{3,2},{4,5},{5,4},{6,7},{7,6},{8,9},{9,8},{10,11... | collective-permute-start | bytes 2433032 | tf_op jit(solution)/shard_map/ppermute | solution.py:41
  36.4 36.7 %collective-permute-start.7 = (bf16[528,768]{1,0:T(8,128)(2,1)S(1)}, bf16[528,768]{1,0:T(8,128)(2,1)S(1)}, u32[]{:S(2)}, u32[]{:S(2)}) collective-permute-start(bf16[528,768]{1,0:T(8,128)(2,1)S(1)} %get-tuple-element.278), channel_id=1, source_target_pairs={{0,2},{1,3},{2,0},{3,1},{4,6},{5,7},{6,4},{7,5},{8,10},{9,11},{10,... | collective-permute-start | bytes 2433032 | tf_op jit(solution)/shard_map/ppermute | solution.py:41
  37.1 36.0 %collective-permute-start.8 = (bf16[528,768]{1,0:T(8,128)(2,1)S(1)}, bf16[528,768]{1,0:T(8,128)(2,1)S(1)}, u32[]{:S(2)}, u32[]{:S(2)}) collective-permute-start(bf16[528,768]{1,0:T(8,128)(2,1)S(1)} %get-tuple-element.276), channel_id=1, source_target_pairs={{0,3},{1,2},{2,1},{3,0},{4,7},{5,6},{6,5},{7,4},{8,11},{9,10},{10,... | collective-permute-start | bytes 2433032 | tf_op jit(solution)/shard_map/ppermute | solution.py:41
  38.4 19.8 %collective-permute-start.4 = (bf16[272,512]{1,0:T(8,128)(2,1)S(1)}, bf16[272,512]{1,0:T(8,128)(2,1)S(1)}, u32[]{:S(2)}, u32[]{:S(2)}) collective-permute-start(bf16[272,512]{1,0:T(8,128)(2,1)S(1)} %get-tuple-element.234), channel_id=1, source_target_pairs={{0,16},{8,24},{16,0},{24,8},{1,17},{9,25},{17,1},{25,9},{2,18},{10... | collective-permute-start | bytes 835592 | tf_op jit(solution)/shard_map/ppermute | solution.py:46
  40.2 22.5 %collective-permute-start.3 = (bf16[272,512]{1,0:T(8,128)(2,1)S(1)}, bf16[272,512]{1,0:T(8,128)(2,1)S(1)}, u32[]{:S(2)}, u32[]{:S(2)}) collective-permute-start(bf16[272,512]{1,0:T(8,128)(2,1)S(1)} %get-tuple-element.235), channel_id=1, source_target_pairs={{0,8},{8,0},{16,24},{24,16},{1,9},{9,1},{17,25},{25,17},{2,10},{10... | collective-permute-start | bytes 835592 | tf_op jit(solution)/shard_map/ppermute | solution.py:46
  74.1 23.8 %collective-permute-start.11 = (bf16[1024,512]{1,0:T(8,128)(2,1)S(1)}, bf16[1024,512]{1,0:T(8,128)(2,1)}, u32[]{:S(2)}, u32[]{:S(2)}) collective-permute-start(bf16[1024,512]{1,0:T(8,128)(2,1)S(1)} %bitcast.279), channel_id=1, source_target_pairs={{0,2},{1,3},{2,0},{3,1},{4,6},{5,7},{6,4},{7,5},{8,10},{9,11},{10,... | collective-permute-start | bytes 3145736 | tf_op jit(solution)/shard_map/ppermute | solution.py:41
  74.5 24.8 %collective-permute-start.10 = (bf16[1024,512]{1,0:T(8,128)(2,1)S(1)}, bf16[1024,512]{1,0:T(8,128)(2,1)}, u32[]{:S(2)}, u32[]{:S(2)}) collective-permute-start(bf16[1024,512]{1,0:T(8,128)(2,1)S(1)} %bitcast.280), channel_id=1, source_target_pairs={{0,1},{1,0},{2,3},{3,2},{4,5},{5,4},{6,7},{7,6},{8,9},{9,8},{10,11... | collective-permute-start | bytes 3145736 | tf_op jit(solution)/shard_map/ppermute | solution.py:41
  113.8 32.5 %collective-permute-start.21 = (bf16[512,1024]{1,0:T(8,128)(2,1)}, bf16[512,1024]{1,0:T(8,128)(2,1)}, u32[]{:S(2)}, u32[]{:S(2)}) collective-permute-start(bf16[512,1024]{1,0:T(8,128)(2,1)} %get-tuple-element.94), channel_id=1, source_target_pairs={{0,3},{1,2},{2,1},{3,0},{4,7},{5,6},{6,5},{7,4},{8,11},{9,10},{10,... | collective-permute-start | bytes 3145736 | tf_op jit(solution)/shard_map/ppermute | solution.py:41
  146.3 51.8 %collective-permute-start.22 = (bf16[512,2048]{1,0:T(8,128)(2,1)}, bf16[512,2048]{1,0:T(8,128)(2,1)}, u32[]{:S(2)}, u32[]{:S(2)}) collective-permute-start(bf16[512,2048]{1,0:T(8,128)(2,1)} %pad_maximum_fusion.4), channel_id=1, source_target_pairs={{0,1},{1,0},{2,3},{3,2},{4,5},{5,4},{6,7},{7,6},{8,9},{9,8},{10,11... | collective-permute-start | bytes 6291464 | tf_op jit(solution)/shard_map/ppermute | solution.py:41
  148.1 50.0 %collective-permute-start.23 = (bf16[512,2048]{1,0:T(8,128)(2,1)}, bf16[512,2048]{1,0:T(8,128)(2,1)}, u32[]{:S(2)}, u32[]{:S(2)}) collective-permute-start(bf16[512,2048]{1,0:T(8,128)(2,1)} %pad_maximum_fusion.5), channel_id=1, source_target_pairs={{0,2},{1,3},{2,0},{3,1},{4,6},{5,7},{6,4},{7,5},{8,10},{9,11},{10,... | collective-permute-start | bytes 6291464 | tf_op jit(solution)/shard_map/ppermute | solution.py:41
  171.1 27.0 %all-to-all-start = ((bf16[4,512,256]{2,1,0:T(8,128)(2,1)}), bf16[4,512,256]{2,1,0:T(8,128)(2,1)S(1)}, u32[]{:S(2)}, u32[]{:S(2)}) async-start(bf16[4,512,256]{2,1,0:T(8,128)(2,1)} %bitcast.22), calls=%async_computation | async-start | bytes 2097152 | tf_op jit(solution)/shard_map/all_to_all | solution.py:655
  174.6 421.2 %reduce-scatter.5.cloned.1.call-start = ((), (), s32[]{:S(2)}) async-start(), calls=%async_computation.6 | async-start | bytes 5242880 | tf_op jit(solution)/shard_map/reduce_scatter | solution.py:694
  200.6 26.6 %collective-permute-start.24 = (bf16[4,256,2048]{2,1,0:T(8,128)(2,1)S(1)}, bf16[4,256,2048]{2,1,0:T(8,128)(2,1)S(1)}, u32[]{:S(2)}, u32[]{:S(2)}) collective-permute-start(bf16[4,256,2048]{2,1,0:T(8,128)(2,1)S(1)} %convolution_convert_fusion.1), channel_id=1, source_target_pairs={{0,4},{4,0},{1,5},{5,1},{2,6},{6,2},{3,7},{7,3},{8,12},{12,8},{9,1... | collective-permute-start | bytes 12582920 | tf_op jit(solution)/shard_map/ppermute | solution.py:36
  200.7 26.5 %collective-permute-start.25 = (bf16[512,1024]{1,0:T(8,128)(2,1)S(1)}, bf16[512,1024]{1,0:T(8,128)(2,1)S(1)}, u32[]{:S(2)}, u32[]{:S(2)}) collective-permute-start(bf16[512,1024]{1,0:T(8,128)(2,1)S(1)} %copy-done.50), channel_id=1, source_target_pairs={{0,3},{1,2},{2,1},{3,0},{4,7},{5,6},{6,5},{7,4},{8,11},{9,10},{10,... | collective-permute-start | bytes 3145736 | tf_op jit(solution)/shard_map/ppermute | solution.py:41
  247.4 23.6 %collective-permute-start.29 = (bf16[256,2048]{1,0:T(8,128)(2,1)S(1)}, bf16[256,2048]{1,0:T(8,128)(2,1)S(1)}, u32[]{:S(2)}, u32[]{:S(2)}) collective-permute-start(bf16[256,2048]{1,0:T(8,128)(2,1)S(1)} %pad_maximum_fusion.16), channel_id=1, source_target_pairs={{0,2},{1,3},{2,0},{3,1},{4,6},{5,7},{6,4},{7,5},{8,10},{9,11},{10,... | collective-permute-start | bytes 3145736 | tf_op jit(solution)/shard_map/ppermute | solution.py:41
  248.0 23.4 %collective-permute-start.27 = (bf16[256,2048]{1,0:T(8,128)(2,1)S(1)}, bf16[256,2048]{1,0:T(8,128)(2,1)S(1)}, u32[]{:S(2)}, u32[]{:S(2)}) collective-permute-start(bf16[256,2048]{1,0:T(8,128)(2,1)S(1)} %pad_maximum_fusion.15), channel_id=1, source_target_pairs={{0,1},{1,0},{2,3},{3,2},{4,5},{5,4},{6,7},{7,6},{8,9},{9,8},{10,11... | collective-permute-start | bytes 3145736 | tf_op jit(solution)/shard_map/ppermute | solution.py:41
  276.7 22.8 %collective-permute-start.30 = (bf16[256,2048]{1,0:T(8,128)(2,1)}, bf16[256,2048]{1,0:T(8,128)(2,1)}, u32[]{:S(2)}, u32[]{:S(2)}) collective-permute-start(bf16[256,2048]{1,0:T(8,128)(2,1)} %get-tuple-element.183), channel_id=1, source_target_pairs={{0,1},{1,0},{2,3},{3,2},{4,5},{5,4},{6,7},{7,6},{8,9},{9,8},{10,11... | collective-permute-start | bytes 3145736 | tf_op jit(solution)/shard_map/ppermute | solution.py:41
  277.9 24.1 %collective-permute-start.31 = (bf16[256,2048]{1,0:T(8,128)(2,1)}, bf16[256,2048]{1,0:T(8,128)(2,1)}, u32[]{:S(2)}, u32[]{:S(2)}) collective-permute-start(bf16[256,2048]{1,0:T(8,128)(2,1)} %get-tuple-element.183), channel_id=1, source_target_pairs={{0,2},{1,3},{2,0},{3,1},{4,6},{5,7},{6,4},{7,5},{8,10},{9,11},{10,... | collective-permute-start | bytes 3145736 | tf_op jit(solution)/shard_map/ppermute | solution.py:41
  358.0 14.3 %collective-permute-start.39 = (bf16[128,2048]{1,0:T(8,128)(2,1)S(1)}, bf16[128,2048]{1,0:T(8,128)(2,1)S(1)}, u32[]{:S(2)}, u32[]{:S(2)}) collective-permute-start(bf16[128,2048]{1,0:T(8,128)(2,1)S(1)} %get-tuple-element.203), channel_id=1, source_target_pairs={{0,2},{1,3},{2,0},{3,1},{4,6},{5,7},{6,4},{7,5},{8,10},{9,11},{10,... | collective-permute-start | bytes 1572872 | tf_op jit(solution)/shard_map/ppermute | solution.py:41
  373.5 24.4 %collective-permute-start.42 = (bf16[256,2048]{1,0:T(8,128)(2,1)S(1)}, bf16[256,2048]{1,0:T(8,128)(2,1)S(1)}, u32[]{:S(2)}, u32[]{:S(2)}) collective-permute-start(bf16[256,2048]{1,0:T(8,128)(2,1)S(1)} %pad_maximum_fusion.19), channel_id=1, source_target_pairs={{0,2},{1,3},{2,0},{3,1},{4,6},{5,7},{6,4},{7,5},{8,10},{9,11},{10,... | collective-permute-start | bytes 3145736 | tf_op jit(solution)/shard_map/ppermute | solution.py:41
  374.9 24.1 %collective-permute-start.40 = (bf16[256,2048]{1,0:T(8,128)(2,1)S(1)}, bf16[256,2048]{1,0:T(8,128)(2,1)S(1)}, u32[]{:S(2)}, u32[]{:S(2)}) collective-permute-start(bf16[256,2048]{1,0:T(8,128)(2,1)S(1)} %pad_maximum_fusion.18), channel_id=1, source_target_pairs={{0,1},{1,0},{2,3},{3,2},{4,5},{5,4},{6,7},{7,6},{8,9},{9,8},{10,11... | collective-permute-start | bytes 3145736 | tf_op jit(solution)/shard_map/ppermute | solution.py:41
  403.7 23.2 %collective-permute-start.43 = (bf16[256,2048]{1,0:T(8,128)(2,1)S(1)}, bf16[256,2048]{1,0:T(8,128)(2,1)S(1)}, u32[]{:S(2)}, u32[]{:S(2)}) collective-permute-start(bf16[256,2048]{1,0:T(8,128)(2,1)S(1)} %get-tuple-element.162), channel_id=1, source_target_pairs={{0,1},{1,0},{2,3},{3,2},{4,5},{5,4},{6,7},{7,6},{8,9},{9,8},{10,11... | collective-permute-start | bytes 3145736 | tf_op jit(solution)/shard_map/ppermute | solution.py:41
  404.2 23.7 %collective-permute-start.44 = (bf16[256,2048]{1,0:T(8,128)(2,1)S(1)}, bf16[256,2048]{1,0:T(8,128)(2,1)S(1)}, u32[]{:S(2)}, u32[]{:S(2)}) collective-permute-start(bf16[256,2048]{1,0:T(8,128)(2,1)S(1)} %get-tuple-element.162), channel_id=1, source_target_pairs={{0,2},{1,3},{2,0},{3,1},{4,6},{5,7},{6,4},{7,5},{8,10},{9,11},{10,... | collective-permute-start | bytes 3145736 | tf_op jit(solution)/shard_map/ppermute | solution.py:41
  455.8 255.7 %reduce-scatter.7.cloned.1.call-start = ((), (), s32[]{:S(2)}) async-start(), calls=%async_computation.7 | async-start | bytes 5242880 | tf_op jit(solution)/shard_map/reduce_scatter | solution.py:694
  512.4 220.2 %reduce-scatter.9.cloned.1.call-start = ((), (), s32[]{:S(2)}) async-start(), calls=%async_computation.8 | async-start | bytes 5242880 | tf_op jit(solution)/shard_map/reduce_scatter | solution.py:694
  546.6 249.9 %all-gather.9.cloned.1.call-start = ((), (), s32[]{:S(2)}) async-start(), calls=%async_computation.10 | async-start | bytes 9437184 | tf_op jit(solution)/shard_map/all_gather | solution.py:705
  550.2 14.4 %collective-permute-start.52 = (bf16[128,2048]{1,0:T(8,128)(2,1)S(1)}, bf16[128,2048]{1,0:T(8,128)(2,1)S(1)}, u32[]{:S(2)}, u32[]{:S(2)}) collective-permute-start(bf16[128,2048]{1,0:T(8,128)(2,1)S(1)} %get-tuple-element.197), channel_id=1, source_target_pairs={{0,2},{1,3},{2,0},{3,1},{4,6},{5,7},{6,4},{7,5},{8,10},{9,11},{10,... | collective-permute-start | bytes 1572872 | tf_op jit(solution)/shard_map/ppermute | solution.py:41
  551.4 14.0 %collective-permute-start.54 = (bf16[128,2048]{1,0:T(8,128)(2,1)S(1)}, bf16[128,2048]{1,0:T(8,128)(2,1)S(1)}, u32[]{:S(2)}, u32[]{:S(2)}) collective-permute-start(bf16[128,2048]{1,0:T(8,128)(2,1)S(1)} %get-tuple-element.196), channel_id=1, source_target_pairs={{0,1},{1,0},{2,3},{3,2},{4,5},{5,4},{6,7},{7,6},{8,9},{9,8},{10,11... | collective-permute-start | bytes 1572872 | tf_op jit(solution)/shard_map/ppermute | solution.py:41
  567.3 24.6 %collective-permute-start.55 = (bf16[256,2048]{1,0:T(8,128)(2,1)S(1)}, bf16[256,2048]{1,0:T(8,128)(2,1)S(1)}, u32[]{:S(2)}, u32[]{:S(2)}) collective-permute-start(bf16[256,2048]{1,0:T(8,128)(2,1)S(1)} %pad_maximum_fusion.22), channel_id=1, source_target_pairs={{0,2},{1,3},{2,0},{3,1},{4,6},{5,7},{6,4},{7,5},{8,10},{9,11},{10,... | collective-permute-start | bytes 3145736 | tf_op jit(solution)/shard_map/ppermute | solution.py:41
  568.3 24.3 %collective-permute-start.53 = (bf16[256,2048]{1,0:T(8,128)(2,1)S(1)}, bf16[256,2048]{1,0:T(8,128)(2,1)S(1)}, u32[]{:S(2)}, u32[]{:S(2)}) collective-permute-start(bf16[256,2048]{1,0:T(8,128)(2,1)S(1)} %pad_maximum_fusion.21), channel_id=1, source_target_pairs={{0,1},{1,0},{2,3},{3,2},{4,5},{5,4},{6,7},{7,6},{8,9},{9,8},{10,11... | collective-permute-start | bytes 3145736 | tf_op jit(solution)/shard_map/ppermute | solution.py:41
  601.6 23.4 %collective-permute-start.56 = (bf16[256,2048]{1,0:T(8,128)(2,1)S(1)}, bf16[256,2048]{1,0:T(8,128)(2,1)S(1)}, u32[]{:S(2)}, u32[]{:S(2)}) collective-permute-start(bf16[256,2048]{1,0:T(8,128)(2,1)S(1)} %get-tuple-element.160), channel_id=1, source_target_pairs={{0,1},{1,0},{2,3},{3,2},{4,5},{5,4},{6,7},{7,6},{8,9},{9,8},{10,11... | collective-permute-start | bytes 3145736 | tf_op jit(solution)/shard_map/ppermute | solution.py:41
  602.9 24.2 %collective-permute-start.57 = (bf16[256,2048]{1,0:T(8,128)(2,1)S(1)}, bf16[256,2048]{1,0:T(8,128)(2,1)S(1)}, u32[]{:S(2)}, u32[]{:S(2)}) collective-permute-start(bf16[256,2048]{1,0:T(8,128)(2,1)S(1)} %get-tuple-element.160), channel_id=1, source_target_pairs={{0,2},{1,3},{2,0},{3,1},{4,6},{5,7},{6,4},{7,5},{8,10},{9,11},{10,... | collective-permute-start | bytes 3145736 | tf_op jit(solution)/shard_map/ppermute | solution.py:41
  628.9 15.6 %collective-permute-start.60 = (bf16[256,2048]{1,0:T(8,128)(2,1)}, bf16[256,2048]{1,0:T(8,128)(2,1)S(1)}, u32[]{:S(2)}, u32[]{:S(2)}) collective-permute-start(bf16[256,2048]{1,0:T(8,128)(2,1)} %copy-done.53), channel_id=1, source_target_pairs={{0,4},{4,0},{1,5},{5,1},{2,6},{6,2},{3,7},{7,3},{8,12},{12,8},{9,1... | collective-permute-start | bytes 3145736 | tf_op jit(solution)/shard_map/ppermute | solution.py:36
  628.9 16.7 %collective-permute-start.61 = (bf16[256,2048]{1,0:T(8,128)(2,1)}, bf16[256,2048]{1,0:T(8,128)(2,1)S(1)}, u32[]{:S(2)}, u32[]{:S(2)}) collective-permute-start(bf16[256,2048]{1,0:T(8,128)(2,1)} %copy-done.48), channel_id=1, source_target_pairs={{0,4},{4,0},{1,5},{5,1},{2,6},{6,2},{3,7},{7,3},{8,12},{12,8},{9,1... | collective-permute-start | bytes 3145736 | tf_op jit(solution)/shard_map/ppermute | solution.py:36
  629.4 17.2 %collective-permute-start.62 = (bf16[256,2048]{1,0:T(8,128)(2,1)S(1)}, bf16[256,2048]{1,0:T(8,128)(2,1)S(1)}, u32[]{:S(2)}, u32[]{:S(2)}) collective-permute-start(bf16[256,2048]{1,0:T(8,128)(2,1)S(1)} %collective-permute-done.57), channel_id=1, source_target_pairs={{0,4},{4,0},{1,5},{5,1},{2,6},{6,2},{3,7},{7,3},{8,12},{12,8},{9,1... | collective-permute-start | bytes 3145736 | tf_op jit(solution)/shard_map/ppermute | solution.py:36
  655.8 55.7 %all-to-all-start.1 = ((bf16[4,512,256]{2,1,0:T(8,128)(2,1)}), bf16[4,512,256]{2,1,0:T(8,128)(2,1)S(1)}, u32[]{:S(2)}, u32[]{:S(2)}) async-start(bf16[4,512,256]{2,1,0:T(8,128)(2,1)} %bitcast.317), calls=%async_computation.2 | async-start | bytes 2097152 | tf_op jit(solution)/shard_map/all_to_all | solution.py:741
  659.3 215.4 %reduce-scatter.11.cloned.1.call-start = ((), (), s32[]{:S(2)}) async-start(), calls=%async_computation.9 | async-start | bytes 5242880 | tf_op jit(solution)/shard_map/reduce_scatter | solution.py:694
  796.6 245.9 %all-gather.13.cloned.1.call-start = ((), (), s32[]{:S(2)}) async-start(), calls=%async_computation.12 | async-start | bytes 9437184 | tf_op jit(solution)/shard_map/all_gather | solution.py:705
  813.2 245.8 %all-gather.15.cloned.1.call-start = ((), (), s32[]{:S(2)}) async-start(), calls=%async_computation.13 | async-start | bytes 9437184 | tf_op jit(solution)/shard_map/all_gather | solution.py:705
  829.8 312.0 %all-gather.11.cloned.1.call-start = ((), (), s32[]{:S(2)}) async-start(), calls=%async_computation.11 | async-start | bytes 9437184 | tf_op jit(solution)/shard_map/all_gather | solution.py:705
  904.0 14.1 %collective-permute-start.68 = (bf16[512,512]{1,0:T(8,128)(2,1)S(1)}, bf16[512,512]{1,0:T(8,128)(2,1)S(1)}, u32[]{:S(2)}, u32[]{:S(2)}) collective-permute-start(bf16[512,512]{1,0:T(8,128)(2,1)S(1)} %get-tuple-element.191), channel_id=1, source_target_pairs={{0,2},{1,3},{2,0},{3,1},{4,6},{5,7},{6,4},{7,5},{8,10},{9,11},{10,... | collective-permute-start | bytes 1572872 | tf_op jit(solution)/shard_map/ppermute | solution.py:41
  920.9 44.3 %collective-permute-start.71 = (bf16[1024,512]{1,0:T(8,128)(2,1)}, bf16[1024,512]{1,0:T(8,128)(2,1)S(1)}, u32[]{:S(2)}, u32[]{:S(2)}) collective-permute-start(bf16[1024,512]{1,0:T(8,128)(2,1)} %pad_maximum_fusion.25), channel_id=1, source_target_pairs={{0,2},{1,3},{2,0},{3,1},{4,6},{5,7},{6,4},{7,5},{8,10},{9,11},{10,... | collective-permute-start | bytes 3145736 | tf_op jit(solution)/shard_map/ppermute | solution.py:41
  922.4 42.9 %collective-permute-start.69 = (bf16[1024,512]{1,0:T(8,128)(2,1)}, bf16[1024,512]{1,0:T(8,128)(2,1)}, u32[]{:S(2)}, u32[]{:S(2)}) collective-permute-start(bf16[1024,512]{1,0:T(8,128)(2,1)} %pad_maximum_fusion.24), channel_id=1, source_target_pairs={{0,1},{1,0},{2,3},{3,2},{4,5},{5,4},{6,7},{7,6},{8,9},{9,8},{10,11... | collective-permute-start | bytes 3145736 | tf_op jit(solution)/shard_map/ppermute | solution.py:41
  925.0 22.3 %collective-permute-start.92 = (f32[33,128]{1,0:T(8,128)S(1)}, f32[33,128]{1,0:T(8,128)S(1)}, u32[]{:S(2)}, u32[]{:S(2)}) collective-permute-start(f32[33,128]{1,0:T(8,128)S(1)} %fusion.127), channel_id=1, source_target_pairs={{0,1},{1,0},{2,3},{3,2},{4,5},{5,4},{6,7},{7,6},{8,9},{9,8},{10,11... | collective-permute-start | bytes 50696 | tf_op jit(solution)/shard_map/ppermute | solution.py:41
  967.7 16.0 %collective-permute-start.74 = (bf16[256,512]{1,0:T(8,128)(2,1)S(1)}, bf16[256,512]{1,0:T(8,128)(2,1)S(1)}, u32[]{:S(2)}, u32[]{:S(2)}) collective-permute-start(bf16[256,512]{1,0:T(8,128)(2,1)S(1)} %get-tuple-element.265), channel_id=1, source_target_pairs={{0,24},{8,16},{16,8},{24,0},{1,25},{9,17},{17,9},{25,1},{2,26},{10... | collective-permute-start | bytes 786440 | tf_op jit(solution)/shard_map/ppermute | solution.py:46
  969.2 48.7 %collective-permute-start.73 = (bf16[256,512]{1,0:T(8,128)(2,1)S(1)}, bf16[256,512]{1,0:T(8,128)(2,1)S(1)}, u32[]{:S(2)}, u32[]{:S(2)}) collective-permute-start(bf16[256,512]{1,0:T(8,128)(2,1)S(1)} %get-tuple-element.266), channel_id=1, source_target_pairs={{0,16},{8,24},{16,0},{24,8},{1,17},{9,25},{17,1},{25,9},{2,18},{10... | collective-permute-start | bytes 786440 | tf_op jit(solution)/shard_map/ppermute | solution.py:46
  969.3 48.6 %collective-permute-start.72 = (bf16[256,512]{1,0:T(8,128)(2,1)S(1)}, bf16[256,512]{1,0:T(8,128)(2,1)S(1)}, u32[]{:S(2)}, u32[]{:S(2)}) collective-permute-start(bf16[256,512]{1,0:T(8,128)(2,1)S(1)} %get-tuple-element.267), channel_id=1, source_target_pairs={{0,8},{8,0},{16,24},{24,16},{1,9},{9,1},{17,25},{25,17},{2,10},{10... | collective-permute-start | bytes 786440 | tf_op jit(solution)/shard_map/ppermute | solution.py:46
  972.9 48.8 %collective-permute-start.90 = (f32[2,256]{1,0:T(2,128)S(1)}, f32[2,256]{1,0:T(2,128)S(1)}, u32[]{:S(2)}, u32[]{:S(2)}) collective-permute-start(f32[2,256]{1,0:T(2,128)S(1)} %add_add_fusion.1), channel_id=1, source_target_pairs={{0,4},{4,0},{1,5},{5,1},{2,6},{6,2},{3,7},{7,3},{8,12},{12,8},{9,1... | collective-permute-start | bytes 6152 | tf_op jit(solution)/shard_map/ppermute | solution.py:36
  (129 other events, 1487.6 us)
Sparse Core Ops, SparseCore 0:
  455.9 74.9 reduce-scatter.4
  533.9 77.2 reduce-scatter.6
  614.1 93.7 reduce-scatter.8
  709.4 87.0 all-gather.8
  799.4 75.2 reduce-scatter.10
  876.7 84.2 all-gather.12
  962.7 96.2 all-gather.14
  1060.6 81.0 all-gather.10

commit v4 on v3

--- a/solution.py
+++ b/solution.py
@@ -662,9 +662,10 @@
     def blocks_of(values):
         return values.reshape(shards, rows, values.shape[-1])
 
-    branch_attn, up_last = reduce_plane(
-        blocks_of(mm(attended[half:], out_block)), blocks_of(mm(attended[:half], out_block)), up_last
-    )
+    branch_attn, _ = reduce_plane(
+        blocks_of(mm(attended[half:], out_block)), blocks_of(mm(attended[:half], out_block)), ()
+    )
+    branch_attn, up_last = tie((branch_attn, up_last))
     feed_blocks.append(jnp.concatenate([gate_last, up_last], 1))
     whole_feed = jnp.zeros((width, 2 * feed_cols), BF)
     for k in range(shards):

time: 1170 us -> 1170 us (level)
  transfers between devices with their start and end apart: 107 -> 107, of which waited for: 70 -> 71; matrix products, arithmetic and copies ran while one was open for 17% -> 17% of each run, Pallas kernels for 10% -> 10%
where the time goes in v4:
time: 1170 us; the launch traced here: 1160 us
  waiting for transfers between devices  617 us (53%)
  matrix products  140 us (12%)
  Pallas kernels  125 us (11%)
  starting transfers between devices  109 us (9%)
  local copies, waits for them, and re-layouts  80.6 us (7%)
  other arithmetic  71.8 us (6%)
  between operations  17.1 us (1%)
    ppermute x60, waiting for transfers between devices, send_shard(): return lax.ppermute(values, 'shard', [(i, i ^ k) for i in range(count)])  323 us
    all_gather x4, waiting for transfers between devices, copies(): whole = lax.all_gather(values, ('z', 'core'), axis=0)  108 us
    dot_general x14, matrix products, contract_cols(): lax.dot_general(left, right, (((1,), (1,)), ((), ())), preferred_element_...  79.3 us
    ppermute x60, starting transfers between devices, send_shard(): return lax.ppermute(values, 'shard', [(i, i ^ k) for i in range(count)])  67.5 us
    ppermute x12, waiting for transfers between devices, send_plane(): return lax.ppermute(values, 'z', [(i, i ^ k) for i in range(count)])  54.6 us
    reduce_scatter x4, waiting for transfers between devices, plane_share(): share = lax.psum_scatter(flat, 'z', scatter_dimension=0, tiled=True)  44.9 us
    unnamed x175, local copies, waits for them, and re-layouts  44.6 us
    all_to_all x1, waiting for transfers between devices, per_device(): lax.all_to_all(grad_mixed.reshape(shards, 2 * rows, head_cols), 'z', 0, 0...  44.5 us
  transfers between devices with their start and end apart: 107, of which 71 were waited for; matrix products, arithmetic and copies ran while one was open for 17% of the time, Pallas kernels for 10%

profile of v4, /device:TPU:0, one launch (start us, length us, event | category | flops | bytes accessed | tf_op | source)
XLA Modules:
  0.0 1161.2 jit_solution(7694341656430891556)
XLA Ops:
  40.2 12.3 %collective-permute-start.3 = (bf16[272,512]{1,0:T(8,128)(2,1)S(1)}, bf16[272,512]{1,0:T(8,128)(2,1)S(1)}, u32[]{:S(2)}, u32[]{:S(2)}) collective-permute-start(bf16[272,512]{1,0:T(8,128)(2,1)S(1)} %get-tuple-element.235), channel_id=1, source_target_pairs={{0,8},{8,0},{16,24},{24,16},{1,9},{9,1},{17,25},{25,17},{2,10},{10... | collective-permute-start | bytes 835592 | tf_op jit(solution)/shard_map/ppermute | solution.py:46
  62.9 10.2 collective-permute-done.7.refs_10_
  83.5 14.5 %collective-permute-done.11.refs_2_ = bf16[1024,512]{1,0:T(8,128)(2,1)} collective-permute-done((bf16[1024,512]{1,0:T(8,128)(2,1)S(1)}, bf16[1024,512]{1,0:T(8,128)(2,1)}, u32[]{:S(2)}, u32[]{:S(2)}) %collective-permute-start.11) | collective-permute-done | bytes 1048608 | tf_op jit(solution)/shard_map/ppermute | solution.py:41
  124.9 12.3 %project.1 = (f32[2048,768]{1,0:T(8,128)}, f32[2,8,256]{2,1,0:T(8,128)S(1)}) custom-call(bf16[1024,512]{1,0:T(8,128)(2,1)S(1)} %bitcast.281, bf16[1024,512]{1,0:T(8,128)(2,1)} %collective-permute-done.10.refs_1_, bf16[1024,512]{1,0:T(8,128)(2,1)} %collective-permute-done.11.refs_2_, bf16[1024,512]{1,0:T(8,128)(2,1)} %pad_maximum_fusion.14.refs_3_, ...), custom_call_target="tpu_custom_call" | custom-call | tf_op jit(solution)/shard_map/project/pallas_call | solution.py:217
  150.8 19.8 %attend_forward.1 = (bf16[2048,256]{1,0:T(8,128)(2,1)}, bf16[2048,256]{1,0:T(8,128)(2,1)}, bf16[2048,256]{1,0:T(8,128)(2,1)}, bf16[2048,256]{1,0:T(8,128)(2,1)}, f32[2,1,2048]{2,1,0:T(1,128)S(1)}) custom-call(s32[10]{0:T(128)S(1)} %pad_add_fusion.flags, f32[2048,768]{1,0:T(8,128)} %get-tuple-element.93.raw_q.raw_k.raw_v.raw, ...), custom_call_target="tpu_custom_call" | custom-call | tf_op jit(solution)/shard_map/attend_forward/pallas_call | solution.py:352
  175.0 23.2 %all-to-all-done = bf16[4,512,256]{2,1,0:T(8,128)(2,1)S(1)} async-done(((bf16[4,512,256]{2,1,0:T(8,128)(2,1)}), bf16[4,512,256]{2,1,0:T(8,128)(2,1)S(1)}, u32[]{:S(2)}, u32[]{:S(2)}) %all-to-all-start) | async-done | bytes 1048608 | tf_op jit(solution)/shard_map/all_to_all | solution.py:655
  212.9 11.6 %collective-permute-done.25 = bf16[128,2048]{1,0:T(8,128)(2,1)} collective-permute-done((bf16[128,2048]{1,0:T(8,128)(2,1)}, bf16[128,2048]{1,0:T(8,128)(2,1)}, u32[]{:S(2)}, u32[]{:S(2)}) %collective-permute-start.25) | collective-permute-done | bytes 524320 | tf_op jit(solution)/shard_map/ppermute | solution.py:41
  234.2 19.1 %collective-permute-done.28 = bf16[256,2048]{1,0:T(8,128)(2,1)S(1)} collective-permute-done((bf16[256,2048]{1,0:T(8,128)(2,1)S(1)}, bf16[256,2048]{1,0:T(8,128)(2,1)S(1)}, u32[]{:S(2)}, u32[]{:S(2)}) %collective-permute-start.28) | collective-permute-done | bytes 1048608 | tf_op jit(solution)/shard_map/ppermute | solution.py:41
  257.2 19.0 %collective-permute-done.29 = bf16[512,1024]{1,0:T(8,128)(2,1)S(1)} collective-permute-done((bf16[512,1024]{1,0:T(8,128)(2,1)S(1)}, bf16[512,1024]{1,0:T(8,128)(2,1)S(1)}, u32[]{:S(2)}, u32[]{:S(2)}) %collective-permute-start.29) | collective-permute-done | bytes 1048608 | tf_op jit(solution)/shard_map/ppermute | solution.py:41
  286.5 15.4 %collective-permute-done.30 = bf16[256,2048]{1,0:T(8,128)(2,1)} collective-permute-done((bf16[256,2048]{1,0:T(8,128)(2,1)}, bf16[256,2048]{1,0:T(8,128)(2,1)}, u32[]{:S(2)}, u32[]{:S(2)}) %collective-permute-start.30) | collective-permute-done | bytes 1048608 | tf_op jit(solution)/shard_map/ppermute | solution.py:41
  318.5 11.7 %fusion.8 = f32[2048,1024]{1,0:T(8,128)} fusion(bf16[2048,2048]{1,0:T(8,128)(2,1)S(1)} %constant_dynamic-update-slice_fusion.tokens, bf16[2048,2048]{1,0:T(8,128)(2,1)S(1)} %maximum_dynamic-update-slice_fusion), kind=kOutput, calls=%fused_computation.22 | convolution fusion | flops 8589934592 | bytes 20971520 | tf_op jit(solution)/shard_map/dot_general | solution.py:24
  330.3 14.6 %multiply_convert_fusion.2 = (bf16[2048,1024]{1,0:T(8,128)(2,1)}, f32[2048,1024]{1,0:T(8,128)}) fusion(f32[2048,1024]{1,0:T(8,128)} %fusion.8, bf16[2048,2048]{1,0:T(8,128)(2,1)S(1)} %constant_dynamic-update-slice_fusion.tokens, bf16[2048,2048]{1,0:T(8,128)(2,1)S(1)} %maximum_dynamic-update-slice_fusion), kind=kOutput, calls=%fused_computation.4 | convolution fusion | flops 8602517504 | bytes 33554432 | tf_op jit(solution)/shard_map/dot_general | solution.py:24
  344.8 7.5 convolution_convert_fusion.3
  352.5 7.3 convolution_convert_fusion.4
  362.2 12.8 %collective-permute-done.39 = bf16[128,2048]{1,0:T(8,128)(2,1)S(1)} collective-permute-done((bf16[128,2048]{1,0:T(8,128)(2,1)S(1)}, bf16[128,2048]{1,0:T(8,128)(2,1)S(1)}, u32[]{:S(2)}, u32[]{:S(2)}) %collective-permute-start.39) | collective-permute-done | bytes 524320 | tf_op jit(solution)/shard_map/ppermute | solution.py:41
  378.4 22.4 %collective-permute-done.42 = bf16[256,2048]{1,0:T(8,128)(2,1)S(1)} collective-permute-done((bf16[256,2048]{1,0:T(8,128)(2,1)S(1)}, bf16[256,2048]{1,0:T(8,128)(2,1)S(1)}, u32[]{:S(2)}, u32[]{:S(2)}) %collective-permute-start.42) | collective-permute-done | bytes 1048608 | tf_op jit(solution)/shard_map/ppermute | solution.py:41
  407.9 21.7 %collective-permute-done.43 = bf16[256,2048]{1,0:T(8,128)(2,1)S(1)} collective-permute-done((bf16[256,2048]{1,0:T(8,128)(2,1)S(1)}, bf16[256,2048]{1,0:T(8,128)(2,1)S(1)}, u32[]{:S(2)}, u32[]{:S(2)}) %collective-permute-start.43) | collective-permute-done | bytes 1048608 | tf_op jit(solution)/shard_map/ppermute | solution.py:41
  433.2 8.1 collective-permute-done.45
  447.7 10.9 convolution_convert_fusion
  458.7 22.1 %multiply_convert_fusion = (bf16[2048,1024]{1,0:T(8,128)(2,1)S(1)}, bf16[2048,1024]{1,0:T(8,128)(2,1)}) fusion(f32[2048,1024]{1,0:T(8,128)} %fusion.8, f32[2048,1024]{1,0:T(8,128)} %get-tuple-element.308, bf16[2048,2048]{1,0:T(8,128)(2,1)} %copy-done.57, bf16[2048,2048]{1,0:T(8,128)(2,1)} %param.25, s32[]{:T(128)S(6)} %select_n.247), kind=kOutput, calls=%fused_computation.2 | convolution fusion | flops 8617197568 | bytes 37748740 | tf_op jit(solution)/shard_map/dot_general | solution.py:32
  480.8 12.3 %fusion.6 = f32[1024,2048]{1,0:T(8,128)} fusion(bf16[2048,2048]{1,0:T(8,128)(2,1)} %copy-done.40, bf16[2048,1024]{1,0:T(8,128)(2,1)} %get-tuple-element.120.grads), kind=kOutput, calls=%fused_computation.20 | convolution fusion | flops 4294967296 | bytes 14680064 | tf_op jit(solution)/shard_map/dot_general | solution.py:32
  493.1 8.4 add_convert_fusion.1
  501.7 11.5 weight_terms.2
  515.3 11.0 fusion
  526.3 9.8 add_convert_fusion
  536.1 11.3 weight_terms.3
  555.2 12.2 %collective-permute-done.52 = bf16[128,2048]{1,0:T(8,128)(2,1)S(1)} collective-permute-done((bf16[128,2048]{1,0:T(8,128)(2,1)S(1)}, bf16[128,2048]{1,0:T(8,128)(2,1)S(1)}, u32[]{:S(2)}, u32[]{:S(2)}) %collective-permute-start.52) | collective-permute-done | bytes 524320 | tf_op jit(solution)/shard_map/ppermute | solution.py:41
  572.2 22.2 %collective-permute-done.55 = bf16[256,2048]{1,0:T(8,128)(2,1)S(1)} collective-permute-done((bf16[256,2048]{1,0:T(8,128)(2,1)S(1)}, bf16[256,2048]{1,0:T(8,128)(2,1)S(1)}, u32[]{:S(2)}, u32[]{:S(2)}) %collective-permute-start.55) | collective-permute-done | bytes 1048608 | tf_op jit(solution)/shard_map/ppermute | solution.py:41
  606.5 21.5 %collective-permute-done.56 = bf16[256,2048]{1,0:T(8,128)(2,1)S(1)} collective-permute-done((bf16[256,2048]{1,0:T(8,128)(2,1)S(1)}, bf16[256,2048]{1,0:T(8,128)(2,1)S(1)}, u32[]{:S(2)}, u32[]{:S(2)}) %collective-permute-start.56) | collective-permute-done | bytes 1048608 | tf_op jit(solution)/shard_map/ppermute | solution.py:41
  662.2 6.2 convolution_convert_fusion.6
  669.7 44.5 %all-to-all-done.1 = bf16[4,512,256]{2,1,0:T(8,128)(2,1)S(1)} async-done(((bf16[4,512,256]{2,1,0:T(8,128)(2,1)}), bf16[4,512,256]{2,1,0:T(8,128)(2,1)S(1)}, u32[]{:S(2)}, u32[]{:S(2)}) %all-to-all-start.1) | async-done | bytes 1048608 | tf_op jit(solution)/shard_map/all_to_all | solution.py:742
  715.2 20.1 %attend_backward.1 = (f32[2048,256]{1,0:T(8,128)}, f32[2048,256]{1,0:T(8,128)}, bf16[2048,256]{1,0:T(8,128)(2,1)}, f32[2,2,8,256]{3,2,1,0:T(8,128)}, f32[2,2,128]{2,1,0:T(2,128)}) custom-call(s32[10]{0:T(128)} %copy-done.26, bf16[2048,256]{1,0:T(8,128)(2,1)} %get-tuple-element.128.queries, bf16[2048,256]{1,0:T(8,128)(2,1)} %get-tuple-element.129.keys, ...), custom_call_target="tpu_custom_call" | custom-call | tf_op jit(solution)/shard_map/attend_backward/pallas_call | solution.py:443
  745.8 8.8 finish.1.refs_8_
  754.6 12.8 %input_terms.1 = bf16[4,4,3,128,256]{4,3,2,1,0:T(8,128)(2,1)} custom-call(bf16[1024,512]{1,0:T(8,128)(2,1)} %bitcast.282, bf16[1024,512]{1,0:T(8,128)(2,1)} %collective-permute-done.10.refs_1_, bf16[1024,512]{1,0:T(8,128)(2,1)} %collective-permute-done.11.refs_2_, bf16[1024,512]{1,0:T(8,128)(2,1)} %pad_maximum_fusion.14.refs_3_, ...), custom_call_target="tpu_custom_call" | custom-call | tf_op jit(solution)/shard_map/input_terms/pallas_call | solution.py:248
  771.6 27.7 %all-gather.9.cloned.1.call-done = bf16[2048,2048]{1,0:T(8,128)(2,1)} async-done(((bf16[256,2048]{1,0:T(8,128)(2,1)}), bf16[2048,2048]{1,0:T(8,128)(2,1)}) %all-gather.9.cloned.1.call-update) | async-done | bytes 8388624 | tf_op jit(solution)/shard_map/all_gather | solution.py:706
  803.1 6.6 collective-permute-done.83
  819.8 6.6 collective-permute-done.86
  832.6 44.9 %reduce-scatter.11.cloned.1.call-done = bf16[2048,256]{1,0:T(8,128)(2,1)} async-done(((bf16[8192,256]{1,0:T(8,128)(2,1)}), bf16[2048,256]{1,0:T(8,128)(2,1)}) %reduce-scatter.11.cloned.1.call-update) | async-done | bytes 1048592 | tf_op jit(solution)/shard_map/reduce_scatter | solution.py:695
  912.3 8.6 collective-permute-done.68
  928.4 21.7 %collective-permute-done.92 = f32[33,128]{1,0:T(8,128)S(1)} collective-permute-done((f32[33,128]{1,0:T(8,128)S(1)}, f32[33,128]{1,0:T(8,128)S(1)}, u32[]{:S(2)}, u32[]{:S(2)}) %collective-permute-start.92) | collective-permute-done | bytes 16928 | tf_op jit(solution)/shard_map/ppermute | solution.py:41
  975.7 10.8 collective-permute-done.74
  986.6 34.1 %collective-permute-done.73 = bf16[256,512]{1,0:T(8,128)(2,1)S(1)} collective-permute-done((bf16[256,512]{1,0:T(8,128)(2,1)S(1)}, bf16[256,512]{1,0:T(8,128)(2,1)S(1)}, u32[]{:S(2)}, u32[]{:S(2)}) %collective-permute-start.73) | collective-permute-done | bytes 262176 | tf_op jit(solution)/shard_map/ppermute | solution.py:46
  1035.0 10.3 rows_out.1
  1048.6 6.2 columns_out.2
  1054.8 6.9 all-gather.15.cloned.1.call-done
  1065.2 6.4 columns_out.3
  1071.6 73.0 %all-gather.11.cloned.1.call-done = bf16[16384,256]{1,0:T(8,128)(2,1)} async-done(((bf16[2048,256]{1,0:T(8,128)(2,1)}), bf16[16384,256]{1,0:T(8,128)(2,1)}) %all-gather.11.cloned.1.call-update) | async-done | bytes 8388624 | tf_op jit(solution)/shard_map/all_gather | solution.py:706
  1147.9 6.0 attention_out.1
  (538 shorter events, 365.2 us)
Async XLA Ops:
  34.9 28.0 %collective-permute-start.6 = (bf16[528,768]{1,0:T(8,128)(2,1)S(1)}, bf16[528,768]{1,0:T(8,128)(2,1)S(1)}, u32[]{:S(2)}, u32[]{:S(2)}) collective-permute-start(bf16[528,768]{1,0:T(8,128)(2,1)S(1)} %get-tuple-element.277), channel_id=1, source_target_pairs={{0,1},{1,0},{2,3},{3,2},{4,5},{5,4},{6,7},{7,6},{8,9},{9,8},{10,11... | collective-permute-start | bytes 2433032 | tf_op jit(solution)/shard_map/ppermute | solution.py:41
  36.4 36.7 %collective-permute-start.7 = (bf16[528,768]{1,0:T(8,128)(2,1)S(1)}, bf16[528,768]{1,0:T(8,128)(2,1)S(1)}, u32[]{:S(2)}, u32[]{:S(2)}) collective-permute-start(bf16[528,768]{1,0:T(8,128)(2,1)S(1)} %get-tuple-element.278), channel_id=1, source_target_pairs={{0,2},{1,3},{2,0},{3,1},{4,6},{5,7},{6,4},{7,5},{8,10},{9,11},{10,... | collective-permute-start | bytes 2433032 | tf_op jit(solution)/shard_map/ppermute | solution.py:41
  37.1 36.0 %collective-permute-start.8 = (bf16[528,768]{1,0:T(8,128)(2,1)S(1)}, bf16[528,768]{1,0:T(8,128)(2,1)S(1)}, u32[]{:S(2)}, u32[]{:S(2)}) collective-permute-start(bf16[528,768]{1,0:T(8,128)(2,1)S(1)} %get-tuple-element.276), channel_id=1, source_target_pairs={{0,3},{1,2},{2,1},{3,0},{4,7},{5,6},{6,5},{7,4},{8,11},{9,10},{10,... | collective-permute-start | bytes 2433032 | tf_op jit(solution)/shard_map/ppermute | solution.py:41
  38.4 19.8 %collective-permute-start.4 = (bf16[272,512]{1,0:T(8,128)(2,1)S(1)}, bf16[272,512]{1,0:T(8,128)(2,1)S(1)}, u32[]{:S(2)}, u32[]{:S(2)}) collective-permute-start(bf16[272,512]{1,0:T(8,128)(2,1)S(1)} %get-tuple-element.234), channel_id=1, source_target_pairs={{0,16},{8,24},{16,0},{24,8},{1,17},{9,25},{17,1},{25,9},{2,18},{10... | collective-permute-start | bytes 835592 | tf_op jit(solution)/shard_map/ppermute | solution.py:46
  40.2 22.5 %collective-permute-start.3 = (bf16[272,512]{1,0:T(8,128)(2,1)S(1)}, bf16[272,512]{1,0:T(8,128)(2,1)S(1)}, u32[]{:S(2)}, u32[]{:S(2)}) collective-permute-start(bf16[272,512]{1,0:T(8,128)(2,1)S(1)} %get-tuple-element.235), channel_id=1, source_target_pairs={{0,8},{8,0},{16,24},{24,16},{1,9},{9,1},{17,25},{25,17},{2,10},{10... | collective-permute-start | bytes 835592 | tf_op jit(solution)/shard_map/ppermute | solution.py:46
  74.1 23.8 %collective-permute-start.11 = (bf16[1024,512]{1,0:T(8,128)(2,1)S(1)}, bf16[1024,512]{1,0:T(8,128)(2,1)}, u32[]{:S(2)}, u32[]{:S(2)}) collective-permute-start(bf16[1024,512]{1,0:T(8,128)(2,1)S(1)} %bitcast.278), channel_id=1, source_target_pairs={{0,2},{1,3},{2,0},{3,1},{4,6},{5,7},{6,4},{7,5},{8,10},{9,11},{10,... | collective-permute-start | bytes 3145736 | tf_op jit(solution)/shard_map/ppermute | solution.py:41
  74.5 24.8 %collective-permute-start.10 = (bf16[1024,512]{1,0:T(8,128)(2,1)S(1)}, bf16[1024,512]{1,0:T(8,128)(2,1)}, u32[]{:S(2)}, u32[]{:S(2)}) collective-permute-start(bf16[1024,512]{1,0:T(8,128)(2,1)S(1)} %bitcast.279), channel_id=1, source_target_pairs={{0,1},{1,0},{2,3},{3,2},{4,5},{5,4},{6,7},{7,6},{8,9},{9,8},{10,11... | collective-permute-start | bytes 3145736 | tf_op jit(solution)/shard_map/ppermute | solution.py:41
  113.9 32.5 %collective-permute-start.21 = (bf16[512,1024]{1,0:T(8,128)(2,1)}, bf16[512,1024]{1,0:T(8,128)(2,1)}, u32[]{:S(2)}, u32[]{:S(2)}) collective-permute-start(bf16[512,1024]{1,0:T(8,128)(2,1)} %get-tuple-element.95), channel_id=1, source_target_pairs={{0,3},{1,2},{2,1},{3,0},{4,7},{5,6},{6,5},{7,4},{8,11},{9,10},{10,... | collective-permute-start | bytes 3145736 | tf_op jit(solution)/shard_map/ppermute | solution.py:41
  146.3 51.8 %collective-permute-start.22 = (bf16[512,2048]{1,0:T(8,128)(2,1)}, bf16[512,2048]{1,0:T(8,128)(2,1)}, u32[]{:S(2)}, u32[]{:S(2)}) collective-permute-start(bf16[512,2048]{1,0:T(8,128)(2,1)} %pad_maximum_fusion.4), channel_id=1, source_target_pairs={{0,1},{1,0},{2,3},{3,2},{4,5},{5,4},{6,7},{7,6},{8,9},{9,8},{10,11... | collective-permute-start | bytes 6291464 | tf_op jit(solution)/shard_map/ppermute | solution.py:41
  148.1 50.0 %collective-permute-start.23 = (bf16[512,2048]{1,0:T(8,128)(2,1)}, bf16[512,2048]{1,0:T(8,128)(2,1)}, u32[]{:S(2)}, u32[]{:S(2)}) collective-permute-start(bf16[512,2048]{1,0:T(8,128)(2,1)} %pad_maximum_fusion.5), channel_id=1, source_target_pairs={{0,2},{1,3},{2,0},{3,1},{4,6},{5,7},{6,4},{7,5},{8,10},{9,11},{10,... | collective-permute-start | bytes 6291464 | tf_op jit(solution)/shard_map/ppermute | solution.py:41
  171.2 27.0 %all-to-all-start = ((bf16[4,512,256]{2,1,0:T(8,128)(2,1)}), bf16[4,512,256]{2,1,0:T(8,128)(2,1)S(1)}, u32[]{:S(2)}, u32[]{:S(2)}) async-start(bf16[4,512,256]{2,1,0:T(8,128)(2,1)} %bitcast.22), calls=%async_computation | async-start | bytes 2097152 | tf_op jit(solution)/shard_map/all_to_all | solution.py:655
  174.7 424.0 %reduce-scatter.5.cloned.1.call-start = ((), (), s32[]{:S(2)}) async-start(), calls=%async_computation.6 | async-start | bytes 5242880 | tf_op jit(solution)/shard_map/reduce_scatter | solution.py:695
  210.2 14.3 %collective-permute-start.25 = (bf16[128,2048]{1,0:T(8,128)(2,1)}, bf16[128,2048]{1,0:T(8,128)(2,1)}, u32[]{:S(2)}, u32[]{:S(2)}) collective-permute-start(bf16[128,2048]{1,0:T(8,128)(2,1)} %get-tuple-element.209), channel_id=1, source_target_pairs={{0,2},{1,3},{2,0},{3,1},{4,6},{5,7},{6,4},{7,5},{8,10},{9,11},{10,... | collective-permute-start | bytes 1572872 | tf_op jit(solution)/shard_map/ppermute | solution.py:41
  228.3 25.1 %collective-permute-start.28 = (bf16[256,2048]{1,0:T(8,128)(2,1)S(1)}, bf16[256,2048]{1,0:T(8,128)(2,1)S(1)}, u32[]{:S(2)}, u32[]{:S(2)}) collective-permute-start(bf16[256,2048]{1,0:T(8,128)(2,1)S(1)} %pad_maximum_fusion.16), channel_id=1, source_target_pairs={{0,2},{1,3},{2,0},{3,1},{4,6},{5,7},{6,4},{7,5},{8,10},{9,11},{10,... | collective-permute-start | bytes 3145736 | tf_op jit(solution)/shard_map/ppermute | solution.py:41
  228.8 26.2 %collective-permute-start.26 = (bf16[256,2048]{1,0:T(8,128)(2,1)S(1)}, bf16[256,2048]{1,0:T(8,128)(2,1)S(1)}, u32[]{:S(2)}, u32[]{:S(2)}) collective-permute-start(bf16[256,2048]{1,0:T(8,128)(2,1)S(1)} %pad_maximum_fusion.15), channel_id=1, source_target_pairs={{0,1},{1,0},{2,3},{3,2},{4,5},{5,4},{6,7},{7,6},{8,9},{9,8},{10,11... | collective-permute-start | bytes 3145736 | tf_op jit(solution)/shard_map/ppermute | solution.py:41
  232.4 43.8 %collective-permute-start.29 = (bf16[512,1024]{1,0:T(8,128)(2,1)S(1)}, bf16[512,1024]{1,0:T(8,128)(2,1)S(1)}, u32[]{:S(2)}, u32[]{:S(2)}) collective-permute-start(bf16[512,1024]{1,0:T(8,128)(2,1)S(1)} %copy-done.50), channel_id=1, source_target_pairs={{0,3},{1,2},{2,1},{3,0},{4,7},{5,6},{6,5},{7,4},{8,11},{9,10},{10,... | collective-permute-start | bytes 3145736 | tf_op jit(solution)/shard_map/ppermute | solution.py:41
  278.8 23.2 %collective-permute-start.30 = (bf16[256,2048]{1,0:T(8,128)(2,1)}, bf16[256,2048]{1,0:T(8,128)(2,1)}, u32[]{:S(2)}, u32[]{:S(2)}) collective-permute-start(bf16[256,2048]{1,0:T(8,128)(2,1)} %get-tuple-element.185), channel_id=1, source_target_pairs={{0,1},{1,0},{2,3},{3,2},{4,5},{5,4},{6,7},{7,6},{8,9},{9,8},{10,11... | collective-permute-start | bytes 3145736 | tf_op jit(solution)/shard_map/ppermute | solution.py:41
  279.2 24.7 %collective-permute-start.31 = (bf16[256,2048]{1,0:T(8,128)(2,1)}, bf16[256,2048]{1,0:T(8,128)(2,1)}, u32[]{:S(2)}, u32[]{:S(2)}) collective-permute-start(bf16[256,2048]{1,0:T(8,128)(2,1)} %get-tuple-element.185), channel_id=1, source_target_pairs={{0,2},{1,3},{2,0},{3,1},{4,6},{5,7},{6,4},{7,5},{8,10},{9,11},{10,... | collective-permute-start | bytes 3145736 | tf_op jit(solution)/shard_map/ppermute | solution.py:41
  286.5 29.4 %collective-permute-start.34 = (bf16[256,2048]{1,0:T(8,128)(2,1)}, bf16[256,2048]{1,0:T(8,128)(2,1)S(1)}, u32[]{:S(2)}, u32[]{:S(2)}) collective-permute-start(bf16[256,2048]{1,0:T(8,128)(2,1)} %get-tuple-element.185), channel_id=1, source_target_pairs={{0,4},{4,0},{1,5},{5,1},{2,6},{6,2},{3,7},{7,3},{8,12},{12,8},{9,1... | collective-permute-start | bytes 3145736 | tf_op jit(solution)/shard_map/ppermute | solution.py:36
  360.7 14.3 %collective-permute-start.39 = (bf16[128,2048]{1,0:T(8,128)(2,1)S(1)}, bf16[128,2048]{1,0:T(8,128)(2,1)S(1)}, u32[]{:S(2)}, u32[]{:S(2)}) collective-permute-start(bf16[128,2048]{1,0:T(8,128)(2,1)S(1)} %get-tuple-element.203), channel_id=1, source_target_pairs={{0,2},{1,3},{2,0},{3,1},{4,6},{5,7},{6,4},{7,5},{8,10},{9,11},{10,... | collective-permute-start | bytes 1572872 | tf_op jit(solution)/shard_map/ppermute | solution.py:41
  376.4 24.4 %collective-permute-start.42 = (bf16[256,2048]{1,0:T(8,128)(2,1)S(1)}, bf16[256,2048]{1,0:T(8,128)(2,1)S(1)}, u32[]{:S(2)}, u32[]{:S(2)}) collective-permute-start(bf16[256,2048]{1,0:T(8,128)(2,1)S(1)} %pad_maximum_fusion.19), channel_id=1, source_target_pairs={{0,2},{1,3},{2,0},{3,1},{4,6},{5,7},{6,4},{7,5},{8,10},{9,11},{10,... | collective-permute-start | bytes 3145736 | tf_op jit(solution)/shard_map/ppermute | solution.py:41
  377.5 24.1 %collective-permute-start.40 = (bf16[256,2048]{1,0:T(8,128)(2,1)S(1)}, bf16[256,2048]{1,0:T(8,128)(2,1)S(1)}, u32[]{:S(2)}, u32[]{:S(2)}) collective-permute-start(bf16[256,2048]{1,0:T(8,128)(2,1)S(1)} %pad_maximum_fusion.18), channel_id=1, source_target_pairs={{0,1},{1,0},{2,3},{3,2},{4,5},{5,4},{6,7},{7,6},{8,9},{9,8},{10,11... | collective-permute-start | bytes 3145736 | tf_op jit(solution)/shard_map/ppermute | solution.py:41
  406.4 23.2 %collective-permute-start.43 = (bf16[256,2048]{1,0:T(8,128)(2,1)S(1)}, bf16[256,2048]{1,0:T(8,128)(2,1)S(1)}, u32[]{:S(2)}, u32[]{:S(2)}) collective-permute-start(bf16[256,2048]{1,0:T(8,128)(2,1)S(1)} %get-tuple-element.164), channel_id=1, source_target_pairs={{0,1},{1,0},{2,3},{3,2},{4,5},{5,4},{6,7},{7,6},{8,9},{9,8},{10,11... | collective-permute-start | bytes 3145736 | tf_op jit(solution)/shard_map/ppermute | solution.py:41
  407.2 23.5 %collective-permute-start.44 = (bf16[256,2048]{1,0:T(8,128)(2,1)S(1)}, bf16[256,2048]{1,0:T(8,128)(2,1)S(1)}, u32[]{:S(2)}, u32[]{:S(2)}) collective-permute-start(bf16[256,2048]{1,0:T(8,128)(2,1)S(1)} %get-tuple-element.164), channel_id=1, source_target_pairs={{0,2},{1,3},{2,0},{3,1},{4,6},{5,7},{6,4},{7,5},{8,10},{9,11},{10,... | collective-permute-start | bytes 3145736 | tf_op jit(solution)/shard_map/ppermute | solution.py:41
  458.6 255.6 %reduce-scatter.7.cloned.1.call-start = ((), (), s32[]{:S(2)}) async-start(), calls=%async_computation.7 | async-start | bytes 5242880 | tf_op jit(solution)/shard_map/reduce_scatter | solution.py:695
  515.2 220.1 %reduce-scatter.9.cloned.1.call-start = ((), (), s32[]{:S(2)}) async-start(), calls=%async_computation.8 | async-start | bytes 5242880 | tf_op jit(solution)/shard_map/reduce_scatter | solution.py:695
  549.4 249.9 %all-gather.9.cloned.1.call-start = ((), (), s32[]{:S(2)}) async-start(), calls=%async_computation.10 | async-start | bytes 9437184 | tf_op jit(solution)/shard_map/all_gather | solution.py:706
  553.0 14.4 %collective-permute-start.52 = (bf16[128,2048]{1,0:T(8,128)(2,1)S(1)}, bf16[128,2048]{1,0:T(8,128)(2,1)S(1)}, u32[]{:S(2)}, u32[]{:S(2)}) collective-permute-start(bf16[128,2048]{1,0:T(8,128)(2,1)S(1)} %get-tuple-element.197), channel_id=1, source_target_pairs={{0,2},{1,3},{2,0},{3,1},{4,6},{5,7},{6,4},{7,5},{8,10},{9,11},{10,... | collective-permute-start | bytes 1572872 | tf_op jit(solution)/shard_map/ppermute | solution.py:41
  569.9 24.6 %collective-permute-start.55 = (bf16[256,2048]{1,0:T(8,128)(2,1)S(1)}, bf16[256,2048]{1,0:T(8,128)(2,1)S(1)}, u32[]{:S(2)}, u32[]{:S(2)}) collective-permute-start(bf16[256,2048]{1,0:T(8,128)(2,1)S(1)} %pad_maximum_fusion.22), channel_id=1, source_target_pairs={{0,2},{1,3},{2,0},{3,1},{4,6},{5,7},{6,4},{7,5},{8,10},{9,11},{10,... | collective-permute-start | bytes 3145736 | tf_op jit(solution)/shard_map/ppermute | solution.py:41
  571.1 24.4 %collective-permute-start.53 = (bf16[256,2048]{1,0:T(8,128)(2,1)S(1)}, bf16[256,2048]{1,0:T(8,128)(2,1)S(1)}, u32[]{:S(2)}, u32[]{:S(2)}) collective-permute-start(bf16[256,2048]{1,0:T(8,128)(2,1)S(1)} %pad_maximum_fusion.21), channel_id=1, source_target_pairs={{0,1},{1,0},{2,3},{3,2},{4,5},{5,4},{6,7},{7,6},{8,9},{9,8},{10,11... | collective-permute-start | bytes 3145736 | tf_op jit(solution)/shard_map/ppermute | solution.py:41
  604.5 23.5 %collective-permute-start.56 = (bf16[256,2048]{1,0:T(8,128)(2,1)S(1)}, bf16[256,2048]{1,0:T(8,128)(2,1)S(1)}, u32[]{:S(2)}, u32[]{:S(2)}) collective-permute-start(bf16[256,2048]{1,0:T(8,128)(2,1)S(1)} %get-tuple-element.162), channel_id=1, source_target_pairs={{0,1},{1,0},{2,3},{3,2},{4,5},{5,4},{6,7},{7,6},{8,9},{9,8},{10,11... | collective-permute-start | bytes 3145736 | tf_op jit(solution)/shard_map/ppermute | solution.py:41
  605.5 24.3 %collective-permute-start.57 = (bf16[256,2048]{1,0:T(8,128)(2,1)S(1)}, bf16[256,2048]{1,0:T(8,128)(2,1)S(1)}, u32[]{:S(2)}, u32[]{:S(2)}) collective-permute-start(bf16[256,2048]{1,0:T(8,128)(2,1)S(1)} %get-tuple-element.162), channel_id=1, source_target_pairs={{0,2},{1,3},{2,0},{3,1},{4,6},{5,7},{6,4},{7,5},{8,10},{9,11},{10,... | collective-permute-start | bytes 3145736 | tf_op jit(solution)/shard_map/ppermute | solution.py:41
  631.7 15.3 %collective-permute-start.60 = (bf16[256,2048]{1,0:T(8,128)(2,1)}, bf16[256,2048]{1,0:T(8,128)(2,1)S(1)}, u32[]{:S(2)}, u32[]{:S(2)}) collective-permute-start(bf16[256,2048]{1,0:T(8,128)(2,1)} %copy-done.51), channel_id=1, source_target_pairs={{0,4},{4,0},{1,5},{5,1},{2,6},{6,2},{3,7},{7,3},{8,12},{12,8},{9,1... | collective-permute-start | bytes 3145736 | tf_op jit(solution)/shard_map/ppermute | solution.py:36
  631.7 16.4 %collective-permute-start.61 = (bf16[256,2048]{1,0:T(8,128)(2,1)}, bf16[256,2048]{1,0:T(8,128)(2,1)S(1)}, u32[]{:S(2)}, u32[]{:S(2)}) collective-permute-start(bf16[256,2048]{1,0:T(8,128)(2,1)} %copy-done.48), channel_id=1, source_target_pairs={{0,4},{4,0},{1,5},{5,1},{2,6},{6,2},{3,7},{7,3},{8,12},{12,8},{9,1... | collective-permute-start | bytes 3145736 | tf_op jit(solution)/shard_map/ppermute | solution.py:36
  632.2 17.0 %collective-permute-start.62 = (bf16[256,2048]{1,0:T(8,128)(2,1)S(1)}, bf16[256,2048]{1,0:T(8,128)(2,1)S(1)}, u32[]{:S(2)}, u32[]{:S(2)}) collective-permute-start(bf16[256,2048]{1,0:T(8,128)(2,1)S(1)} %collective-permute-done.57), channel_id=1, source_target_pairs={{0,4},{4,0},{1,5},{5,1},{2,6},{6,2},{3,7},{7,3},{8,12},{12,8},{9,1... | collective-permute-start | bytes 3145736 | tf_op jit(solution)/shard_map/ppermute | solution.py:36
  658.4 55.8 %all-to-all-start.1 = ((bf16[4,512,256]{2,1,0:T(8,128)(2,1)}), bf16[4,512,256]{2,1,0:T(8,128)(2,1)S(1)}, u32[]{:S(2)}, u32[]{:S(2)}) async-start(bf16[4,512,256]{2,1,0:T(8,128)(2,1)} %bitcast.316), calls=%async_computation.2 | async-start | bytes 2097152 | tf_op jit(solution)/shard_map/all_to_all | solution.py:742
  661.9 215.6 %reduce-scatter.11.cloned.1.call-start = ((), (), s32[]{:S(2)}) async-start(), calls=%async_computation.9 | async-start | bytes 5242880 | tf_op jit(solution)/shard_map/reduce_scatter | solution.py:695
  799.4 245.9 %all-gather.13.cloned.1.call-start = ((), (), s32[]{:S(2)}) async-start(), calls=%async_computation.12 | async-start | bytes 9437184 | tf_op jit(solution)/shard_map/all_gather | solution.py:706
  816.1 245.7 %all-gather.15.cloned.1.call-start = ((), (), s32[]{:S(2)}) async-start(), calls=%async_computation.13 | async-start | bytes 9437184 | tf_op jit(solution)/shard_map/all_gather | solution.py:706
  832.6 312.0 %all-gather.11.cloned.1.call-start = ((), (), s32[]{:S(2)}) async-start(), calls=%async_computation.11 | async-start | bytes 9437184 | tf_op jit(solution)/shard_map/all_gather | solution.py:706
  906.8 14.1 %collective-permute-start.68 = (bf16[512,512]{1,0:T(8,128)(2,1)S(1)}, bf16[512,512]{1,0:T(8,128)(2,1)S(1)}, u32[]{:S(2)}, u32[]{:S(2)}) collective-permute-start(bf16[512,512]{1,0:T(8,128)(2,1)S(1)} %get-tuple-element.191), channel_id=1, source_target_pairs={{0,2},{1,3},{2,0},{3,1},{4,6},{5,7},{6,4},{7,5},{8,10},{9,11},{10,... | collective-permute-start | bytes 1572872 | tf_op jit(solution)/shard_map/ppermute | solution.py:41
  923.7 44.3 %collective-permute-start.71 = (bf16[1024,512]{1,0:T(8,128)(2,1)}, bf16[1024,512]{1,0:T(8,128)(2,1)S(1)}, u32[]{:S(2)}, u32[]{:S(2)}) collective-permute-start(bf16[1024,512]{1,0:T(8,128)(2,1)} %pad_maximum_fusion.25), channel_id=1, source_target_pairs={{0,2},{1,3},{2,0},{3,1},{4,6},{5,7},{6,4},{7,5},{8,10},{9,11},{10,... | collective-permute-start | bytes 3145736 | tf_op jit(solution)/shard_map/ppermute | solution.py:41
  925.2 42.9 %collective-permute-start.69 = (bf16[1024,512]{1,0:T(8,128)(2,1)}, bf16[1024,512]{1,0:T(8,128)(2,1)}, u32[]{:S(2)}, u32[]{:S(2)}) collective-permute-start(bf16[1024,512]{1,0:T(8,128)(2,1)} %pad_maximum_fusion.24), channel_id=1, source_target_pairs={{0,1},{1,0},{2,3},{3,2},{4,5},{5,4},{6,7},{7,6},{8,9},{9,8},{10,11... | collective-permute-start | bytes 3145736 | tf_op jit(solution)/shard_map/ppermute | solution.py:41
  927.8 22.3 %collective-permute-start.92 = (f32[33,128]{1,0:T(8,128)S(1)}, f32[33,128]{1,0:T(8,128)S(1)}, u32[]{:S(2)}, u32[]{:S(2)}) collective-permute-start(f32[33,128]{1,0:T(8,128)S(1)} %fusion.127), channel_id=1, source_target_pairs={{0,1},{1,0},{2,3},{3,2},{4,5},{5,4},{6,7},{7,6},{8,9},{9,8},{10,11... | collective-permute-start | bytes 50696 | tf_op jit(solution)/shard_map/ppermute | solution.py:41
  970.5 16.0 %collective-permute-start.74 = (bf16[256,512]{1,0:T(8,128)(2,1)S(1)}, bf16[256,512]{1,0:T(8,128)(2,1)S(1)}, u32[]{:S(2)}, u32[]{:S(2)}) collective-permute-start(bf16[256,512]{1,0:T(8,128)(2,1)S(1)} %get-tuple-element.265), channel_id=1, source_target_pairs={{0,24},{8,16},{16,8},{24,0},{1,25},{9,17},{17,9},{25,1},{2,26},{10... | collective-permute-start | bytes 786440 | tf_op jit(solution)/shard_map/ppermute | solution.py:46
  972.0 48.6 %collective-permute-start.73 = (bf16[256,512]{1,0:T(8,128)(2,1)S(1)}, bf16[256,512]{1,0:T(8,128)(2,1)S(1)}, u32[]{:S(2)}, u32[]{:S(2)}) collective-permute-start(bf16[256,512]{1,0:T(8,128)(2,1)S(1)} %get-tuple-element.266), channel_id=1, source_target_pairs={{0,16},{8,24},{16,0},{24,8},{1,17},{9,25},{17,1},{25,9},{2,18},{10... | collective-permute-start | bytes 786440 | tf_op jit(solution)/shard_map/ppermute | solution.py:46
  972.1 48.6 %collective-permute-start.72 = (bf16[256,512]{1,0:T(8,128)(2,1)S(1)}, bf16[256,512]{1,0:T(8,128)(2,1)S(1)}, u32[]{:S(2)}, u32[]{:S(2)}) collective-permute-start(bf16[256,512]{1,0:T(8,128)(2,1)S(1)} %get-tuple-element.267), channel_id=1, source_target_pairs={{0,8},{8,0},{16,24},{24,16},{1,9},{9,1},{17,25},{25,17},{2,10},{10... | collective-permute-start | bytes 786440 | tf_op jit(solution)/shard_map/ppermute | solution.py:46
  975.7 48.8 %collective-permute-start.90 = (f32[2,256]{1,0:T(2,128)S(1)}, f32[2,256]{1,0:T(2,128)S(1)}, u32[]{:S(2)}, u32[]{:S(2)}) collective-permute-start(f32[2,256]{1,0:T(2,128)S(1)} %add_add_fusion.1), channel_id=1, source_target_pairs={{0,4},{4,0},{1,5},{5,1},{2,6},{6,2},{3,7},{7,3},{8,12},{12,8},{9,1... | collective-permute-start | bytes 6152 | tf_op jit(solution)/shard_map/ppermute | solution.py:36
  (129 other events, 1525.7 us)
Sparse Core Ops, SparseCore 0:
  458.8 74.9 reduce-scatter.4
  536.7 77.2 reduce-scatter.6
  616.9 93.7 reduce-scatter.8
  712.2 87.0 all-gather.8
  802.2 75.2 reduce-scatter.10
  879.5 84.2 all-gather.12
  965.5 96.2 all-gather.14
  1063.4 81.1 all-gather.10
